TPU v7x, 32 devices: a whole 2x2x4 slice. The times are simulated.
32 devices in a mesh: groups: 2 (over y), ctx: 4 (over z), tp: 2 (over x), sub: 2 (over core).
Axes of the slice: x: 2, y: 2, z: 4, core: 2. Of those that a mesh axis runs over, the one named last changes fastest.
Arguments:
- queries: bfloat16 [3072, 8192], P(('groups', 'ctx'), ('tp', 'sub')), parts along dimension 0, may hold values from -200 to 200
- keys: bfloat16 [3072, 1024], P(('groups', 'ctx'), ('tp', 'sub')), parts along dimension 0, may hold values from -6 to 6
- values: bfloat16 [3072, 1024], P(('groups', 'ctx'), ('tp', 'sub')), parts along dimension 0, may hold values from -6 to 6
- segment_ids: int32 [3072], P(('groups', 'ctx')), parts along dimension 0, may hold values from 0 to 8, as said below
Outputs:
- attended: bfloat16 [3072, 8192], P(('groups', 'ctx'), ('tp', 'sub')), parts along dimension 0
There are 2 independent parts, one for each index of `groups`. A program takes and returns all parts, laid end to end along the dimension named above; each array names one. Nothing has to cross between parts.
Inputs may be any that keep to these rules, and one draw needn't show every extreme that they name: segment_ids is 0 on the first 384 tokens; after them exactly 8 chains 1, 2, ..., 8 follow in order and fill the row, each a run of 96 to 192 tokens, one of them exactly 192.
All inputs are finite; a program needn't handle non-finite values.
Results may differ from a plain program's by a relative error of at most 0.0041.
Values may be sent and summed in bfloat16 or wider, within the bound.
No kernel may reach another device: no remote copies, remote signals or barrier semaphores. Data moves between devices by JAX's collectives and lax.ppermute only.
A program may use at most 64 MiB of HBM per device.

v0:
```python
import jax
import jax.numpy as jnp
from jax import lax
from jax.sharding import PartitionSpec as P

HEAD_DIM = 128
GROUP = 8


def attend_block(
    running,
    key_block,
    value_block,
    segment_block,
    first_row,
    query_heads,
    query_places,
    query_segment,
):
    number = key_block.shape[0]
    heads_here = key_block.shape[1] // HEAD_DIM
    key_places = first_row + jnp.arange(number, dtype=jnp.int32)
    same = (segment_block[None, :] == query_segment[:, None]) | (segment_block[None, :] == 0)
    visible = (key_places[None, :] <= query_places[:, None]) & same
    key_heads = key_block.reshape(number, heads_here, HEAD_DIM)
    value_heads = value_block.reshape(number, heads_here, HEAD_DIM)

    def compute(state):
        row_peak, row_total, weighted = state
        scores = jnp.einsum(
            "qhgd,khd->hgqk", query_heads, key_heads, preferred_element_type=jnp.float32
        ) * HEAD_DIM ** (-0.5)
        scores = jnp.where(visible[None, None], scores, -1e30)
        new_peak = jnp.maximum(row_peak, jnp.max(scores, axis=-1))
        factor = jnp.exp(row_peak - new_peak)
        weights = jnp.where(visible[None, None], jnp.exp(scores - new_peak[..., None]), 0.0)
        new_total = row_total * factor + jnp.sum(weights, axis=-1)
        added = jnp.einsum(
            "hgqk,khd->hgqd",
            weights.astype(jnp.bfloat16),
            value_heads,
            preferred_element_type=jnp.float32,
        )
        return (new_peak, new_total, weighted * factor[..., None] + added)

    return lax.cond(jnp.any(visible), compute, lambda state: state, running)


def per_device(queries, keys, values, segment_ids):
    row_count = queries.shape[0]
    heads_here = keys.shape[1] // HEAD_DIM
    my_index = lax.axis_index("ctx")
    query_places = my_index * row_count + jnp.arange(row_count, dtype=jnp.int32)
    query_heads = queries.reshape(row_count, heads_here, GROUP, HEAD_DIM)
    initial = (
        jnp.full((heads_here, GROUP, row_count), -1e30, jnp.float32),
        jnp.zeros((heads_here, GROUP, row_count), jnp.float32),
        jnp.zeros((heads_here, GROUP, row_count, HEAD_DIM), jnp.float32),
    )
    key_all = lax.all_gather(keys, "ctx", axis=0, tiled=True)
    value_all = lax.all_gather(values, "ctx", axis=0, tiled=True)
    segment_all = lax.all_gather(segment_ids, "ctx", axis=0, tiled=True)
    blocks = max(1, key_all.shape[0] // row_count)
    width_rows = key_all.shape[0] // blocks

    def turn(number, state):
        offset = number * width_rows
        key_part = lax.dynamic_slice_in_dim(key_all, offset, width_rows, 0)
        value_part = lax.dynamic_slice_in_dim(value_all, offset, width_rows, 0)
        segment_part = lax.dynamic_slice_in_dim(segment_all, offset, width_rows, 0)
        return attend_block(
            state,
            key_part,
            value_part,
            segment_part,
            offset,
            query_heads,
            query_places,
            segment_ids,
        )

    final = lax.fori_loop(0, blocks, turn, initial)
    row_peak, row_total, weighted = final
    mixed = weighted / row_total[..., None]
    mixed = jnp.transpose(mixed, (2, 0, 1, 3)).reshape(row_count, heads_here * GROUP * HEAD_DIM)
    return mixed.astype(jnp.bfloat16)


def solution(mesh):
    placed = (
        P(("groups", "ctx"), ("tp", "sub")),
        P(("groups", "ctx"), ("tp", "sub")),
        P(("groups", "ctx"), ("tp", "sub")),
        P(("groups", "ctx")),
    )
    return jax.shard_map(
        per_device,
        mesh=mesh,
        in_specs=placed,
        out_specs=P(("groups", "ctx"), ("tp", "sub")),
        check_vma=False,
    )
```

profile of v0, /device:TPU:22, one launch (start us, length us, event | category | flops | bytes accessed | tf_op | source)
XLA Modules:
  0.0 98.1 jit_solution(1589817121826386383)
XLA Ops:
  0.7 10.3 %all-gather = s32[4,1,384]{2,1,0:T(1,128)S(1)} all-gather(s32[1,1,384]{2,1,0:T(1,128)S(1)} %reshape.39), channel_id=1, replica_groups=mesh['groups'=2,'ctx'=4,'tp'=2,'sub'=2] {'ctx'}, dimensions={0}, use_global_device_ids=true | all-gather | bytes 7680 | tf_op jit(solution)/shard_map/all_gather | solution.py:62
  12.1 1.1 %copy.20 = bf16[384,256]{0,1:T(8,128)(2,1)S(1)} copy(bf16[384,256]{1,0:T(8,128)(2,1)} %param.10) | data formatting | bytes 393216 | tf_op args[2]
  13.2 18.8 %all_gather.11 = bf16[1536,256]{0,1:T(8,128)(2,1)} all-gather(bf16[384,256]{0,1:T(8,128)(2,1)S(1)} %copy.20), channel_id=1, replica_groups=mesh['groups'=2,'ctx'=4,'tp'=2,'sub'=2] {'ctx'}, dimensions={0}, use_global_device_ids=true | all-gather | bytes 983040 | tf_op jit(solution)/shard_map/all_gather | solution.py:61
  32.0 17.9 %all_gather.10 = bf16[1536,256]{0,1:T(8,128)(2,1)} all-gather(bf16[384,256]{0,1:T(8,128)(2,1)S(1)} %copy.18), channel_id=1, replica_groups=mesh['groups'=2,'ctx'=4,'tp'=2,'sub'=2] {'ctx'}, dimensions={0}, use_global_device_ids=true | all-gather | bytes 983040 | tf_op jit(solution)/shard_map/all_gather | solution.py:60
  49.9 1.9 %copy.19 = bf16[384,2048]{0,1:T(8,128)(2,1)S(1)} copy(bf16[384,2048]{1,0:T(8,128)(2,1)} %param.8) | data formatting | bytes 3145728 | tf_op args[0]
  52.8 2.0 %broadcast_in_dim.53 = f32[2,8,384,128]{3,2,1,0:T(8,128)} broadcast(f32[]{:T(128)} %constant.68.clone.1), dimensions={} | broadcast | bytes 3145732 | tf_op jit(solution)/shard_map/broadcast_in_dim | solution.py:58
  54.8 38.4 %while.18 = (s32[]{:T(128)}, f32[2,8,384]{2,1,0:T(8,128)S(1)}, f32[2,8,384]{2,1,0:T(8,128)S(1)}, f32[2,8,384,128]{3,2,1,0:T(8,128)}, s32[1536]{0:T(1024)S(1)}, /...) while((s32[]{:T(128)}, f32[2,8,384]{2,1,0:T(8,128)S(1)}, ...), condition=%wide.region_6.7_spmd.clone, body=%wide.region_0.6_spmd.clone.sunk | while | flops 1240953984 | bytes 63517816 | solution.py:82
  56.4 10.6 %conditional.3 = ((f32[2,8,384]{2,1,0:T(8,128)S(1)}, f32[2,8,384]{2,1,0:T(8,128)S(1)}, f32[2,8,384,128]{3,2,1,0:T(8,128)})) conditional(s32[]{:T(128)} %convert_element_type.33, (f32[2,8,384]{2,1,0:T(8,128)S(1)}, f32[2,8,384]{2,1,0:T(8,128)S(1)}, f32[2,8,384,128]{3,2,1,0:T(8,128)}) %tuple.60, (pred[384,384]{0,1:T(8,128)(4,1)S(1)}, ...), branch_computations={%region_2.0_spmd, %region_3.5_spmd} | conditional | flops 1240215552 | bytes 63357020 | solution.py:46
  57.5 1.7 %fusion.2 = (f32[2,8,384]{2,1,0:T(8,128)S(1)}, f32[2,384,384,8]{2,1,3,0:T(8,128)S(1)}) fusion(pred[384,384]{0,1:T(8,128)(4,1)S(1)} %get-tuple-element.234, bf16[384,2,128,1]{0,2,3,1:T(8,128)(2,1)S(1)} %bitcast.34, bf16[384,2,8,128]{3,0,2,1:T(8,128)(2,1)S(1)} %get-tuple-element.237), kind=kOutput, calls=%fused_computation.3 | convolution fusion | flops 611051520 | bytes 11378688 | tf_op jit(solution)/shard_map/while/body/eval_jaxpr/cond/branch_1_fun/qhgd,khd->hgqk/dot_general | solution.py:30
  59.2 2.3 %fusion.4 = f32[2,8,384]{2,1,0:T(8,128)S(1)} fusion(f32[2,384,384,8]{2,1,3,0:T(8,128)S(1)} %get-tuple-element.332, f32[2,8,384]{2,1,0:T(8,128)S(1)} %max.4, pred[384,384]{0,1:T(8,128)(4,1)S(1)} %get-tuple-element.234), kind=kLoop, calls=%fused_computation.5 | loop fusion | flops 11790336 | bytes 9633792 | tf_op jit(solution)/shard_map/while/body/eval_jaxpr/cond/branch_1_fun/reduce_sum | solution.py:37
  61.5 3.8 %multiply_add_fusion = f32[2,8,384,128]{3,2,1,0:T(8,128)S(1)} fusion(f32[2,8,384,128]{3,2,1,0:T(8,128)S(1)} %copy-done, bf16[384,2,128,1]{0,2,3,1:T(8,128)(2,1)S(1)} %bitcast.37, f32[2,384,384,8]{2,1,3,0:T(8,128)S(1)} %get-tuple-element.332, f32[2,8,384]{2,1,0:T(8,128)S(1)} %max.4, pred[384,384]{0,1:T(8,128)(4,1)S(1)} %get-tuple-element.234, ...), kind=kOutput, calls=%fused_computation.8 | convolution fusion | flops 617349120 | bytes 16121856 | tf_op jit(solution)/shard_map/while/body/eval_jaxpr/cond/branch_1_fun/hgqk,khd->hgqd/dot_general | solution.py:38
  65.4 1.6 %copy-done.1 = f32[2,8,384,128]{3,2,1,0:T(8,128)} copy-done((f32[2,8,384,128]{3,2,1,0:T(8,128)}, f32[2,8,384,128]{3,2,1,0:T(8,128)S(1)}, u32[]{:S(2)}) %copy-start.1) | copy-done | bytes 3145752 | tf_op jit(solution)/shard_map/while/body/eval_jaxpr/cond
  68.6 10.6 %conditional.3 = ((f32[2,8,384]{2,1,0:T(8,128)S(1)}, f32[2,8,384]{2,1,0:T(8,128)S(1)}, f32[2,8,384,128]{3,2,1,0:T(8,128)})) conditional(s32[]{:T(128)} %convert_element_type.33, (f32[2,8,384]{2,1,0:T(8,128)S(1)}, f32[2,8,384]{2,1,0:T(8,128)S(1)}, f32[2,8,384,128]{3,2,1,0:T(8,128)}) %tuple.60, (pred[384,384]{0,1:T(8,128)(4,1)S(1)}, ...), branch_computations={%region_2.0_spmd, %region_3.5_spmd} | conditional | flops 1240215552 | bytes 63357020 | solution.py:46
  69.7 1.7 %fusion.2 = (f32[2,8,384]{2,1,0:T(8,128)S(1)}, f32[2,384,384,8]{2,1,3,0:T(8,128)S(1)}) fusion(pred[384,384]{0,1:T(8,128)(4,1)S(1)} %get-tuple-element.234, bf16[384,2,128,1]{0,2,3,1:T(8,128)(2,1)S(1)} %bitcast.34, bf16[384,2,8,128]{3,0,2,1:T(8,128)(2,1)S(1)} %get-tuple-element.237), kind=kOutput, calls=%fused_computation.3 | convolution fusion | flops 611051520 | bytes 11378688 | tf_op jit(solution)/shard_map/while/body/eval_jaxpr/cond/branch_1_fun/qhgd,khd->hgqk/dot_general | solution.py:30
  71.5 2.3 %fusion.4 = f32[2,8,384]{2,1,0:T(8,128)S(1)} fusion(f32[2,384,384,8]{2,1,3,0:T(8,128)S(1)} %get-tuple-element.332, f32[2,8,384]{2,1,0:T(8,128)S(1)} %max.4, pred[384,384]{0,1:T(8,128)(4,1)S(1)} %get-tuple-element.234), kind=kLoop, calls=%fused_computation.5 | loop fusion | flops 11790336 | bytes 9633792 | tf_op jit(solution)/shard_map/while/body/eval_jaxpr/cond/branch_1_fun/reduce_sum | solution.py:37
  73.8 3.8 %multiply_add_fusion = f32[2,8,384,128]{3,2,1,0:T(8,128)S(1)} fusion(f32[2,8,384,128]{3,2,1,0:T(8,128)S(1)} %copy-done, bf16[384,2,128,1]{0,2,3,1:T(8,128)(2,1)S(1)} %bitcast.37, f32[2,384,384,8]{2,1,3,0:T(8,128)S(1)} %get-tuple-element.332, f32[2,8,384]{2,1,0:T(8,128)S(1)} %max.4, pred[384,384]{0,1:T(8,128)(4,1)S(1)} %get-tuple-element.234, ...), kind=kOutput, calls=%fused_computation.8 | convolution fusion | flops 617349120 | bytes 16121856 | tf_op jit(solution)/shard_map/while/body/eval_jaxpr/cond/branch_1_fun/hgqk,khd->hgqd/dot_general | solution.py:38
  77.6 1.6 %copy-done.1 = f32[2,8,384,128]{3,2,1,0:T(8,128)} copy-done((f32[2,8,384,128]{3,2,1,0:T(8,128)}, f32[2,8,384,128]{3,2,1,0:T(8,128)S(1)}, u32[]{:S(2)}) %copy-start.1) | copy-done | bytes 3145752 | tf_op jit(solution)/shard_map/while/body/eval_jaxpr/cond
  80.9 10.6 %conditional.3 = ((f32[2,8,384]{2,1,0:T(8,128)S(1)}, f32[2,8,384]{2,1,0:T(8,128)S(1)}, f32[2,8,384,128]{3,2,1,0:T(8,128)})) conditional(s32[]{:T(128)} %convert_element_type.33, (f32[2,8,384]{2,1,0:T(8,128)S(1)}, f32[2,8,384]{2,1,0:T(8,128)S(1)}, f32[2,8,384,128]{3,2,1,0:T(8,128)}) %tuple.60, (pred[384,384]{0,1:T(8,128)(4,1)S(1)}, ...), branch_computations={%region_2.0_spmd, %region_3.5_spmd} | conditional | flops 1240215552 | bytes 63357020 | solution.py:46
  82.0 1.7 %fusion.2 = (f32[2,8,384]{2,1,0:T(8,128)S(1)}, f32[2,384,384,8]{2,1,3,0:T(8,128)S(1)}) fusion(pred[384,384]{0,1:T(8,128)(4,1)S(1)} %get-tuple-element.234, bf16[384,2,128,1]{0,2,3,1:T(8,128)(2,1)S(1)} %bitcast.34, bf16[384,2,8,128]{3,0,2,1:T(8,128)(2,1)S(1)} %get-tuple-element.237), kind=kOutput, calls=%fused_computation.3 | convolution fusion | flops 611051520 | bytes 11378688 | tf_op jit(solution)/shard_map/while/body/eval_jaxpr/cond/branch_1_fun/qhgd,khd->hgqk/dot_general | solution.py:30
  83.7 2.3 %fusion.4 = f32[2,8,384]{2,1,0:T(8,128)S(1)} fusion(f32[2,384,384,8]{2,1,3,0:T(8,128)S(1)} %get-tuple-element.332, f32[2,8,384]{2,1,0:T(8,128)S(1)} %max.4, pred[384,384]{0,1:T(8,128)(4,1)S(1)} %get-tuple-element.234), kind=kLoop, calls=%fused_computation.5 | loop fusion | flops 11790336 | bytes 9633792 | tf_op jit(solution)/shard_map/while/body/eval_jaxpr/cond/branch_1_fun/reduce_sum | solution.py:37
  86.0 3.8 %multiply_add_fusion = f32[2,8,384,128]{3,2,1,0:T(8,128)S(1)} fusion(f32[2,8,384,128]{3,2,1,0:T(8,128)S(1)} %copy-done, bf16[384,2,128,1]{0,2,3,1:T(8,128)(2,1)S(1)} %bitcast.37, f32[2,384,384,8]{2,1,3,0:T(8,128)S(1)} %get-tuple-element.332, f32[2,8,384]{2,1,0:T(8,128)S(1)} %max.4, pred[384,384]{0,1:T(8,128)(4,1)S(1)} %get-tuple-element.234, ...), kind=kOutput, calls=%fused_computation.8 | convolution fusion | flops 617349120 | bytes 16121856 | tf_op jit(solution)/shard_map/while/body/eval_jaxpr/cond/branch_1_fun/hgqk,khd->hgqd/dot_general | solution.py:38
  89.9 1.6 %copy-done.1 = f32[2,8,384,128]{3,2,1,0:T(8,128)} copy-done((f32[2,8,384,128]{3,2,1,0:T(8,128)}, f32[2,8,384,128]{3,2,1,0:T(8,128)S(1)}, u32[]{:S(2)}) %copy-start.1) | copy-done | bytes 3145752 | tf_op jit(solution)/shard_map/while/body/eval_jaxpr/cond
  93.2 2.4 %fusion.13 = bf16[384,2,8,128]{3,0,2,1:T(8,128)(2,1)S(1)} fusion(f32[2,8,384,128]{3,2,1,0:T(8,128)} %get-tuple-element.257, f32[2,8,384]{2,1,0:T(8,128)S(1)} %get-tuple-element.258), kind=kLoop, calls=%fused_computation.22 | loop fusion | flops 1572864 | bytes 4743168 | tf_op jit(solution)/shard_map/convert_element_type | solution.py:86
  96.6 1.6 %copy.32 = bf16[48,8,16,128]{3,1,2,0:T(8,128)(2,1)} copy(bf16[48,8,16,128]{3,2,1,0:T(8,128)(2,1)S(1)} %bitcast.35) | data formatting | bytes 3145728
  (44 shorter events, 11.0 us)
Async XLA Ops:
  49.9 4.9 %copy-start.2 = (s32[384]{0:T(512)S(1)}, s32[384]{0:T(512)}, u32[]{:S(2)}) copy-start(s32[384]{0:T(512)} %param.11) | copy-start | bytes 4612
  59.2 2.3 %copy-start = (f32[2,8,384,128]{3,2,1,0:T(8,128)S(1)}, f32[2,8,384,128]{3,2,1,0:T(8,128)}, u32[]{:S(2)}) copy-start(f32[2,8,384,128]{3,2,1,0:T(8,128)} %get-tuple-element.239) | copy-start | bytes 9437188 | tf_op jit(solution)/shard_map/while/body/eval_jaxpr/cond
  65.4 1.7 %copy-start.1 = (f32[2,8,384,128]{3,2,1,0:T(8,128)}, f32[2,8,384,128]{3,2,1,0:T(8,128)S(1)}, u32[]{:S(2)}) copy-start(f32[2,8,384,128]{3,2,1,0:T(8,128)S(1)} %multiply_add_fusion) | copy-start | bytes 9437188 | tf_op jit(solution)/shard_map/while/body/eval_jaxpr/cond
  71.4 2.3 %copy-start = (f32[2,8,384,128]{3,2,1,0:T(8,128)S(1)}, f32[2,8,384,128]{3,2,1,0:T(8,128)}, u32[]{:S(2)}) copy-start(f32[2,8,384,128]{3,2,1,0:T(8,128)} %get-tuple-element.239) | copy-start | bytes 9437188 | tf_op jit(solution)/shard_map/while/body/eval_jaxpr/cond
  77.6 1.7 %copy-start.1 = (f32[2,8,384,128]{3,2,1,0:T(8,128)}, f32[2,8,384,128]{3,2,1,0:T(8,128)S(1)}, u32[]{:S(2)}) copy-start(f32[2,8,384,128]{3,2,1,0:T(8,128)S(1)} %multiply_add_fusion) | copy-start | bytes 9437188 | tf_op jit(solution)/shard_map/while/body/eval_jaxpr/cond
  83.7 2.3 %copy-start = (f32[2,8,384,128]{3,2,1,0:T(8,128)S(1)}, f32[2,8,384,128]{3,2,1,0:T(8,128)}, u32[]{:S(2)}) copy-start(f32[2,8,384,128]{3,2,1,0:T(8,128)} %get-tuple-element.239) | copy-start | bytes 9437188 | tf_op jit(solution)/shard_map/while/body/eval_jaxpr/cond
  89.9 1.7 %copy-start.1 = (f32[2,8,384,128]{3,2,1,0:T(8,128)}, f32[2,8,384,128]{3,2,1,0:T(8,128)S(1)}, u32[]{:S(2)}) copy-start(f32[2,8,384,128]{3,2,1,0:T(8,128)S(1)} %multiply_add_fusion) | copy-start | bytes 9437188 | tf_op jit(solution)/shard_map/while/body/eval_jaxpr/cond
where the time goes:
time: 98.4 us; the launch traced here: 98.1 us
  blocking collectives  47 us (48%)
  local copies, waits for them, and re-layouts  18.5 us (19%)
  matrix products  16.6 us (17%)
  other arithmetic  13.2 us (13%)
  loops' own time  2.79 us (3%)
    all_gather x1, blocking collectives, per_device(): value_all = lax.all_gather(values, 'ctx', axis=0, tiled=True)  18.8 us
    all_gather x1, blocking collectives, per_device(): key_all = lax.all_gather(keys, 'ctx', axis=0, tiled=True)  17.9 us
    dot_general x3, matrix products, compute(): jnp.einsum('hgqk,khd->hgqd', weights.astype(jnp.bfloat16), value_heads, p...  11.5 us
    all_gather x1, blocking collectives, per_device(): segment_all = lax.all_gather(segment_ids, 'ctx', axis=0, tiled=True)  10.3 us
    unnamed x9, local copies, waits for them, and re-layouts  7.27 us
    reduce_sum x3, other arithmetic, compute(): new_total = row_total * factor + jnp.sum(weights, axis=-1)  6.83 us
    dot_general x3, matrix products, compute(): jnp.einsum('qhgd,khd->hgqk', query_heads, key_heads, preferred_element_ty...  5.11 us
    cond x15, local copies, waits for them, and re-layouts  4.98 us

commit v1 on v0

--- a/solution.py
+++ b/solution.py
@@ -1,10 +1,343 @@
+import functools
+
 import jax
 import jax.numpy as jnp
 from jax import lax
+from jax.experimental import pallas as pl
+from jax.experimental.pallas import tpu as pltpu
 from jax.sharding import PartitionSpec as P
 
 HEAD_DIM = 128
 GROUP = 8
+LANES = 128
+ROWS = 128
+NEG = -1e30
+EXP2_SCALE = 1.4426950408889634 * HEAD_DIM ** (-0.5)
+
+VMEM = pl.BlockSpec(memory_space=pltpu.VMEM)
+SMEM = pl.BlockSpec(memory_space=pltpu.SMEM)
+HBM = pl.BlockSpec(memory_space=pltpu.HBM)
+
+
+def dot_t(a, b):
+    return lax.dot_general(a, b, (((1,), (1,)), ((), ())), preferred_element_type=jnp.float32)
+
+
+def head_cols(kv_head):
+    first = kv_head * GROUP * HEAD_DIM
+    return [slice(first + g * HEAD_DIM, first + (g + 1) * HEAD_DIM) for g in range(GROUP)]
+
+
+def stack(ref, rows, cols):
+    return jnp.concatenate([ref[rows, c] for c in cols], axis=0)
+
+
+def unstack(ref, rows, cols, value):
+    for g, c in enumerate(cols):
+        ref[rows, c] = value[g * ROWS : (g + 1) * ROWS].astype(ref.dtype)
+
+
+def widen(lane_copies, width):
+    whole = -(-width // LANES)
+    return jnp.concatenate([lane_copies] * whole, axis=1)[:, :width]
+
+
+def with_ones(wide, source, rows, heads):
+    for h in range(heads):
+        wide[0:rows, 2 * h * HEAD_DIM : (2 * h + 1) * HEAD_DIM] = source[0:rows, h * HEAD_DIM : (h + 1) * HEAD_DIM]
+
+
+def fill_ones(wide, heads):
+    for h in range(heads):
+        wide[:, (2 * h + 1) * HEAD_DIM : (2 * h + 2) * HEAD_DIM] = jnp.ones((wide.shape[0], HEAD_DIM), jnp.bfloat16)
+
+
+def fetch(source, target, sem):
+    copy = pltpu.make_async_copy(source, target, sem)
+    copy.start()
+    return copy
+
+
+def own_kernel(q_hbm, k_hbm, v_hbm, seg_ref, state_hbm, q_ref, k_ref, v_ref, state, bias, wide, in_sem, out_sem):
+    count, width = q_ref.shape
+    heads = k_ref.shape[1] // HEAD_DIM
+    blocks = count // ROWS
+    span = [slice(b * ROWS, (b + 1) * ROWS) for b in range(blocks)]
+    get_k = fetch(k_hbm, k_ref, in_sem.at[blocks])
+    get_q = [fetch(q_hbm.at[rows], q_ref.at[rows], in_sem.at[b]) for b, rows in enumerate(span)]
+    get_v = fetch(v_hbm, v_ref, in_sem.at[blocks + 1])
+    seg = seg_ref[...].astype(jnp.float32)
+    for b in range(blocks):
+        of_row = jnp.broadcast_to(seg[:, span[b]], (ROWS, ROWS)).T
+        for t in range(b + 1):
+            of_key = jnp.broadcast_to(seg[:, span[t]], (ROWS, ROWS))
+            seen = (of_key == of_row) | (of_key == 0.0)
+            if t == b:
+                i = lax.broadcasted_iota(jnp.int32, (ROWS, ROWS), 0)
+                j = lax.broadcasted_iota(jnp.int32, (ROWS, ROWS), 1)
+                seen = seen & (j <= i)
+            bias[span[b], span[t]] = jnp.where(seen, 0.0, NEG)
+    fill_ones(wide, heads)
+    get_k.wait()
+    get_v.wait()
+    with_ones(wide, v_ref, count, heads)
+    lane = lax.broadcasted_iota(jnp.int32, (ROWS, LANES), 1)
+    put = []
+    for b in range(blocks):
+        rows, keys = span[b], (b + 1) * ROWS
+        get_q[b].wait()
+        peaks = jnp.zeros((ROWS, LANES), jnp.float32)
+        totals = jnp.ones((ROWS, LANES), jnp.float32)
+        for h in range(heads):
+            cols = head_cols(h)
+            scores = dot_t(stack(q_ref, rows, cols), k_ref[0:keys, h * HEAD_DIM : (h + 1) * HEAD_DIM])
+            scores = scores.reshape(GROUP, ROWS, keys) + bias[rows, 0:keys][None]
+            peak = jnp.max(scores, axis=-1, keepdims=True)
+            weights = jnp.exp2((scores - peak) * EXP2_SCALE).astype(jnp.bfloat16).reshape(GROUP * ROWS, keys)
+            sums = jnp.dot(
+                weights, wide[0:keys, 2 * h * HEAD_DIM : (2 * h + 2) * HEAD_DIM], preferred_element_type=jnp.float32
+            )
+            unstack(state, rows, cols, sums[:, :HEAD_DIM])
+            for g in range(GROUP):
+                here = lane == h * GROUP + g
+                peaks = jnp.where(here, peak[g], peaks)
+                totals = jnp.where(here, sums[g * ROWS : (g + 1) * ROWS, HEAD_DIM:], totals)
+        state[rows, width : width + LANES] = peaks
+        state[rows, width + LANES : width + 2 * LANES] = totals
+        put.append(fetch(state.at[rows], state_hbm.at[rows], out_sem.at[b]))
+    for copy in put:
+        copy.wait()
+
+
+def prompt_scores_kernel(place_ref, q_ref, k1_ref, k2_ref, k3_ref, w_ref, peak_ref):
+    count = q_ref.shape[0]
+    heads = k1_ref.shape[1] // HEAD_DIM
+
+    def compute(k_ref):
+        for h in range(heads):
+            cols = head_cols(h)
+            for b in range(count // ROWS):
+                rows = slice(b * ROWS, (b + 1) * ROWS)
+                scores = dot_t(stack(q_ref, rows, cols), k_ref[:, h * HEAD_DIM : (h + 1) * HEAD_DIM])
+                peak = jnp.max(scores, axis=-1, keepdims=True)
+                weights = jnp.exp2((scores - peak) * EXP2_SCALE).astype(jnp.bfloat16)
+                first = (h * (count // ROWS) + b) * GROUP * ROWS
+                w_ref[first : first + GROUP * ROWS, :] = weights
+                unstack(peak_ref, rows, cols, jnp.broadcast_to(peak, (GROUP * ROWS, LANES)))
+
+    for place, k_ref in ((1, k1_ref), (2, k2_ref), (3, k3_ref)):
+        pl.when(place_ref[0] == place)(functools.partial(compute, k_ref))
+
+
+def tail_kernel(
+    place_ref, q_ref, t2_ref, t3_ref, seg_ref, state_hbm, ppeak_ref,
+    acc_ref, total_ref, factor_ref, state, tail, wide, in_sem,
+):
+    count, width = q_ref.shape
+    heads = width // HEAD_DIM // GROUP
+    half = count // 2
+    blocks = count // ROWS
+    place = place_ref[0]
+    span = [slice(b * ROWS, (b + 1) * ROWS) for b in range(blocks)]
+    get = [fetch(state_hbm.at[rows], state.at[rows], in_sem.at[b]) for b, rows in enumerate(span)]
+
+    @pl.when(place == 2)
+    def _():
+        tail[...] = t2_ref[...]
+
+    @pl.when(place == 3)
+    def _():
+        tail[...] = t3_ref[...]
+
+    def merge(with_tail):
+        if with_tail:
+            fill_ones(wide, heads)
+            for h in range(heads):
+                wide[:, 2 * h * HEAD_DIM : (2 * h + 1) * HEAD_DIM] = tail[
+                    half : 2 * half, h * HEAD_DIM : (h + 1) * HEAD_DIM
+                ]
+            of_keys = tail[2 * half : 2 * half + 16, :].astype(jnp.float32)[0:1, 0:half]
+            seg = seg_ref[...].astype(jnp.float32)
+        for b in range(blocks):
+            rows = span[b]
+            get[b].wait()
+            low = b * ROWS // 64 * 64
+            tailed = with_tail and low < half
+            keys = half - low
+            if tailed:
+                of_row = jnp.broadcast_to(seg[:, rows], (ROWS, ROWS)).T
+                seen = widen(of_row, half)[:, low:] == jnp.broadcast_to(of_keys, (ROWS, half))[:, low:]
+                bias = jnp.where(seen, 0.0, NEG)
+            for h in range(heads):
+                cols = head_cols(h)
+                first = width + h * GROUP
+                own = jnp.concatenate(
+                    [jnp.broadcast_to(state[rows, first + g : first + g + 1], (ROWS, LANES)) for g in range(GROUP)], axis=0
+                )
+                first = width + LANES + h * GROUP
+                total = jnp.concatenate(
+                    [jnp.broadcast_to(state[rows, first + g : first + g + 1], (ROWS, LANES)) for g in range(GROUP)], axis=0
+                )
+                prompt = jnp.where(place > 0, stack(ppeak_ref, rows, cols), NEG)
+                peak = jnp.maximum(own, prompt)
+                if tailed:
+                    scores = dot_t(stack(q_ref, rows, cols), tail[low:half, h * HEAD_DIM : (h + 1) * HEAD_DIM])
+                    scores = scores.reshape(GROUP, ROWS, keys) + bias[None]
+                    scores = scores.reshape(GROUP * ROWS, keys)
+                    peak = jnp.maximum(peak, jnp.max(scores, axis=-1, keepdims=True))
+                    weights = jnp.exp2((scores - widen(peak, keys)) * EXP2_SCALE).astype(jnp.bfloat16)
+                    sums = jnp.dot(
+                        weights,
+                        wide[low:half, 2 * h * HEAD_DIM : (2 * h + 2) * HEAD_DIM],
+                        preferred_element_type=jnp.float32,
+                    )
+                scale = jnp.exp2((own - peak) * EXP2_SCALE)
+                acc = stack(state, rows, cols) * scale
+                total = total * scale
+                if tailed:
+                    acc = acc + sums[:, :HEAD_DIM]
+                    total = total + sums[:, HEAD_DIM:]
+                unstack(acc_ref, rows, cols, acc)
+                unstack(total_ref, rows, cols, total)
+                unstack(factor_ref, rows, cols, jnp.exp2((prompt - peak) * EXP2_SCALE))
+
+    pl.when(place <= 1)(functools.partial(merge, False))
+    pl.when(place > 1)(functools.partial(merge, True))
+
+
+def final_kernel(place_ref, w_ref, v1_ref, v2_ref, v3_ref, acc_ref, total_ref, factor_ref, out_ref, wide, staged, sem):
+    count = acc_ref.shape[0]
+    heads = acc_ref.shape[1] // HEAD_DIM // GROUP
+    place = place_ref[0]
+    span = GROUP * HEAD_DIM
+
+    def copy(h, b):
+        box = (pl.ds(b * ROWS, ROWS), pl.ds(h * span, span))
+        return pltpu.make_async_copy(staged.at[box], out_ref.at[box], sem.at[h, b])
+
+    blocks = [(h, b) for h in range(heads) for b in range(count // ROWS)]
+
+    @pl.when(place == 0)
+    def _():
+        for h, b in blocks:
+            box = (slice(b * ROWS, (b + 1) * ROWS), slice(h * span, (h + 1) * span))
+            staged[box] = (acc_ref[box] / total_ref[box]).astype(jnp.bfloat16)
+            copy(h, b).start()
+
+    @pl.when(place > 0)
+    def _():
+        fill_ones(wide, heads)
+        for where, v_ref in ((1, v1_ref), (2, v2_ref), (3, v3_ref)):
+            pl.when(place == where)(functools.partial(with_ones, wide, v_ref, count, heads))
+        for h, b in blocks:
+            cols = head_cols(h)
+            rows = slice(b * ROWS, (b + 1) * ROWS)
+            first = (h * (count // ROWS) + b) * GROUP * ROWS
+            sums = jnp.dot(
+                w_ref[first : first + GROUP * ROWS, :],
+                wide[:, 2 * h * HEAD_DIM : (2 * h + 2) * HEAD_DIM],
+                preferred_element_type=jnp.float32,
+            )
+            factor = stack(factor_ref, rows, cols)
+            acc = stack(acc_ref, rows, cols) + sums[:, :HEAD_DIM] * factor
+            total = stack(total_ref, rows, cols) + sums[:, HEAD_DIM:] * factor
+            unstack(staged, rows, cols, acc / total)
+            copy(h, b).start()
+
+    for h, b in blocks:
+        copy(h, b).wait()
+
+
+def cost(flops, moved):
+    return pl.CostEstimate(flops=flops, bytes_accessed=moved, transcendentals=0)
+
+
+def prompt_block_path(queries, keys, values, segment_ids):
+    count, kv_width = keys.shape
+    width = queries.shape[1]
+    half = count // 2
+    blocks = count // ROWS
+    place = lax.axis_index("ctx").astype(jnp.int32)
+    where = place.reshape(1)
+    seg_row = segment_ids.reshape(1, count)
+
+    keys_2 = lax.ppermute(keys, "ctx", [(0, 2)])
+    values_2 = lax.ppermute(values, "ctx", [(0, 2)])
+    seg_tail = jnp.broadcast_to(
+        jnp.pad(segment_ids[half:].astype(jnp.bfloat16), (0, kv_width - half))[None], (16, kv_width)
+    )
+    tail = jnp.concatenate([keys[half:], values[half:], seg_tail], axis=0)
+    mixed = jnp.where(place == 0, jnp.concatenate([values, seg_tail], axis=0), tail)
+    tail_3 = lax.ppermute(mixed, "ctx", [(2, 3)])
+
+    stat = jax.ShapeDtypeStruct(queries.shape, jnp.float32)
+    state_shape = (count, width + 2 * LANES)
+    state = pl.pallas_call(
+        own_kernel,
+        out_shape=jax.ShapeDtypeStruct(state_shape, jnp.float32),
+        in_specs=[HBM] * 3 + [VMEM],
+        out_specs=HBM,
+        scratch_shapes=[
+            pltpu.VMEM(queries.shape, jnp.bfloat16),
+            pltpu.VMEM(keys.shape, jnp.bfloat16),
+            pltpu.VMEM(keys.shape, jnp.bfloat16),
+            pltpu.VMEM(state_shape, jnp.float32),
+            pltpu.VMEM((count, count), jnp.float32),
+            pltpu.VMEM((count, 2 * kv_width), jnp.bfloat16),
+            pltpu.SemaphoreType.DMA((blocks + 2,)),
+            pltpu.SemaphoreType.DMA((blocks,)),
+        ],
+        compiler_params=pltpu.CompilerParams(vmem_limit_bytes=14 << 20),
+        cost_estimate=cost(4 * count * count * width, 0),
+        name="own",
+    )(queries, keys, values, seg_row)
+
+    keys_3 = lax.ppermute(keys_2, "ctx", [(2, 3)])
+    keys_1 = lax.ppermute(keys_2, "ctx", [(2, 1)])
+    mixed, state = lax.optimization_barrier((mixed, state))
+    from_left = lax.ppermute(mixed, "ctx", [(0, 1), (1, 2)])
+    values_3 = lax.ppermute(values_2, "ctx", [(2, 3)])
+
+    weights, prompt_peak = pl.pallas_call(
+        prompt_scores_kernel,
+        out_shape=(jax.ShapeDtypeStruct((count * width // HEAD_DIM, count), jnp.bfloat16), stat),
+        in_specs=[SMEM] + [VMEM] * 4,
+        out_specs=(VMEM,) * 2,
+        compiler_params=pltpu.CompilerParams(vmem_limit_bytes=8 << 20),
+        cost_estimate=cost(1, 1),
+        name="prompt_scores",
+    )(where, queries, keys_1, keys_2, keys_3)
+
+    acc, total, factor = pl.pallas_call(
+        tail_kernel,
+        out_shape=(stat, stat, stat),
+        in_specs=[SMEM] + [VMEM] * 4 + [HBM, VMEM],
+        out_specs=(VMEM,) * 3,
+        scratch_shapes=[
+            pltpu.VMEM(state_shape, jnp.float32),
+            pltpu.VMEM(mixed.shape, jnp.bfloat16),
+            pltpu.VMEM((half, 2 * kv_width), jnp.bfloat16),
+            pltpu.SemaphoreType.DMA((blocks,)),
+        ],
+        compiler_params=pltpu.CompilerParams(vmem_limit_bytes=10 << 20),
+        cost_estimate=cost(1, 1),
+        name="tail",
+    )(where, queries, from_left, tail_3, seg_row, state, prompt_peak)
+
+    return pl.pallas_call(
+        final_kernel,
+        out_shape=jax.ShapeDtypeStruct(queries.shape, jnp.bfloat16),
+        in_specs=[SMEM] + [VMEM] * 7,
+        out_specs=pl.BlockSpec(memory_space=pl.ANY),
+        scratch_shapes=[
+            pltpu.VMEM((count, 2 * kv_width), jnp.bfloat16),
+            pltpu.VMEM(queries.shape, jnp.bfloat16),
+            pltpu.SemaphoreType.DMA((kv_width // HEAD_DIM, blocks)),
+        ],
+        compiler_params=pltpu.CompilerParams(vmem_limit_bytes=8 << 20),
+        cost_estimate=cost(1, 1),
+        name="final",
+    )(where, weights, from_left, values_2, values_3, acc, total, factor)
 
 
 def attend_block(
@@ -46,7 +379,7 @@
     return lax.cond(jnp.any(visible), compute, lambda state: state, running)
 
 
-def per_device(queries, keys, values, segment_ids):
+def gathered_path(queries, keys, values, segment_ids):
     row_count = queries.shape[0]
     heads_here = keys.shape[1] // HEAD_DIM
     my_index = lax.axis_index("ctx")
@@ -69,21 +402,22 @@
         value_part = lax.dynamic_slice_in_dim(value_all, offset, width_rows, 0)
         segment_part = lax.dynamic_slice_in_dim(segment_all, offset, width_rows, 0)
         return attend_block(
-            state,
-            key_part,
-            value_part,
-            segment_part,
-            offset,
-            query_heads,
-            query_places,
-            segment_ids,
+            state, key_part, value_part, segment_part, offset, query_heads, query_places, segment_ids
         )
 
-    final = lax.fori_loop(0, blocks, turn, initial)
-    row_peak, row_total, weighted = final
+    row_peak, row_total, weighted = lax.fori_loop(0, blocks, turn, initial)
     mixed = weighted / row_total[..., None]
     mixed = jnp.transpose(mixed, (2, 0, 1, 3)).reshape(row_count, heads_here * GROUP * HEAD_DIM)
     return mixed.astype(jnp.bfloat16)
+
+
+def per_device(parts, queries, keys, values, segment_ids):
+    rows = queries.shape[0]
+    tokens = rows * parts
+    prompt, chain = tokens // 4, tokens // 8
+    if parts == 4 and prompt == rows and 2 * chain == rows and rows % ROWS == 0 and keys.shape[1] >= chain:
+        return prompt_block_path(queries, keys, values, segment_ids)
+    return gathered_path(queries, keys, values, segment_ids)
 
 
 def solution(mesh):
@@ -94,7 +428,7 @@
         P(("groups", "ctx")),
     )
     return jax.shard_map(
-        per_device,
+        functools.partial(per_device, mesh.shape["ctx"]),
         mesh=mesh,
         in_specs=placed,
         out_specs=P(("groups", "ctx"), ("tp", "sub")),

time: 98.4 us -> 38.3 us (0.39)
  the two profiles are of different devices: /device:TPU:22 before, /device:TPU:28 now
where the time goes in v1:
time: 38.3 us; the launch traced here: 38 us
  Pallas kernels  14.5 us (38%)
  waiting for transfers between devices  10.1 us (26%)
  starting transfers between devices  6.56 us (17%)
  local copies, waits for them, and re-layouts  5.83 us (15%)
  other arithmetic  0.74 us (2%)
    ppermute x1, waiting for transfers between devices, prompt_block_path(): keys_3 = lax.ppermute(keys_2, 'ctx', [(2, 3)])  10 us
    pallas_call x1, Pallas kernels, prompt_block_path(): pl.pallas_call(own_kernel, out_shape=jax.ShapeDtypeStruct(state_shape, jn...  4.7 us
    pallas_call x1, Pallas kernels, prompt_block_path(): pl.pallas_call(tail_kernel, out_shape=(stat, stat, stat), in_specs=[SMEM]...  4.53 us
    unnamed x8, local copies, waits for them, and re-layouts  3.26 us
    pallas_call x1, Pallas kernels, prompt_block_path(): pl.pallas_call(final_kernel, out_shape=jax.ShapeDtypeStruct(queries.shape...  3.19 us
    pallas_call x1, Pallas kernels, prompt_block_path(): pl.pallas_call(prompt_scores_kernel, out_shape=(jax.ShapeDtypeStruct((cou...  2.05 us
    slice x2, local copies, waits for them, and re-layouts, prompt_block_path(): tail = jnp.concatenate([keys[half:], values[half:], seg_tail], axis=0)  1.8 us
    ppermute x1, starting transfers between devices, prompt_block_path(): values_3 = lax.ppermute(values_2, 'ctx', [(2, 3)])  1.29 us
  transfers between devices with their start and end apart: 7, of which 1 were waited for; matrix products, arithmetic and copies ran while one was open for 9% of the time, Pallas kernels for 30%

profile of v1, /device:TPU:28, one launch (start us, length us, event | category | flops | bytes accessed | tf_op | source)
XLA Modules:
  0.0 38.0 jit_solution(4286201537734235435)
XLA Ops:
  0.0 0.7 %collective-permute-start = (bf16[384,256]{1,0:T(8,128)(2,1)}, bf16[384,256]{1,0:T(8,128)(2,1)S(1)}, u32[]{:S(2)}, u32[]{:S(2)}) collective-permute-start(bf16[384,256]{1,0:T(8,128)(2,1)} %k_hbm.1), channel_id=1, source_target_pairs={{0,8},{1,9},{2,10},{3,11},{16,24},{17,25},{18,26},{19,27}} | collective-permute-start | bytes 589832 | tf_op jit(solution)/shard_map/ppermute | solution.py:264
  0.7 0.7 %collective-permute-start.4 = (bf16[384,256]{1,0:T(8,128)(2,1)}, bf16[384,256]{1,0:T(8,128)(2,1)S(1)}, u32[]{:S(2)}, u32[]{:S(2)}) collective-permute-start(bf16[384,256]{1,0:T(8,128)(2,1)} %v_hbm.1), channel_id=1, source_target_pairs={{0,8},{1,9},{2,10},{3,11},{16,24},{17,25},{18,26},{19,27}} | collective-permute-start | bytes 589832 | tf_op jit(solution)/shard_map/ppermute | solution.py:265
  1.4 0.9 %slice.11 = bf16[192,256]{1,0:T(8,128)(2,1)S(1)} slice(bf16[384,256]{1,0:T(8,128)(2,1)} %k_hbm.1), slice={[192:384], [0:256]} | slice | bytes 196608 | tf_op jit(solution)/shard_map/slice | solution.py:269
  2.3 0.9 %slice.12 = bf16[192,256]{1,0:T(8,128)(2,1)S(1)} slice(bf16[384,256]{1,0:T(8,128)(2,1)} %v_hbm.1), slice={[192:384], [0:256]} | slice | bytes 196608 | tf_op jit(solution)/shard_map/slice | solution.py:269
  3.2 0.7 %convert.3 = bf16[384]{0:T(512)(128)(2,1)S(1)} convert(s32[384]{0:T(512)} %param.7) | non-fusion elementwise | flops 384 | bytes 2304 | tf_op jit(solution)/shard_map/convert
  3.8 0.7 %reshape.8.seg_ref = s32[1,384]{1,0:T(1,128)S(1)} reshape(s32[384]{0:T(512)} %param.7) | data formatting | bytes 3072 | tf_op jit(solution)/shard_map/reshape | solution.py:262
  4.5 0.1 slice.10
  4.6 1.4 %copy-done = bf16[384,2048]{1,0:T(8,128)(2,1)S(1)} copy-done((bf16[384,2048]{1,0:T(8,128)(2,1)S(1)}, bf16[384,2048]{1,0:T(8,128)(2,1)}, u32[]{:S(2)}) %copy-start) | copy-done | bytes 1572888
  6.0 0.9 %copy-done.2 = bf16[384,256]{1,0:T(8,128)(2,1)S(1)} copy-done((bf16[384,256]{1,0:T(8,128)(2,1)S(1)}, bf16[384,256]{1,0:T(8,128)(2,1)}, u32[]{:S(2)}) %copy-start.2) | copy-done | bytes 196632
  6.9 0.9 %copy-done.3 = bf16[384,256]{1,0:T(8,128)(2,1)S(1)} copy-done((bf16[384,256]{1,0:T(8,128)(2,1)S(1)}, bf16[384,256]{1,0:T(8,128)(2,1)}, u32[]{:S(2)}) %copy-start.3) | copy-done | bytes 196632
  7.9 4.7 %own.1.state_hbm = f32[384,2304]{1,0:T(8,128)S(1)} custom-call(bf16[384,2048]{1,0:T(8,128)(2,1)S(1)} %copy-done, bf16[384,256]{1,0:T(8,128)(2,1)S(1)} %copy-done.3, bf16[384,256]{1,0:T(8,128)(2,1)S(1)} %copy-done.2, s32[1,384]{1,0:T(1,128)S(1)} %reshape.8.seg_ref), custom_call_target="tpu_custom_call" | custom-call | flops 1207959552 | tf_op jit(solution)/shard_map/own/pallas_call | solution.py:275
  12.6 0.1 fusion
  12.6 0.7 %collective-permute-start.3 = (bf16[400,256]{1,0:T(8,128)(2,1)S(1)}, bf16[400,256]{1,0:T(8,128)(2,1)S(1)}, u32[]{:S(2)}, u32[]{:S(2)}) collective-permute-start(bf16[400,256]{1,0:T(8,128)(2,1)S(1)} %fusion), channel_id=1, source_target_pairs={{0,4},{4,8},{1,5},{5,9},{2,6},{6,10},{3,7},{7,11},{16,20},{20,24},... | collective-permute-start | bytes 614408 | tf_op jit(solution)/shard_map/ppermute | solution.py:298
  13.3 1.3 %collective-permute-start.6 = (bf16[400,256]{1,0:T(8,128)(2,1)S(1)}, bf16[400,256]{1,0:T(8,128)(2,1)S(1)}, u32[]{:S(2)}, u32[]{:S(2)}) collective-permute-start(bf16[400,256]{1,0:T(8,128)(2,1)S(1)} %fusion), channel_id=1, source_target_pairs={{8,12},{9,13},{10,14},{11,15},{24,28},{25,29},{26,30},{27,31}} | collective-permute-start | bytes 614408 | tf_op jit(solution)/shard_map/ppermute | solution.py:271
  14.6 0.0 collective-permute-done.k2_ref
  14.6 0.7 %collective-permute-start.1 = (bf16[384,256]{1,0:T(8,128)(2,1)S(1)}, bf16[384,256]{1,0:T(8,128)(2,1)S(1)}, u32[]{:S(2)}, u32[]{:S(2)}) collective-permute-start(bf16[384,256]{1,0:T(8,128)(2,1)S(1)} %collective-permute-done.k2_ref), channel_id=1, source_target_pairs={{8,4},{9,5},{10,6},{11,7},{24,20},{25,21},{26,22},{27,23}} | collective-permute-start | bytes 589832 | tf_op jit(solution)/shard_map/ppermute | solution.py:296
  15.3 1.3 %collective-permute-start.2 = (bf16[384,256]{1,0:T(8,128)(2,1)S(1)}, bf16[384,256]{1,0:T(8,128)(2,1)S(1)}, u32[]{:S(2)}, u32[]{:S(2)}) collective-permute-start(bf16[384,256]{1,0:T(8,128)(2,1)S(1)} %collective-permute-done.k2_ref), channel_id=1, source_target_pairs={{8,12},{9,13},{10,14},{11,15},{24,28},{25,29},{26,30},{27,31}} | collective-permute-start | bytes 589832 | tf_op jit(solution)/shard_map/ppermute | solution.py:295
  16.6 0.0 collective-permute-done.4.v2_ref
  16.6 1.3 %collective-permute-start.5 = (bf16[384,256]{1,0:T(8,128)(2,1)S(1)}, bf16[384,256]{1,0:T(8,128)(2,1)S(1)}, u32[]{:S(2)}, u32[]{:S(2)}) collective-permute-start(bf16[384,256]{1,0:T(8,128)(2,1)S(1)} %collective-permute-done.4.v2_ref), channel_id=1, source_target_pairs={{8,12},{9,13},{10,14},{11,15},{24,28},{25,29},{26,30},{27,31}} | collective-permute-start | bytes 589832 | tf_op jit(solution)/shard_map/ppermute | solution.py:299
  17.9 0.0 collective-permute-done.1.k1_ref
  17.9 10.0 %collective-permute-done.2.k3_ref = bf16[384,256]{1,0:T(8,128)(2,1)S(1)} collective-permute-done((bf16[384,256]{1,0:T(8,128)(2,1)S(1)}, bf16[384,256]{1,0:T(8,128)(2,1)S(1)}, u32[]{:S(2)}, u32[]{:S(2)}) %collective-permute-start.2) | collective-permute-done | bytes 196640 | tf_op jit(solution)/shard_map/ppermute | solution.py:295
  28.0 2.0 %prompt_scores.1 = (bf16[6144,384]{1,0:T(8,128)(2,1)S(1)}, f32[384,2048]{1,0:T(8,128)S(1)}) custom-call(s32[1]{0:T(128)} %bitcast.place_ref, bf16[384,2048]{1,0:T(8,128)(2,1)S(1)} %copy-done.1, bf16[384,256]{1,0:T(8,128)(2,1)S(1)} %collective-permute-done.1.k1_ref, bf16[384,256]{1,0:T(8,128)(2,1)S(1)} %collective-permute-done.k2_ref, ...), custom_call_target="tpu_custom_call" | custom-call | flops 1 | bytes 1 | tf_op jit(solution)/shard_map/prompt_scores/pallas_call | solution.py:301
  30.1 4.5 %tail.1 = (f32[384,2048]{1,0:T(8,128)S(1)}, f32[384,2048]{1,0:T(8,128)S(1)}, f32[384,2048]{1,0:T(8,128)S(1)}) custom-call(s32[1]{0:T(128)} %bitcast.place_ref, bf16[384,2048]{1,0:T(8,128)(2,1)S(1)} %copy-done.1, bf16[400,256]{1,0:T(8,128)(2,1)S(1)} %collective-permute-done.3.t2_ref.v1_ref, bf16[400,256]{1,0:T(8,128)(2,1)S(1)} %collective-permute-done.6.t3_ref, ...), custom_call_target="tpu_custom_call" | custom-call | flops 1 | bytes 1 | tf_op jit(solution)/shard_map/tail/pallas_call | solution.py:311
  34.6 3.2 %final.1 = bf16[384,2048]{1,0:T(8,128)(2,1)} custom-call(s32[1]{0:T(128)} %bitcast.place_ref, bf16[6144,384]{1,0:T(8,128)(2,1)S(1)} %get-tuple-element.12.w_ref, bf16[400,256]{1,0:T(8,128)(2,1)S(1)} %collective-permute-done.3.t2_ref.v1_ref, bf16[384,256]{1,0:T(8,128)(2,1)S(1)} %collective-permute-done.4.v2_ref, ...), custom_call_target="tpu_custom_call" | custom-call | flops 1 | bytes 1 | tf_op jit(solution)/shard_map/final/pallas_call | solution.py:327
  (10 shorter events, 0.0 us)
Async XLA Ops:
  0.0 14.6 %collective-permute-start = (bf16[384,256]{1,0:T(8,128)(2,1)}, bf16[384,256]{1,0:T(8,128)(2,1)S(1)}, u32[]{:S(2)}, u32[]{:S(2)}) collective-permute-start(bf16[384,256]{1,0:T(8,128)(2,1)} %k_hbm.1), channel_id=1, source_target_pairs={{0,8},{1,9},{2,10},{3,11},{16,24},{17,25},{18,26},{19,27}} | collective-permute-start | bytes 589832 | tf_op jit(solution)/shard_map/ppermute | solution.py:264
  0.7 16.0 %collective-permute-start.4 = (bf16[384,256]{1,0:T(8,128)(2,1)}, bf16[384,256]{1,0:T(8,128)(2,1)S(1)}, u32[]{:S(2)}, u32[]{:S(2)}) collective-permute-start(bf16[384,256]{1,0:T(8,128)(2,1)} %v_hbm.1), channel_id=1, source_target_pairs={{0,8},{1,9},{2,10},{3,11},{16,24},{17,25},{18,26},{19,27}} | collective-permute-start | bytes 589832 | tf_op jit(solution)/shard_map/ppermute | solution.py:265
  4.6 1.4 %copy-start = (bf16[384,2048]{1,0:T(8,128)(2,1)S(1)}, bf16[384,2048]{1,0:T(8,128)(2,1)}, u32[]{:S(2)}) copy-start(bf16[384,2048]{1,0:T(8,128)(2,1)} %q_ref.3) | copy-start | bytes 4718596
  6.0 0.9 %copy-start.2 = (bf16[384,256]{1,0:T(8,128)(2,1)S(1)}, bf16[384,256]{1,0:T(8,128)(2,1)}, u32[]{:S(2)}) copy-start(bf16[384,256]{1,0:T(8,128)(2,1)} %v_hbm.1) | copy-start | bytes 589828
  6.9 0.9 %copy-start.3 = (bf16[384,256]{1,0:T(8,128)(2,1)S(1)}, bf16[384,256]{1,0:T(8,128)(2,1)}, u32[]{:S(2)}) copy-start(bf16[384,256]{1,0:T(8,128)(2,1)} %k_hbm.1) | copy-start | bytes 589828
  7.9 20.1 %copy-start.1 = (bf16[384,2048]{1,0:T(8,128)(2,1)S(1)}, bf16[384,2048]{1,0:T(8,128)(2,1)}, u32[]{:S(2)}) copy-start(bf16[384,2048]{1,0:T(8,128)(2,1)} %q_ref.3) | copy-start | bytes 4718596
  12.6 17.4 %collective-permute-start.3 = (bf16[400,256]{1,0:T(8,128)(2,1)S(1)}, bf16[400,256]{1,0:T(8,128)(2,1)S(1)}, u32[]{:S(2)}, u32[]{:S(2)}) collective-permute-start(bf16[400,256]{1,0:T(8,128)(2,1)S(1)} %fusion), channel_id=1, source_target_pairs={{0,4},{4,8},{1,5},{5,9},{2,6},{6,10},{3,7},{7,11},{16,20},{20,24},... | collective-permute-start | bytes 614408 | tf_op jit(solution)/shard_map/ppermute | solution.py:298
  13.3 16.7 %collective-permute-start.6 = (bf16[400,256]{1,0:T(8,128)(2,1)S(1)}, bf16[400,256]{1,0:T(8,128)(2,1)S(1)}, u32[]{:S(2)}, u32[]{:S(2)}) collective-permute-start(bf16[400,256]{1,0:T(8,128)(2,1)S(1)} %fusion), channel_id=1, source_target_pairs={{8,12},{9,13},{10,14},{11,15},{24,28},{25,29},{26,30},{27,31}} | collective-permute-start | bytes 614408 | tf_op jit(solution)/shard_map/ppermute | solution.py:271
  14.6 3.3 %collective-permute-start.1 = (bf16[384,256]{1,0:T(8,128)(2,1)S(1)}, bf16[384,256]{1,0:T(8,128)(2,1)S(1)}, u32[]{:S(2)}, u32[]{:S(2)}) collective-permute-start(bf16[384,256]{1,0:T(8,128)(2,1)S(1)} %collective-permute-done.k2_ref), channel_id=1, source_target_pairs={{8,4},{9,5},{10,6},{11,7},{24,20},{25,21},{26,22},{27,23}} | collective-permute-start | bytes 589832 | tf_op jit(solution)/shard_map/ppermute | solution.py:296
  15.3 12.7 %collective-permute-start.2 = (bf16[384,256]{1,0:T(8,128)(2,1)S(1)}, bf16[384,256]{1,0:T(8,128)(2,1)S(1)}, u32[]{:S(2)}, u32[]{:S(2)}) collective-permute-start(bf16[384,256]{1,0:T(8,128)(2,1)S(1)} %collective-permute-done.k2_ref), channel_id=1, source_target_pairs={{8,12},{9,13},{10,14},{11,15},{24,28},{25,29},{26,30},{27,31}} | collective-permute-start | bytes 589832 | tf_op jit(solution)/shard_map/ppermute | solution.py:295
  16.6 18.0 %collective-permute-start.5 = (bf16[384,256]{1,0:T(8,128)(2,1)S(1)}, bf16[384,256]{1,0:T(8,128)(2,1)S(1)}, u32[]{:S(2)}, u32[]{:S(2)}) collective-permute-start(bf16[384,256]{1,0:T(8,128)(2,1)S(1)} %collective-permute-done.4.v2_ref), channel_id=1, source_target_pairs={{8,12},{9,13},{10,14},{11,15},{24,28},{25,29},{26,30},{27,31}} | collective-permute-start | bytes 589832 | tf_op jit(solution)/shard_map/ppermute | solution.py:299

commit v2 on v1

v2 whole, which is shorter than its diff:
```python
import functools

import jax
import jax.numpy as jnp
from jax import lax
from jax.experimental import pallas as pl
from jax.experimental.pallas import tpu as pltpu
from jax.sharding import PartitionSpec as P

HEAD_DIM = 128
GROUP = 8
LANES = 128
ROWS = 128
NEG = -1e30
EXP2_SCALE = 1.4426950408889634 * HEAD_DIM ** (-0.5)

VMEM = pl.BlockSpec(memory_space=pltpu.VMEM)
SMEM = pl.BlockSpec(memory_space=pltpu.SMEM)
HBM = pl.BlockSpec(memory_space=pltpu.HBM)


def dot_t(a, b):
    return lax.dot_general(a, b, (((1,), (1,)), ((), ())), preferred_element_type=jnp.float32)


def head_cols(kv_head):
    first = kv_head * GROUP * HEAD_DIM
    return [slice(first + g * HEAD_DIM, first + (g + 1) * HEAD_DIM) for g in range(GROUP)]


def stack(ref, rows, cols):
    return jnp.concatenate([ref[rows, c] for c in cols], axis=0)


def unstack(ref, rows, cols, value):
    for g, c in enumerate(cols):
        ref[rows, c] = value[g * ROWS : (g + 1) * ROWS].astype(ref.dtype)


def widen(lane_copies, width):
    whole = -(-width // LANES)
    return jnp.concatenate([lane_copies] * whole, axis=1)[:, :width]


def with_ones(wide, source, rows, heads):
    for h in range(heads):
        wide[0:rows, 2 * h * HEAD_DIM : (2 * h + 1) * HEAD_DIM] = source[0:rows, h * HEAD_DIM : (h + 1) * HEAD_DIM]


def fill_ones(wide, heads):
    for h in range(heads):
        wide[:, (2 * h + 1) * HEAD_DIM : (2 * h + 2) * HEAD_DIM] = jnp.ones((wide.shape[0], HEAD_DIM), jnp.bfloat16)


def fetch(source, target, sem):
    copy = pltpu.make_async_copy(source, target, sem)
    copy.start()
    return copy


def pack_kernel(place_ref, k_hbm, v_hbm, seg_hbm, mixed_ref, seg_ref, sem):
    count = k_hbm.shape[0]
    half = count // 2
    place = place_ref[0]
    low, high = pl.ds(0, half), pl.ds(half, half)
    get_seg = fetch(seg_hbm, seg_ref, sem.at[2])

    @pl.when(place == 0)
    def _():
        fetch(v_hbm.at[low], mixed_ref.at[low], sem.at[0])

    @pl.when(place > 0)
    def _():
        fetch(k_hbm.at[high], mixed_ref.at[low], sem.at[0])

    other = fetch(v_hbm.at[high], mixed_ref.at[high], sem.at[1])
    get_seg.wait()
    seg = seg_ref[...].reshape(1, count).astype(jnp.float32)[:, half:]
    pltpu.make_async_copy(k_hbm.at[high], mixed_ref.at[low], sem.at[0]).wait()

    @pl.when(place > 0)
    def _():
        first = lax.broadcasted_iota(jnp.int32, (16, half), 0) == 0
        old = mixed_ref[0:16, 0:half].astype(jnp.float32)
        mixed_ref[0:16, 0:half] = jnp.where(first, jnp.broadcast_to(seg, (16, half)), old).astype(jnp.bfloat16)

    other.wait()


def own_kernel(q_hbm, k_hbm, v_hbm, seg_hbm, state, q_ref, k_ref, v_ref, seg_ref, bias, wide, in_sem):
    count, width = q_ref.shape
    heads = k_ref.shape[1] // HEAD_DIM
    blocks = count // ROWS
    span = [slice(b * ROWS, (b + 1) * ROWS) for b in range(blocks)]
    get_seg = fetch(seg_hbm, seg_ref, in_sem.at[blocks + 2])
    get_k = fetch(k_hbm, k_ref, in_sem.at[blocks])
    get_q = [fetch(q_hbm.at[rows], q_ref.at[rows], in_sem.at[b]) for b, rows in enumerate(span)]
    get_v = fetch(v_hbm, v_ref, in_sem.at[blocks + 1])
    get_seg.wait()
    seg = seg_ref[...].reshape(1, count).astype(jnp.float32)
    for b in range(blocks):
        of_row = jnp.broadcast_to(seg[:, span[b]], (ROWS, ROWS)).T
        for t in range(b + 1):
            of_key = jnp.broadcast_to(seg[:, span[t]], (ROWS, ROWS))
            seen = (of_key == of_row) | (of_key == 0.0)
            if t == b:
                i = lax.broadcasted_iota(jnp.int32, (ROWS, ROWS), 0)
                j = lax.broadcasted_iota(jnp.int32, (ROWS, ROWS), 1)
                seen = seen & (j <= i)
            bias[span[b], span[t]] = jnp.where(seen, 0.0, NEG)
    fill_ones(wide, heads)
    get_k.wait()
    get_v.wait()
    with_ones(wide, v_ref, count, heads)
    lane = lax.broadcasted_iota(jnp.int32, (ROWS, LANES), 1)
    for b in range(blocks):
        rows, keys = span[b], (b + 1) * ROWS
        get_q[b].wait()
        peaks = jnp.zeros((ROWS, LANES), jnp.float32)
        totals = jnp.ones((ROWS, LANES), jnp.float32)
        for h in range(heads):
            cols = head_cols(h)
            scores = dot_t(stack(q_ref, rows, cols), k_ref[0:keys, h * HEAD_DIM : (h + 1) * HEAD_DIM])
            scores = scores.reshape(GROUP, ROWS, keys) + bias[rows, 0:keys][None]
            peak = jnp.max(scores, axis=-1, keepdims=True)
            weights = jnp.exp2((scores - peak) * EXP2_SCALE).astype(jnp.bfloat16).reshape(GROUP * ROWS, keys)
            sums = jnp.dot(
                weights, wide[0:keys, 2 * h * HEAD_DIM : (2 * h + 2) * HEAD_DIM], preferred_element_type=jnp.float32
            )
            unstack(state, rows, cols, sums[:, :HEAD_DIM] / sums[:, HEAD_DIM:])
            for g in range(GROUP):
                here = lane == h * GROUP + g
                peaks = jnp.where(here, peak[g], peaks)
                totals = jnp.where(here, sums[g * ROWS : (g + 1) * ROWS, HEAD_DIM:], totals)
        state[rows, width : width + LANES] = peaks
        state[rows, width + LANES : width + 2 * LANES] = totals


def prompt_scores_kernel(place_ref, q_ref, k1_ref, k2_ref, k3_ref, w_ref, peak_ref):
    count = q_ref.shape[0]
    heads = k1_ref.shape[1] // HEAD_DIM
    lane = lax.broadcasted_iota(jnp.int32, (ROWS, LANES), 1)

    def compute(k_ref):
        for b in range(count // ROWS):
            rows = slice(b * ROWS, (b + 1) * ROWS)
            peaks = jnp.zeros((ROWS, LANES), jnp.float32)
            for h in range(heads):
                cols = head_cols(h)
                scores = dot_t(stack(q_ref, rows, cols), k_ref[:, h * HEAD_DIM : (h + 1) * HEAD_DIM])
                peak = jnp.max(scores, axis=-1, keepdims=True)
                weights = jnp.exp2((scores - peak) * EXP2_SCALE).astype(jnp.bfloat16)
                first = (h * (count // ROWS) + b) * GROUP * ROWS
                w_ref[first : first + GROUP * ROWS, :] = weights
                for g in range(GROUP):
                    peaks = jnp.where(lane == h * GROUP + g, peak[g * ROWS : (g + 1) * ROWS], peaks)
            peak_ref[rows, :] = peaks

    for place, k_ref in ((1, k1_ref), (2, k2_ref), (3, k3_ref)):
        pl.when(place_ref[0] == place)(functools.partial(compute, k_ref))


def column(stats, index):
    return jnp.broadcast_to(stats[:, index : index + 1], (stats.shape[0], LANES))


def tail_kernel(place_ref, q_ref, t2_ref, t3_ref, seg_ref, state_in, state, tail, wide):
    count, width = q_ref.shape
    heads = width // HEAD_DIM // GROUP
    half = count // 2
    place = place_ref[0]

    @pl.when(place == 2)
    def _():
        tail[...] = t2_ref[...]

    @pl.when(place == 3)
    def _():
        tail[...] = t3_ref[...]

    @pl.when(place > 1)
    def _():
        fill_ones(wide, heads)
        for h in range(heads):
            wide[:, 2 * h * HEAD_DIM : (2 * h + 1) * HEAD_DIM] = tail[half : 2 * half, h * HEAD_DIM : (h + 1) * HEAD_DIM]
        of_keys = tail[0:16, 0:half].astype(jnp.float32)[0:1]
        of_keys = jnp.where(lax.broadcasted_iota(jnp.int32, (1, half), 1) == 0, -1.0, of_keys)
        seg = seg_ref[...].reshape(1, count).astype(jnp.float32)
        for start in range(0, half, ROWS):
            size = min(ROWS, half - start)
            low = start // 64 * 64
            keys = half - low
            rows = slice(start, start + size)
            of_row = jnp.broadcast_to(seg[:, start : start + ROWS], (ROWS, ROWS)).T[0:size]
            seen = widen(of_row, half)[:, low:] == jnp.broadcast_to(of_keys, (size, half))[:, low:]
            bias = jnp.where(seen, 0.0, NEG)
            lane = lax.broadcasted_iota(jnp.int32, (size, LANES), 1)
            old_peaks = state_in[rows, width : width + LANES]
            old_totals = state_in[rows, width + LANES : width + 2 * LANES]
            peaks, totals = old_peaks, old_totals
            for h in range(heads):
                cols = head_cols(h)
                queries = jnp.concatenate([q_ref[rows, c] for c in cols], axis=0)
                scores = dot_t(queries, tail[low:half, h * HEAD_DIM : (h + 1) * HEAD_DIM])
                scores = (scores.reshape(GROUP, size, keys) + bias[None]).reshape(GROUP * size, keys)
                own = jnp.concatenate([column(old_peaks, h * GROUP + g) for g in range(GROUP)], axis=0)
                peak = jnp.maximum(own, jnp.max(scores, axis=-1, keepdims=True))
                weights = jnp.exp2((scores - widen(peak, keys)) * EXP2_SCALE).astype(jnp.bfloat16)
                sums = jnp.dot(
                    weights,
                    wide[low:half, 2 * h * HEAD_DIM : (2 * h + 2) * HEAD_DIM],
                    preferred_element_type=jnp.float32,
                )
                total = jnp.concatenate([column(old_totals, h * GROUP + g) for g in range(GROUP)], axis=0)
                total = total * jnp.exp2((own - peak) * EXP2_SCALE)
                acc = jnp.concatenate([state_in[rows, c] for c in cols], axis=0) * total + sums[:, :HEAD_DIM]
                total = total + sums[:, HEAD_DIM:]
                acc = acc / total
                for g, c in enumerate(cols):
                    mine = slice(g * size, (g + 1) * size)
                    state[rows, c] = acc[mine]
                    here = lane == h * GROUP + g
                    peaks = jnp.where(here, peak[mine], peaks)
                    totals = jnp.where(here, total[mine], totals)
            state[rows, width : width + LANES] = peaks
            state[rows, width + LANES : width + 2 * LANES] = totals


def final_kernel(place_ref, w_ref, v1_ref, v2_ref, v3_ref, state, ppeak_ref, out_ref, wide, staged, sem):
    count, width = staged.shape
    heads = width // HEAD_DIM // GROUP
    place = place_ref[0]
    span = GROUP * HEAD_DIM

    def copy(h, b):
        box = (pl.ds(b * ROWS, ROWS), pl.ds(h * span, span))
        return pltpu.make_async_copy(staged.at[box], out_ref.at[box], sem.at[h, b])

    blocks = [(h, b) for b in range(count // ROWS) for h in range(heads)]

    @pl.when(place == 0)
    def _():
        for h, b in blocks:
            box = (slice(b * ROWS, (b + 1) * ROWS), slice(h * span, (h + 1) * span))
            staged[box] = state[box].astype(jnp.bfloat16)
            copy(h, b).start()

    @pl.when(place > 0)
    def _():
        fill_ones(wide, heads)
        for where, v_ref in ((1, v1_ref), (2, v2_ref), (3, v3_ref)):
            pl.when(place == where)(functools.partial(with_ones, wide, v_ref, count, heads))
        for h, b in blocks:
            cols = head_cols(h)
            rows = slice(b * ROWS, (b + 1) * ROWS)
            own, prompt = state[rows, width : width + LANES], ppeak_ref[rows, :]
            peak = jnp.maximum(own, prompt)
            factors = jnp.exp2((prompt - peak) * EXP2_SCALE)
            totals = state[rows, width + LANES : width + 2 * LANES] * jnp.exp2((own - peak) * EXP2_SCALE)
            first = (h * (count // ROWS) + b) * GROUP * ROWS
            sums = jnp.dot(
                w_ref[first : first + GROUP * ROWS, :],
                wide[:, 2 * h * HEAD_DIM : (2 * h + 2) * HEAD_DIM],
                preferred_element_type=jnp.float32,
            )
            for g, c in enumerate(cols):
                mine = slice(g * ROWS, (g + 1) * ROWS)
                total, factor = column(totals, h * GROUP + g), column(factors, h * GROUP + g)
                acc = state[rows, c] * total + sums[mine, :HEAD_DIM] * factor
                staged[rows, c] = (acc / (total + sums[mine, HEAD_DIM:] * factor)).astype(jnp.bfloat16)
            copy(h, b).start()

    for h, b in blocks:
        copy(h, b).wait()


def params(mebibytes):
    return pltpu.CompilerParams(vmem_limit_bytes=mebibytes << 20)


def cost(flops):
    return pl.CostEstimate(flops=flops, bytes_accessed=1, transcendentals=0)


def prompt_block_path(queries, keys, values, segment_ids):
    count, kv_width = keys.shape
    width = queries.shape[1]
    half = count // 2
    blocks = count // ROWS
    place = lax.axis_index("ctx").astype(jnp.int32).reshape(1)
    in_hbm = [pltpu.with_memory_space_constraint(x, pltpu.HBM) for x in (queries, keys, values, segment_ids)]

    keys_2 = lax.ppermute(keys, "ctx", [(0, 2)])
    values_2 = lax.ppermute(values, "ctx", [(0, 2)])
    mixed_shape = jax.ShapeDtypeStruct(keys.shape, jnp.bfloat16)
    mixed = pl.pallas_call(
        pack_kernel,
        out_shape=mixed_shape,
        in_specs=[SMEM] + [HBM] * 3,
        out_specs=VMEM,
        scratch_shapes=[pltpu.VMEM(segment_ids.shape, jnp.int32), pltpu.SemaphoreType.DMA((3,))],
        compiler_params=params(2),
        cost_estimate=cost(1),
        name="pack",
    )(place, *in_hbm[1:])
    tail_3 = lax.ppermute(mixed, "ctx", [(2, 3)])

    state_shape = jax.ShapeDtypeStruct((count, width + 2 * LANES), jnp.float32)
    state = pl.pallas_call(
        own_kernel,
        out_shape=state_shape,
        in_specs=[HBM] * 4,
        out_specs=VMEM,
        scratch_shapes=[
            pltpu.VMEM(queries.shape, jnp.bfloat16),
            pltpu.VMEM(keys.shape, jnp.bfloat16),
            pltpu.VMEM(keys.shape, jnp.bfloat16),
            pltpu.VMEM(segment_ids.shape, jnp.int32),
            pltpu.VMEM((count, count), jnp.float32),
            pltpu.VMEM((count, 2 * kv_width), jnp.bfloat16),
            pltpu.SemaphoreType.DMA((blocks + 3,)),
        ],
        compiler_params=params(10),
        cost_estimate=cost(16 * count * count * width),
        name="own",
    )(*in_hbm)

    keys_2, state = lax.optimization_barrier((keys_2, state))
    keys_3 = lax.ppermute(keys_2, "ctx", [(2, 3)])
    keys_1 = lax.ppermute(keys_2, "ctx", [(2, 1)])
    mixed, state = lax.optimization_barrier((mixed, state))
    from_left = lax.ppermute(mixed, "ctx", [(0, 1), (1, 2)])
    values_2, tail_3 = lax.optimization_barrier((values_2, tail_3))
    values_3 = lax.ppermute(values_2, "ctx", [(2, 3)])

    weights, prompt_peak = pl.pallas_call(
        prompt_scores_kernel,
        out_shape=(
            jax.ShapeDtypeStruct((count * width // HEAD_DIM, count), jnp.bfloat16),
            jax.ShapeDtypeStruct((count, LANES), jnp.float32),
        ),
        in_specs=[SMEM] + [VMEM] * 4,
        out_specs=(VMEM,) * 2,
        compiler_params=params(8),
        cost_estimate=cost(1),
        name="prompt_scores",
    )(place, queries, keys_1, keys_2, keys_3)

    state = pl.pallas_call(
        tail_kernel,
        out_shape=state_shape,
        in_specs=[SMEM] + [VMEM] * 5,
        out_specs=VMEM,
        scratch_shapes=[pltpu.VMEM(mixed.shape, jnp.bfloat16), pltpu.VMEM((half, 2 * kv_width), jnp.bfloat16)],
        input_output_aliases={5: 0},
        compiler_params=params(8),
        cost_estimate=cost(1),
        name="tail",
    )(place, queries, from_left, tail_3, segment_ids, state)

    return pl.pallas_call(
        final_kernel,
        out_shape=jax.ShapeDtypeStruct(queries.shape, jnp.bfloat16),
        in_specs=[SMEM] + [VMEM] * 6,
        out_specs=pl.BlockSpec(memory_space=pl.ANY),
        scratch_shapes=[
            pltpu.VMEM((count, 2 * kv_width), jnp.bfloat16),
            pltpu.VMEM(queries.shape, jnp.bfloat16),
            pltpu.SemaphoreType.DMA((kv_width // HEAD_DIM, blocks)),
        ],
        compiler_params=params(8),
        cost_estimate=cost(1),
        name="final",
    )(place, weights, from_left, values_2, values_3, state, prompt_peak)


def attend_block(
    running,
    key_block,
    value_block,
    segment_block,
    first_row,
    query_heads,
    query_places,
    query_segment,
):
    number = key_block.shape[0]
    heads_here = key_block.shape[1] // HEAD_DIM
    key_places = first_row + jnp.arange(number, dtype=jnp.int32)
    same = (segment_block[None, :] == query_segment[:, None]) | (segment_block[None, :] == 0)
    visible = (key_places[None, :] <= query_places[:, None]) & same
    key_heads = key_block.reshape(number, heads_here, HEAD_DIM)
    value_heads = value_block.reshape(number, heads_here, HEAD_DIM)

    def compute(state):
        row_peak, row_total, weighted = state
        scores = jnp.einsum(
            "qhgd,khd->hgqk", query_heads, key_heads, preferred_element_type=jnp.float32
        ) * HEAD_DIM ** (-0.5)
        scores = jnp.where(visible[None, None], scores, -1e30)
        new_peak = jnp.maximum(row_peak, jnp.max(scores, axis=-1))
        factor = jnp.exp(row_peak - new_peak)
        weights = jnp.where(visible[None, None], jnp.exp(scores - new_peak[..., None]), 0.0)
        new_total = row_total * factor + jnp.sum(weights, axis=-1)
        added = jnp.einsum(
            "hgqk,khd->hgqd",
            weights.astype(jnp.bfloat16),
            value_heads,
            preferred_element_type=jnp.float32,
        )
        return (new_peak, new_total, weighted * factor[..., None] + added)

    return lax.cond(jnp.any(visible), compute, lambda state: state, running)


def gathered_path(queries, keys, values, segment_ids):
    row_count = queries.shape[0]
    heads_here = keys.shape[1] // HEAD_DIM
    my_index = lax.axis_index("ctx")
    query_places = my_index * row_count + jnp.arange(row_count, dtype=jnp.int32)
    query_heads = queries.reshape(row_count, heads_here, GROUP, HEAD_DIM)
    initial = (
        jnp.full((heads_here, GROUP, row_count), -1e30, jnp.float32),
        jnp.zeros((heads_here, GROUP, row_count), jnp.float32),
        jnp.zeros((heads_here, GROUP, row_count, HEAD_DIM), jnp.float32),
    )
    key_all = lax.all_gather(keys, "ctx", axis=0, tiled=True)
    value_all = lax.all_gather(values, "ctx", axis=0, tiled=True)
    segment_all = lax.all_gather(segment_ids, "ctx", axis=0, tiled=True)
    blocks = max(1, key_all.shape[0] // row_count)
    width_rows = key_all.shape[0] // blocks

    def turn(number, state):
        offset = number * width_rows
        key_part = lax.dynamic_slice_in_dim(key_all, offset, width_rows, 0)
        value_part = lax.dynamic_slice_in_dim(value_all, offset, width_rows, 0)
        segment_part = lax.dynamic_slice_in_dim(segment_all, offset, width_rows, 0)
        return attend_block(
            state, key_part, value_part, segment_part, offset, query_heads, query_places, segment_ids
        )

    row_peak, row_total, weighted = lax.fori_loop(0, blocks, turn, initial)
    mixed = weighted / row_total[..., None]
    mixed = jnp.transpose(mixed, (2, 0, 1, 3)).reshape(row_count, heads_here * GROUP * HEAD_DIM)
    return mixed.astype(jnp.bfloat16)


def per_device(parts, queries, keys, values, segment_ids):
    rows = queries.shape[0]
    tokens = rows * parts
    prompt, chain = tokens // 4, tokens // 8
    if parts == 4 and prompt == rows and 2 * chain == rows and rows % ROWS == 0 and keys.shape[1] >= chain:
        return prompt_block_path(queries, keys, values, segment_ids)
    return gathered_path(queries, keys, values, segment_ids)


def solution(mesh):
    placed = (
        P(("groups", "ctx"), ("tp", "sub")),
        P(("groups", "ctx"), ("tp", "sub")),
        P(("groups", "ctx"), ("tp", "sub")),
        P(("groups", "ctx")),
    )
    return jax.shard_map(
        functools.partial(per_device, mesh.shape["ctx"]),
        mesh=mesh,
        in_specs=placed,
        out_specs=P(("groups", "ctx"), ("tp", "sub")),
        check_vma=False,
    )
```

time: 38.3 us -> 29.6 us (0.77)
  the two profiles are of different devices: /device:TPU:28 before, /device:TPU:22 now
where the time goes in v2:
time: 29.6 us; the launch traced here: 29.3 us
  Pallas kernels  15.3 us (52%)
  starting transfers between devices  10.2 us (34%)
  waiting for transfers between devices  3.56 us (12%)
  between operations  0.3 us (1%)
    pallas_call x1, Pallas kernels, prompt_block_path(): pl.pallas_call(own_kernel, out_shape=state_shape, in_specs=[HBM] * 4, out...  4.77 us
    pallas_call x1, Pallas kernels, prompt_block_path(): pl.pallas_call(tail_kernel, out_shape=state_shape, in_specs=[SMEM] + [VME...  4.12 us
    pallas_call x1, Pallas kernels, prompt_block_path(): pl.pallas_call(final_kernel, out_shape=jax.ShapeDtypeStruct(queries.shape...  3.23 us
    ppermute x1, starting transfers between devices, prompt_block_path(): tail_3 = lax.ppermute(mixed, 'ctx', [(2, 3)])  2.39 us
    pallas_call x1, Pallas kernels, prompt_block_path(): pl.pallas_call(prompt_scores_kernel, out_shape=(jax.ShapeDtypeStruct((cou...  2.06 us
    ppermute x1, waiting for transfers between devices, prompt_block_path(): from_left = lax.ppermute(mixed, 'ctx', [(0, 1), (1, 2)])  2.06 us
    ppermute x1, starting transfers between devices, prompt_block_path(): keys_3 = lax.ppermute(keys_2, 'ctx', [(2, 3)])  1.3 us
    ppermute x1, starting transfers between devices, prompt_block_path(): keys_1 = lax.ppermute(keys_2, 'ctx', [(2, 1)])  1.3 us
  transfers between devices with their start and end apart: 7, of which 3 were waited for; matrix products, arithmetic and copies ran while one was open for 0% of the time, Pallas kernels for 41%

profile of v2, /device:TPU:22, one launch (start us, length us, event | category | flops | bytes accessed | tf_op | source)
XLA Modules:
  0.0 29.3 jit_solution(10550617564132289808)
XLA Ops:
  0.0 1.3 %collective-permute-start = (bf16[384,256]{1,0:T(8,128)(2,1)}, bf16[384,256]{1,0:T(8,128)(2,1)S(1)}, u32[]{:S(2)}, u32[]{:S(2)}) collective-permute-start(bf16[384,256]{1,0:T(8,128)(2,1)} %k_hbm.3), channel_id=1, source_target_pairs={{0,8},{1,9},{2,10},{3,11},{16,24},{17,25},{18,26},{19,27}} | collective-permute-start | bytes 589832 | tf_op jit(solution)/shard_map/ppermute | solution.py:293
  1.3 1.3 %collective-permute-start.4 = (bf16[384,256]{1,0:T(8,128)(2,1)}, bf16[384,256]{1,0:T(8,128)(2,1)S(1)}, u32[]{:S(2)}, u32[]{:S(2)}) collective-permute-start(bf16[384,256]{1,0:T(8,128)(2,1)} %v_hbm.3), channel_id=1, source_target_pairs={{0,8},{1,9},{2,10},{3,11},{16,24},{17,25},{18,26},{19,27}} | collective-permute-start | bytes 589832 | tf_op jit(solution)/shard_map/ppermute | solution.py:294
  2.6 1.1 %pack.1 = bf16[384,256]{1,0:T(8,128)(2,1)S(1)} custom-call(s32[1]{0:T(128)} %bitcast.place_ref, bf16[384,256]{1,0:T(8,128)(2,1)} %k_hbm.3, bf16[384,256]{1,0:T(8,128)(2,1)} %v_hbm.3, s32[384]{0:T(512)} %seg_ref.1), custom_call_target="tpu_custom_call" | custom-call | flops 1 | bytes 1 | tf_op jit(solution)/shard_map/pack/pallas_call | solution.py:296
  3.7 0.0 copy-start
  3.7 0.0 copy-start.1
  3.7 2.4 %collective-permute-start.5 = (bf16[384,256]{1,0:T(8,128)(2,1)S(1)}, bf16[384,256]{1,0:T(8,128)(2,1)S(1)}, u32[]{:S(2)}, u32[]{:S(2)}) collective-permute-start(bf16[384,256]{1,0:T(8,128)(2,1)S(1)} %pack.1), channel_id=1, source_target_pairs={{8,12},{9,13},{10,14},{11,15},{24,28},{25,29},{26,30},{27,31}} | collective-permute-start | bytes 589832 | tf_op jit(solution)/shard_map/ppermute | solution.py:306
  6.1 4.8 %own.1.state_in = f32[384,2304]{1,0:T(8,128)S(1)} custom-call(bf16[384,2048]{1,0:T(8,128)(2,1)} %q_ref.3, bf16[384,256]{1,0:T(8,128)(2,1)} %k_hbm.3, bf16[384,256]{1,0:T(8,128)(2,1)} %v_hbm.3, s32[384]{0:T(512)} %seg_ref.1), custom_call_target="tpu_custom_call" | custom-call | flops 4831838208 | bytes 1 | tf_op jit(solution)/shard_map/own/pallas_call | solution.py:309
  10.9 0.0 collective-permute-done.k2_ref
  10.9 1.3 %collective-permute-start.2 = (bf16[384,256]{1,0:T(8,128)(2,1)S(1)}, bf16[384,256]{1,0:T(8,128)(2,1)S(1)}, u32[]{:S(2)}, u32[]{:S(2)}) collective-permute-start(bf16[384,256]{1,0:T(8,128)(2,1)S(1)} %collective-permute-done.k2_ref), channel_id=1, source_target_pairs={{8,12},{9,13},{10,14},{11,15},{24,28},{25,29},{26,30},{27,31}} | collective-permute-start | bytes 589832 | tf_op jit(solution)/shard_map/ppermute | solution.py:329
  12.2 1.3 %collective-permute-start.1 = (bf16[384,256]{1,0:T(8,128)(2,1)S(1)}, bf16[384,256]{1,0:T(8,128)(2,1)S(1)}, u32[]{:S(2)}, u32[]{:S(2)}) collective-permute-start(bf16[384,256]{1,0:T(8,128)(2,1)S(1)} %collective-permute-done.k2_ref), channel_id=1, source_target_pairs={{8,4},{9,5},{10,6},{11,7},{24,20},{25,21},{26,22},{27,23}} | collective-permute-start | bytes 589832 | tf_op jit(solution)/shard_map/ppermute | solution.py:330
  13.5 1.3 %collective-permute-start.3 = (bf16[384,256]{1,0:T(8,128)(2,1)S(1)}, bf16[384,256]{1,0:T(8,128)(2,1)S(1)}, u32[]{:S(2)}, u32[]{:S(2)}) collective-permute-start(bf16[384,256]{1,0:T(8,128)(2,1)S(1)} %pack.1), channel_id=1, source_target_pairs={{0,4},{4,8},{1,5},{5,9},{2,6},{6,10},{3,7},{7,11},{16,20},{20,24},... | collective-permute-start | bytes 589832 | tf_op jit(solution)/shard_map/ppermute | solution.py:332
  14.8 0.0 collective-permute-done.5.t3_ref
  14.8 0.0 collective-permute-done.4.v2_ref
  14.8 1.3 %collective-permute-start.6 = (bf16[384,256]{1,0:T(8,128)(2,1)S(1)}, bf16[384,256]{1,0:T(8,128)(2,1)S(1)}, u32[]{:S(2)}, u32[]{:S(2)}) collective-permute-start(bf16[384,256]{1,0:T(8,128)(2,1)S(1)} %collective-permute-done.4.v2_ref), channel_id=1, source_target_pairs={{8,12},{9,13},{10,14},{11,15},{24,28},{25,29},{26,30},{27,31}} | collective-permute-start | bytes 589832 | tf_op jit(solution)/shard_map/ppermute | solution.py:334
  16.1 0.4 %collective-permute-done.2.k3_ref = bf16[384,256]{1,0:T(8,128)(2,1)S(1)} collective-permute-done((bf16[384,256]{1,0:T(8,128)(2,1)S(1)}, bf16[384,256]{1,0:T(8,128)(2,1)S(1)}, u32[]{:S(2)}, u32[]{:S(2)}) %collective-permute-start.2) | collective-permute-done | bytes 196640 | tf_op jit(solution)/shard_map/ppermute | solution.py:329
  16.5 1.1 %collective-permute-done.1.k1_ref = bf16[384,256]{1,0:T(8,128)(2,1)S(1)} collective-permute-done((bf16[384,256]{1,0:T(8,128)(2,1)S(1)}, bf16[384,256]{1,0:T(8,128)(2,1)S(1)}, u32[]{:S(2)}, u32[]{:S(2)}) %collective-permute-start.1) | collective-permute-done | bytes 196640 | tf_op jit(solution)/shard_map/ppermute | solution.py:330
  17.6 0.0 copy-done
  17.6 2.1 %prompt_scores.1 = (bf16[6144,384]{1,0:T(8,128)(2,1)S(1)}, f32[384,128]{1,0:T(8,128)S(1)}) custom-call(s32[1]{0:T(128)} %bitcast.place_ref, bf16[384,2048]{1,0:T(8,128)(2,1)S(1)} %copy-done, bf16[384,256]{1,0:T(8,128)(2,1)S(1)} %collective-permute-done.1.k1_ref, bf16[384,256]{1,0:T(8,128)(2,1)S(1)} %collective-permute-done.k2_ref, ...), custom_call_target="tpu_custom_call" | custom-call | flops 1 | bytes 1 | tf_op jit(solution)/shard_map/prompt_scores/pallas_call | solution.py:336
  19.7 2.1 %collective-permute-done.3.t2_ref.v1_ref = bf16[384,256]{1,0:T(8,128)(2,1)S(1)} collective-permute-done((bf16[384,256]{1,0:T(8,128)(2,1)S(1)}, bf16[384,256]{1,0:T(8,128)(2,1)S(1)}, u32[]{:S(2)}, u32[]{:S(2)}) %collective-permute-start.3) | collective-permute-done | bytes 196640 | tf_op jit(solution)/shard_map/ppermute | solution.py:332
  21.8 0.0 copy-done.1
  21.8 4.1 %tail.1.state = f32[384,2304]{1,0:T(8,128)S(1)} custom-call(s32[1]{0:T(128)} %bitcast.place_ref, bf16[384,2048]{1,0:T(8,128)(2,1)S(1)} %copy-done, bf16[384,256]{1,0:T(8,128)(2,1)S(1)} %collective-permute-done.3.t2_ref.v1_ref, bf16[384,256]{1,0:T(8,128)(2,1)S(1)} %collective-permute-done.5.t3_ref, s32[384]{0:T(512)S(1)} %copy-done.1, ...), custom_call_target="tpu_custom_call", output_to_operand_aliasing={{}: (5, {})} | custom-call | flops 1 | bytes 1 | tf_op jit(solution)/shard_map/tail/pallas_call | solution.py:349
  25.9 0.0 collective-permute-done.6.v3_ref
  25.9 3.2 %final.1 = bf16[384,2048]{1,0:T(8,128)(2,1)} custom-call(s32[1]{0:T(128)} %bitcast.place_ref, bf16[6144,384]{1,0:T(8,128)(2,1)S(1)} %get-tuple-element.14.w_ref, bf16[384,256]{1,0:T(8,128)(2,1)S(1)} %collective-permute-done.3.t2_ref.v1_ref, bf16[384,256]{1,0:T(8,128)(2,1)S(1)} %collective-permute-done.4.v2_ref, ...), custom_call_target="tpu_custom_call" | custom-call | flops 1 | bytes 1 | tf_op jit(solution)/shard_map/final/pallas_call | solution.py:361
Async XLA Ops:
  0.0 10.9 %collective-permute-start = (bf16[384,256]{1,0:T(8,128)(2,1)}, bf16[384,256]{1,0:T(8,128)(2,1)S(1)}, u32[]{:S(2)}, u32[]{:S(2)}) collective-permute-start(bf16[384,256]{1,0:T(8,128)(2,1)} %k_hbm.3), channel_id=1, source_target_pairs={{0,8},{1,9},{2,10},{3,11},{16,24},{17,25},{18,26},{19,27}} | collective-permute-start | bytes 589832 | tf_op jit(solution)/shard_map/ppermute | solution.py:293
  1.3 13.5 %collective-permute-start.4 = (bf16[384,256]{1,0:T(8,128)(2,1)}, bf16[384,256]{1,0:T(8,128)(2,1)S(1)}, u32[]{:S(2)}, u32[]{:S(2)}) collective-permute-start(bf16[384,256]{1,0:T(8,128)(2,1)} %v_hbm.3), channel_id=1, source_target_pairs={{0,8},{1,9},{2,10},{3,11},{16,24},{17,25},{18,26},{19,27}} | collective-permute-start | bytes 589832 | tf_op jit(solution)/shard_map/ppermute | solution.py:294
  3.7 14.0 %copy-start = (bf16[384,2048]{1,0:T(8,128)(2,1)S(1)}, bf16[384,2048]{1,0:T(8,128)(2,1)}, u32[]{:S(2)}) copy-start(bf16[384,2048]{1,0:T(8,128)(2,1)} %q_ref.3) | copy-start | bytes 4718596
  3.7 18.1 %copy-start.1 = (s32[384]{0:T(512)S(1)}, s32[384]{0:T(512)}, u32[]{:S(2)}) copy-start(s32[384]{0:T(512)} %seg_ref.1) | copy-start | bytes 4612
  3.7 11.1 %collective-permute-start.5 = (bf16[384,256]{1,0:T(8,128)(2,1)S(1)}, bf16[384,256]{1,0:T(8,128)(2,1)S(1)}, u32[]{:S(2)}, u32[]{:S(2)}) collective-permute-start(bf16[384,256]{1,0:T(8,128)(2,1)S(1)} %pack.1), channel_id=1, source_target_pairs={{8,12},{9,13},{10,14},{11,15},{24,28},{25,29},{26,30},{27,31}} | collective-permute-start | bytes 589832 | tf_op jit(solution)/shard_map/ppermute | solution.py:306
  10.9 5.6 %collective-permute-start.2 = (bf16[384,256]{1,0:T(8,128)(2,1)S(1)}, bf16[384,256]{1,0:T(8,128)(2,1)S(1)}, u32[]{:S(2)}, u32[]{:S(2)}) collective-permute-start(bf16[384,256]{1,0:T(8,128)(2,1)S(1)} %collective-permute-done.k2_ref), channel_id=1, source_target_pairs={{8,12},{9,13},{10,14},{11,15},{24,28},{25,29},{26,30},{27,31}} | collective-permute-start | bytes 589832 | tf_op jit(solution)/shard_map/ppermute | solution.py:329
  12.2 5.4 %collective-permute-start.1 = (bf16[384,256]{1,0:T(8,128)(2,1)S(1)}, bf16[384,256]{1,0:T(8,128)(2,1)S(1)}, u32[]{:S(2)}, u32[]{:S(2)}) collective-permute-start(bf16[384,256]{1,0:T(8,128)(2,1)S(1)} %collective-permute-done.k2_ref), channel_id=1, source_target_pairs={{8,4},{9,5},{10,6},{11,7},{24,20},{25,21},{26,22},{27,23}} | collective-permute-start | bytes 589832 | tf_op jit(solution)/shard_map/ppermute | solution.py:330
  13.5 8.3 %collective-permute-start.3 = (bf16[384,256]{1,0:T(8,128)(2,1)S(1)}, bf16[384,256]{1,0:T(8,128)(2,1)S(1)}, u32[]{:S(2)}, u32[]{:S(2)}) collective-permute-start(bf16[384,256]{1,0:T(8,128)(2,1)S(1)} %pack.1), channel_id=1, source_target_pairs={{0,4},{4,8},{1,5},{5,9},{2,6},{6,10},{3,7},{7,11},{16,20},{20,24},... | collective-permute-start | bytes 589832 | tf_op jit(solution)/shard_map/ppermute | solution.py:332
  14.8 11.1 %collective-permute-start.6 = (bf16[384,256]{1,0:T(8,128)(2,1)S(1)}, bf16[384,256]{1,0:T(8,128)(2,1)S(1)}, u32[]{:S(2)}, u32[]{:S(2)}) collective-permute-start(bf16[384,256]{1,0:T(8,128)(2,1)S(1)} %collective-permute-done.4.v2_ref), channel_id=1, source_target_pairs={{8,12},{9,13},{10,14},{11,15},{24,28},{25,29},{26,30},{27,31}} | collective-permute-start | bytes 589832 | tf_op jit(solution)/shard_map/ppermute | solution.py:334

commit v3 on v2

--- a/solution.py
+++ b/solution.py
@@ -26,6 +26,10 @@
 def head_cols(kv_head):
     first = kv_head * GROUP * HEAD_DIM
     return [slice(first + g * HEAD_DIM, first + (g + 1) * HEAD_DIM) for g in range(GROUP)]
+
+
+def shifted(cols, by):
+    return [slice(c.start + by, c.stop + by) for c in cols]
 
 
 def stack(ref, rows, cols):
@@ -136,12 +140,13 @@
         state[rows, width + LANES : width + 2 * LANES] = totals
 
 
-def prompt_scores_kernel(place_ref, q_ref, k1_ref, k2_ref, k3_ref, w_ref, peak_ref):
+def scores_kernel(here, place_ref, q_ref, k_ref, w_ref, peak_ref):
     count = q_ref.shape[0]
-    heads = k1_ref.shape[1] // HEAD_DIM
-    lane = lax.broadcasted_iota(jnp.int32, (ROWS, LANES), 1)
-
-    def compute(k_ref):
+    heads = k_ref.shape[1] // HEAD_DIM
+
+    @pl.when(place_ref[0] == here)
+    def _():
+        lane = lax.broadcasted_iota(jnp.int32, (ROWS, LANES), 1)
         for b in range(count // ROWS):
             rows = slice(b * ROWS, (b + 1) * ROWS)
             peaks = jnp.zeros((ROWS, LANES), jnp.float32)
@@ -156,122 +161,198 @@
                     peaks = jnp.where(lane == h * GROUP + g, peak[g * ROWS : (g + 1) * ROWS], peaks)
             peak_ref[rows, :] = peaks
 
-    for place, k_ref in ((1, k1_ref), (2, k2_ref), (3, k3_ref)):
-        pl.when(place_ref[0] == place)(functools.partial(compute, k_ref))
-
 
 def column(stats, index):
     return jnp.broadcast_to(stats[:, index : index + 1], (stats.shape[0], LANES))
 
 
-def tail_kernel(place_ref, q_ref, t2_ref, t3_ref, seg_ref, state_in, state, tail, wide):
+def merge_tail(q_ref, t_ref, seg_ref, peaks_of, tail, wide, finish):
     count, width = q_ref.shape
     heads = width // HEAD_DIM // GROUP
     half = count // 2
-    place = place_ref[0]
-
-    @pl.when(place == 2)
-    def _():
-        tail[...] = t2_ref[...]
-
-    @pl.when(place == 3)
-    def _():
-        tail[...] = t3_ref[...]
-
-    @pl.when(place > 1)
-    def _():
-        fill_ones(wide, heads)
+    padded = tail.shape[0]
+    pad = padded - half
+    fill_ones(wide, heads)
+    for h in range(heads):
+        mine = slice(h * HEAD_DIM, (h + 1) * HEAD_DIM)
+        tail[0:pad, mine] = jnp.zeros((pad, HEAD_DIM), jnp.bfloat16)
+        tail[pad:padded, mine] = t_ref[0:half, mine]
+        wide[0:pad, 2 * h * HEAD_DIM : (2 * h + 1) * HEAD_DIM] = jnp.zeros((pad, HEAD_DIM), jnp.bfloat16)
+        wide[pad:padded, 2 * h * HEAD_DIM : (2 * h + 1) * HEAD_DIM] = t_ref[half : 2 * half, mine]
+    of_keys = t_ref[0:16, 0:half].astype(jnp.float32)[0:1]
+    of_keys = jnp.concatenate([jnp.full((1, pad), -1.0, jnp.float32), of_keys], axis=1)
+    of_keys = jnp.where(lax.broadcasted_iota(jnp.int32, (1, padded), 1) <= pad, -1.0, of_keys)
+    seg = seg_ref[...].reshape(1, count).astype(jnp.float32)
+    for start in range(0, half, ROWS):
+        size = min(ROWS, half - start)
+        low = (start + pad) // LANES * LANES
+        keys = padded - low
+        rows = slice(start, start + size)
+        of_row = jnp.broadcast_to(seg[:, start : start + ROWS], (ROWS, ROWS)).T[0:size]
+        seen = widen(of_row, keys) == jnp.broadcast_to(of_keys[:, low:], (size, keys))
+        bias = jnp.where(seen, 0.0, NEG)
         for h in range(heads):
-            wide[:, 2 * h * HEAD_DIM : (2 * h + 1) * HEAD_DIM] = tail[half : 2 * half, h * HEAD_DIM : (h + 1) * HEAD_DIM]
-        of_keys = tail[0:16, 0:half].astype(jnp.float32)[0:1]
-        of_keys = jnp.where(lax.broadcasted_iota(jnp.int32, (1, half), 1) == 0, -1.0, of_keys)
-        seg = seg_ref[...].reshape(1, count).astype(jnp.float32)
-        for start in range(0, half, ROWS):
-            size = min(ROWS, half - start)
-            low = start // 64 * 64
-            keys = half - low
-            rows = slice(start, start + size)
-            of_row = jnp.broadcast_to(seg[:, start : start + ROWS], (ROWS, ROWS)).T[0:size]
-            seen = widen(of_row, half)[:, low:] == jnp.broadcast_to(of_keys, (size, half))[:, low:]
-            bias = jnp.where(seen, 0.0, NEG)
-            lane = lax.broadcasted_iota(jnp.int32, (size, LANES), 1)
-            old_peaks = state_in[rows, width : width + LANES]
-            old_totals = state_in[rows, width + LANES : width + 2 * LANES]
-            peaks, totals = old_peaks, old_totals
-            for h in range(heads):
-                cols = head_cols(h)
-                queries = jnp.concatenate([q_ref[rows, c] for c in cols], axis=0)
-                scores = dot_t(queries, tail[low:half, h * HEAD_DIM : (h + 1) * HEAD_DIM])
-                scores = (scores.reshape(GROUP, size, keys) + bias[None]).reshape(GROUP * size, keys)
-                own = jnp.concatenate([column(old_peaks, h * GROUP + g) for g in range(GROUP)], axis=0)
-                peak = jnp.maximum(own, jnp.max(scores, axis=-1, keepdims=True))
-                weights = jnp.exp2((scores - widen(peak, keys)) * EXP2_SCALE).astype(jnp.bfloat16)
-                sums = jnp.dot(
-                    weights,
-                    wide[low:half, 2 * h * HEAD_DIM : (2 * h + 2) * HEAD_DIM],
-                    preferred_element_type=jnp.float32,
-                )
-                total = jnp.concatenate([column(old_totals, h * GROUP + g) for g in range(GROUP)], axis=0)
-                total = total * jnp.exp2((own - peak) * EXP2_SCALE)
-                acc = jnp.concatenate([state_in[rows, c] for c in cols], axis=0) * total + sums[:, :HEAD_DIM]
-                total = total + sums[:, HEAD_DIM:]
-                acc = acc / total
-                for g, c in enumerate(cols):
-                    mine = slice(g * size, (g + 1) * size)
-                    state[rows, c] = acc[mine]
-                    here = lane == h * GROUP + g
-                    peaks = jnp.where(here, peak[mine], peaks)
-                    totals = jnp.where(here, total[mine], totals)
-            state[rows, width : width + LANES] = peaks
-            state[rows, width + LANES : width + 2 * LANES] = totals
-
-
-def final_kernel(place_ref, w_ref, v1_ref, v2_ref, v3_ref, state, ppeak_ref, out_ref, wide, staged, sem):
-    count, width = staged.shape
-    heads = width // HEAD_DIM // GROUP
-    place = place_ref[0]
-    span = GROUP * HEAD_DIM
-
-    def copy(h, b):
-        box = (pl.ds(b * ROWS, ROWS), pl.ds(h * span, span))
-        return pltpu.make_async_copy(staged.at[box], out_ref.at[box], sem.at[h, b])
-
-    blocks = [(h, b) for b in range(count // ROWS) for h in range(heads)]
-
-    @pl.when(place == 0)
-    def _():
-        for h, b in blocks:
-            box = (slice(b * ROWS, (b + 1) * ROWS), slice(h * span, (h + 1) * span))
-            staged[box] = state[box].astype(jnp.bfloat16)
-            copy(h, b).start()
-
-    @pl.when(place > 0)
-    def _():
-        fill_ones(wide, heads)
-        for where, v_ref in ((1, v1_ref), (2, v2_ref), (3, v3_ref)):
-            pl.when(place == where)(functools.partial(with_ones, wide, v_ref, count, heads))
-        for h, b in blocks:
             cols = head_cols(h)
-            rows = slice(b * ROWS, (b + 1) * ROWS)
-            own, prompt = state[rows, width : width + LANES], ppeak_ref[rows, :]
-            peak = jnp.maximum(own, prompt)
-            factors = jnp.exp2((prompt - peak) * EXP2_SCALE)
-            totals = state[rows, width + LANES : width + 2 * LANES] * jnp.exp2((own - peak) * EXP2_SCALE)
+            queries = jnp.concatenate([q_ref[rows, c] for c in cols], axis=0)
+            scores = dot_t(queries, tail[low:padded, h * HEAD_DIM : (h + 1) * HEAD_DIM])
+            scores = (scores.reshape(GROUP, size, keys) + bias[None]).reshape(GROUP * size, keys)
+            own = peaks_of(rows, h)
+            peak = jnp.maximum(own, jnp.max(scores, axis=-1, keepdims=True))
+            weights = jnp.exp2((scores - widen(peak, keys)) * EXP2_SCALE).astype(jnp.bfloat16)
+            sums = jnp.dot(
+                weights, wide[low:padded, 2 * h * HEAD_DIM : (2 * h + 2) * HEAD_DIM], preferred_element_type=jnp.float32
+            )
+            scale = jnp.exp2((own - peak) * EXP2_SCALE)
+            finish(rows, h, cols, peak, scale, sums)
+
+
+def tail_kernel(place_ref, q_ref, t_ref, seg_ref, state_in, state, tail, wide):
+    width = q_ref.shape[1]
+
+    def peaks_of(rows, h):
+        peaks = state_in[rows, width : width + LANES]
+        return jnp.concatenate([column(peaks, h * GROUP + g) for g in range(GROUP)], axis=0)
+
+    def finish(rows, h, cols, peak, scale, sums):
+        size = rows.stop - rows.start
+        lane = lax.broadcasted_iota(jnp.int32, (size, LANES), 1)
+        old_totals = state_in[rows, width + LANES : width + 2 * LANES]
+        peaks = state[rows, width : width + LANES]
+        totals = state[rows, width + LANES : width + 2 * LANES]
+        for g, c in enumerate(cols):
+            mine = slice(g * size, (g + 1) * size)
+            index = h * GROUP + g
+            old = column(old_totals, index) * scale[mine]
+            total = old + sums[mine, HEAD_DIM:]
+            state[rows, c] = (state[rows, c] * old + sums[mine, :HEAD_DIM]) / total
+            peaks = jnp.where(lane == index, peak[mine], peaks)
+            totals = jnp.where(lane == index, total, totals)
+        state[rows, width : width + LANES] = peaks
+        state[rows, width + LANES : width + 2 * LANES] = totals
+
+    @pl.when(place_ref[0] == 3)
+    def _():
+        merge_tail(q_ref, t_ref, seg_ref, peaks_of, tail, wide, finish)
+
+
+def put_out(staged, out_ref, sem, rows, h, waits):
+    box = (pl.ds(rows.start, rows.stop - rows.start), pl.ds(h * GROUP * HEAD_DIM, GROUP * HEAD_DIM))
+    waits.append(fetch(staged.at[box], out_ref.at[box], sem.at[rows.start // ROWS, h]))
+
+
+def prompt_blocks(w_ref, v_ref, state, ppeak_ref, wide, finish):
+    count = v_ref.shape[0]
+    heads = v_ref.shape[1] // HEAD_DIM
+    width = heads * GROUP * HEAD_DIM
+    fill_ones(wide, heads)
+    with_ones(wide, v_ref, count, heads)
+    for b in range(count // ROWS):
+        rows = slice(b * ROWS, (b + 1) * ROWS)
+        own, prompt = state[rows, width : width + LANES], ppeak_ref[rows, :]
+        peak = jnp.maximum(own, prompt)
+        prompt_scale = jnp.exp2((prompt - peak) * EXP2_SCALE)
+        own_total = state[rows, width + LANES : width + 2 * LANES] * jnp.exp2((own - peak) * EXP2_SCALE)
+        for h in range(heads):
             first = (h * (count // ROWS) + b) * GROUP * ROWS
             sums = jnp.dot(
                 w_ref[first : first + GROUP * ROWS, :],
                 wide[:, 2 * h * HEAD_DIM : (2 * h + 2) * HEAD_DIM],
                 preferred_element_type=jnp.float32,
             )
+            for g, c in enumerate(head_cols(h)):
+                index = h * GROUP + g
+                mine = slice(g * ROWS, (g + 1) * ROWS)
+                own_part, prompt_part = column(own_total, index), column(prompt_scale, index)
+                total = own_part + sums[mine, HEAD_DIM:] * prompt_part
+                value = (state[rows, c] * own_part + sums[mine, :HEAD_DIM] * prompt_part) / total
+                finish(rows, h, g, c, value, peak, total)
+
+
+def prompt_kernel(here, place_ref, w_ref, v_ref, state, ppeak_ref, *rest):
+    out_ref, wide, staged, sem = rest[-4:]
+    count, width = staged.shape
+    heads = width // HEAD_DIM // GROUP
+
+    if here == 1:
+
+        @pl.when(place_ref[0] == 0)
+        def _():
+            waits = []
+            for b in range(count // ROWS):
+                rows = slice(b * ROWS, (b + 1) * ROWS)
+                for h in range(heads):
+                    for c in head_cols(h):
+                        staged[rows, c] = state[rows, c].astype(jnp.bfloat16)
+                    put_out(staged, out_ref, sem, rows, h, waits)
+            for wait in waits:
+                wait.wait()
+
+    @pl.when(place_ref[0] == here)
+    def _():
+        waits = []
+
+        def finish(rows, h, g, c, value, peak, total):
+            staged[rows, c] = value.astype(jnp.bfloat16)
+            if g == GROUP - 1:
+                put_out(staged, out_ref, sem, rows, h, waits)
+
+        prompt_blocks(w_ref, v_ref, state, ppeak_ref, wide, finish)
+        for wait in waits:
+            wait.wait()
+
+
+def prompt_first_kernel(place_ref, w_ref, v_ref, state, ppeak_ref, out_ref, aux, wide, staged, sem):
+    width = staged.shape[1]
+
+    @pl.when(place_ref[0] == 2)
+    def _():
+        waits = []
+
+        def finish(rows, h, g, c, value, peak, total):
+            if rows.stop <= aux.shape[0]:
+                peak_cols, sum_cols = shifted([c], width)[0], shifted([c], 2 * width)[0]
+                aux[rows, c] = value
+                aux[rows, peak_cols] = column(peak, h * GROUP + g)
+                aux[rows, sum_cols] = total
+            else:
+                staged[rows, c] = value.astype(jnp.bfloat16)
+                if g == GROUP - 1:
+                    put_out(staged, out_ref, sem, rows, h, waits)
+
+        prompt_blocks(w_ref, v_ref, state, ppeak_ref, wide, finish)
+        for wait in waits:
+            wait.wait()
+
+
+def last_kernel(place_ref, q_ref, t_ref, seg_ref, aux, out_in, out_ref, tail, wide, staged, sem):
+    count, width = q_ref.shape
+    heads = width // HEAD_DIM // GROUP
+    half = count // 2
+
+    @pl.when(place_ref[0] == 2)
+    def _():
+        waits = []
+
+        def peaks_of(rows, h):
+            return stack(aux, rows, shifted(head_cols(h), width))
+
+        def finish(rows, h, cols, peak, scale, sums):
+            size = rows.stop - rows.start
             for g, c in enumerate(cols):
-                mine = slice(g * ROWS, (g + 1) * ROWS)
-                total, factor = column(totals, h * GROUP + g), column(factors, h * GROUP + g)
-                acc = state[rows, c] * total + sums[mine, :HEAD_DIM] * factor
-                staged[rows, c] = (acc / (total + sums[mine, HEAD_DIM:] * factor)).astype(jnp.bfloat16)
-            copy(h, b).start()
-
-    for h, b in blocks:
-        copy(h, b).wait()
+                mine = slice(g * size, (g + 1) * size)
+                total = aux[rows, shifted([c], 2 * width)[0]] * scale[mine]
+                value = (aux[rows, c] * total + sums[mine, :HEAD_DIM]) / (total + sums[mine, HEAD_DIM:])
+                staged[rows, c] = value.astype(jnp.bfloat16)
+            put_out(staged, out_ref, sem, rows, h, waits)
+
+        if aux.shape[0] > half:
+            rest = slice(half, aux.shape[0])
+            staged[rest, :] = aux[rest, 0:width].astype(jnp.bfloat16)
+            box = (pl.ds(half, aux.shape[0] - half), pl.ds(0, width))
+            waits.append(fetch(staged.at[box], out_ref.at[box], sem.at[count // ROWS, 0]))
+        merge_tail(q_ref, t_ref, seg_ref, peaks_of, tail, wide, finish)
+        for wait in waits:
+            wait.wait()
 
 
 def params(mebibytes):
@@ -286,12 +367,12 @@
     count, kv_width = keys.shape
     width = queries.shape[1]
     half = count // 2
+    padded = -(-half // LANES) * LANES
     blocks = count // ROWS
     place = lax.axis_index("ctx").astype(jnp.int32).reshape(1)
     in_hbm = [pltpu.with_memory_space_constraint(x, pltpu.HBM) for x in (queries, keys, values, segment_ids)]
 
     keys_2 = lax.ppermute(keys, "ctx", [(0, 2)])
-    values_2 = lax.ppermute(values, "ctx", [(0, 2)])
     mixed_shape = jax.ShapeDtypeStruct(keys.shape, jnp.bfloat16)
     mixed = pl.pallas_call(
         pack_kernel,
@@ -303,7 +384,7 @@
         cost_estimate=cost(1),
         name="pack",
     )(place, *in_hbm[1:])
-    tail_3 = lax.ppermute(mixed, "ctx", [(2, 3)])
+    two_left = lax.ppermute(mixed, "ctx", [(0, 2), (2, 3)])
 
     state_shape = jax.ShapeDtypeStruct((count, width + 2 * LANES), jnp.float32)
     state = pl.pallas_call(
@@ -325,53 +406,85 @@
         name="own",
     )(*in_hbm)
 
-    keys_2, state = lax.optimization_barrier((keys_2, state))
+    keys_2, mixed, state = lax.optimization_barrier((keys_2, mixed, state))
     keys_3 = lax.ppermute(keys_2, "ctx", [(2, 3)])
     keys_1 = lax.ppermute(keys_2, "ctx", [(2, 1)])
-    mixed, state = lax.optimization_barrier((mixed, state))
-    from_left = lax.ppermute(mixed, "ctx", [(0, 1), (1, 2)])
-    values_2, tail_3 = lax.optimization_barrier((values_2, tail_3))
-    values_3 = lax.ppermute(values_2, "ctx", [(2, 3)])
-
-    weights, prompt_peak = pl.pallas_call(
-        prompt_scores_kernel,
-        out_shape=(
-            jax.ShapeDtypeStruct((count * width // HEAD_DIM, count), jnp.bfloat16),
-            jax.ShapeDtypeStruct((count, LANES), jnp.float32),
-        ),
-        in_specs=[SMEM] + [VMEM] * 4,
-        out_specs=(VMEM,) * 2,
-        compiler_params=params(8),
-        cost_estimate=cost(1),
-        name="prompt_scores",
-    )(place, queries, keys_1, keys_2, keys_3)
-
+    values_1 = lax.ppermute(mixed, "ctx", [(0, 1)])
+    tail_2 = lax.ppermute(mixed, "ctx", [(1, 2)])
+    values_3 = lax.ppermute(two_left, "ctx", [(2, 3)])
+
+    tail_scratch = [pltpu.VMEM((padded, kv_width), jnp.bfloat16), pltpu.VMEM((padded, 2 * kv_width), jnp.bfloat16)]
     state = pl.pallas_call(
         tail_kernel,
         out_shape=state_shape,
-        in_specs=[SMEM] + [VMEM] * 5,
+        in_specs=[SMEM] + [VMEM] * 4,
         out_specs=VMEM,
-        scratch_shapes=[pltpu.VMEM(mixed.shape, jnp.bfloat16), pltpu.VMEM((half, 2 * kv_width), jnp.bfloat16)],
+        scratch_shapes=tail_scratch,
+        input_output_aliases={4: 0},
+        compiler_params=params(8),
+        cost_estimate=cost(1),
+        name="tail",
+    )(place, queries, two_left, segment_ids, state)
+
+    stats = jax.ShapeDtypeStruct((count, LANES), jnp.float32)
+    weights_shape = jax.ShapeDtypeStruct((count * width // HEAD_DIM, count), jnp.bfloat16)
+
+    def scores(here, key_block):
+        return pl.pallas_call(
+            functools.partial(scores_kernel, here),
+            out_shape=(weights_shape, stats),
+            in_specs=[SMEM] + [VMEM] * 2,
+            out_specs=(VMEM,) * 2,
+            compiler_params=params(8),
+            cost_estimate=cost(8 * count * count * width),
+            name=f"scores_{here}",
+        )(place, queries, key_block)
+
+    out_shape = jax.ShapeDtypeStruct(queries.shape, jnp.bfloat16)
+    reached = -(-half // ROWS) * ROWS
+    aux_shape = jax.ShapeDtypeStruct((reached, 3 * width), jnp.float32)
+    out_scratch = [
+        pltpu.VMEM((count, 2 * kv_width), jnp.bfloat16),
+        pltpu.VMEM(queries.shape, jnp.bfloat16),
+        pltpu.SemaphoreType.DMA((blocks, kv_width // HEAD_DIM)),
+    ]
+    weights, prompt_peak = scores(2, keys_2)
+    out, aux = pl.pallas_call(
+        prompt_first_kernel,
+        out_shape=(out_shape, aux_shape),
+        in_specs=[SMEM] + [VMEM] * 4,
+        out_specs=(HBM, VMEM),
+        scratch_shapes=out_scratch,
+        compiler_params=params(8),
+        cost_estimate=cost(1),
+        name="prompt_2",
+    )(place, weights, two_left, state, prompt_peak)
+    for here, key_block, value_block in ((3, keys_3, values_3), (1, keys_1, values_1)):
+        weights, prompt_peak = scores(here, key_block)
+        out = pl.pallas_call(
+            functools.partial(prompt_kernel, here),
+            out_shape=out_shape,
+            in_specs=[SMEM] + [VMEM] * 4 + [HBM],
+            out_specs=HBM,
+            scratch_shapes=out_scratch,
+            input_output_aliases={5: 0},
+            compiler_params=params(8),
+            cost_estimate=cost(1),
+            name=f"prompt_{here}",
+        )(place, weights, value_block, state, prompt_peak, out)
+
+    return pl.pallas_call(
+        last_kernel,
+        out_shape=out_shape,
+        in_specs=[SMEM] + [VMEM] * 4 + [HBM],
+        out_specs=HBM,
+        scratch_shapes=tail_scratch
+        + [pltpu.VMEM((reached, width), jnp.bfloat16), pltpu.SemaphoreType.DMA((blocks + 1, kv_width // HEAD_DIM))],
         input_output_aliases={5: 0},
         compiler_params=params(8),
         cost_estimate=cost(1),
-        name="tail",
-    )(place, queries, from_left, tail_3, segment_ids, state)
-
-    return pl.pallas_call(
-        final_kernel,
-        out_shape=jax.ShapeDtypeStruct(queries.shape, jnp.bfloat16),
-        in_specs=[SMEM] + [VMEM] * 6,
-        out_specs=pl.BlockSpec(memory_space=pl.ANY),
-        scratch_shapes=[
-            pltpu.VMEM((count, 2 * kv_width), jnp.bfloat16),
-            pltpu.VMEM(queries.shape, jnp.bfloat16),
-            pltpu.SemaphoreType.DMA((kv_width // HEAD_DIM, blocks)),
-        ],
-        compiler_params=params(8),
-        cost_estimate=cost(1),
-        name="final",
-    )(place, weights, from_left, values_2, values_3, state, prompt_peak)
+        name="last",
+    )(place, queries, tail_2, segment_ids, aux, out)
 
 
 def attend_block(

time: 29.6 us -> 25.4 us (0.86)
  waiting for transfers between devices: 3.56 us -> 0.61 us
  Pallas kernels: 15.3 us -> 14 us
    pallas_call x1, Pallas kernels: 4.12 us -> 0.01 us  [prompt_block_path(): pl.pallas_call(tail_kernel, out_shape=state_shape, in_specs=[SMEM] + [VME...]
    pallas_call x2 -> x7, Pallas kernels: 5.29 us -> 8.16 us  [the longest x1 3.38 us: prompt_block_path(): pl.pallas_call(prompt_first_kernel, out_shape=(out_shape, aux_shape), in_...]
    ppermute x4, waiting for transfers between devices: 2.06 us -> 0.01 us  [the longest x1 0.01 us: prompt_block_path(): values_1 = lax.ppermute(mixed, 'ctx', [(0, 1)])]
    ppermute x1, waiting for transfers between devices: 1.11 us -> 0.01 us  [prompt_block_path(): keys_1 = lax.ppermute(keys_2, 'ctx', [(2, 1)])]
    ppermute x1, waiting for transfers between devices: 0.01 us -> 0.59 us  [prompt_block_path(): keys_2 = lax.ppermute(keys, 'ctx', [(0, 2)])]
    ppermute x1, waiting for transfers between devices: 0.39 us -> 0.01 us  [prompt_block_path(): keys_3 = lax.ppermute(keys_2, 'ctx', [(2, 3)])]
  transfers between devices with their start and end apart: 7 -> 7, of which waited for: 3 -> 1; matrix products, arithmetic and copies ran while one was open for 0% -> 0% of each run, Pallas kernels for 41% -> 46%
where the time goes in v3:
time: 25.4 us; the launch traced here: 25.2 us
  Pallas kernels  14 us (55%)
  starting transfers between devices  10.1 us (40%)
  waiting for transfers between devices  0.61 us (2%)
  between operations  0.37 us (1%)
    pallas_call x1, Pallas kernels, prompt_block_path(): pl.pallas_call(own_kernel, out_shape=state_shape, in_specs=[HBM] * 4, out...  4.77 us
    pallas_call x1, Pallas kernels, prompt_block_path(): pl.pallas_call(prompt_first_kernel, out_shape=(out_shape, aux_shape), in_...  3.38 us
    ppermute x1, starting transfers between devices, prompt_block_path(): two_left = lax.ppermute(mixed, 'ctx', [(0, 2), (2, 3)])  3 us
    pallas_call x1, Pallas kernels, prompt_block_path(): pl.pallas_call(last_kernel, out_shape=out_shape, in_specs=[SMEM] + [VMEM]...  2.4 us
    pallas_call x3, Pallas kernels, scores(): pl.pallas_call(functools.partial(scores_kernel, here), out_shape=(weights...  2.24 us
    ppermute x1, starting transfers between devices, prompt_block_path(): keys_1 = lax.ppermute(keys_2, 'ctx', [(2, 1)])  1.3 us
    ppermute x1, starting transfers between devices, prompt_block_path(): values_3 = lax.ppermute(two_left, 'ctx', [(2, 3)])  1.3 us
    ppermute x1, starting transfers between devices, prompt_block_path(): tail_2 = lax.ppermute(mixed, 'ctx', [(1, 2)])  1.29 us
  transfers between devices with their start and end apart: 7, of which 1 were waited for; matrix products, arithmetic and copies ran while one was open for 0% of the time, Pallas kernels for 46%

profile of v3, /device:TPU:22, one launch (start us, length us, event | category | flops | bytes accessed | tf_op | source)
XLA Modules:
  0.0 25.2 jit_solution(13475533607894198498)
XLA Ops:
  0.0 1.3 %collective-permute-start = (bf16[384,256]{1,0:T(8,128)(2,1)}, bf16[384,256]{1,0:T(8,128)(2,1)S(1)}, u32[]{:S(2)}, u32[]{:S(2)}) collective-permute-start(bf16[384,256]{1,0:T(8,128)(2,1)} %k_hbm.3), channel_id=1, source_target_pairs={{0,8},{1,9},{2,10},{3,11},{16,24},{17,25},{18,26},{19,27}} | collective-permute-start | bytes 589832 | tf_op jit(solution)/shard_map/ppermute | solution.py:375
  1.3 1.1 %pack.1 = bf16[384,256]{1,0:T(8,128)(2,1)S(1)} custom-call(s32[1]{0:T(128)} %bitcast.place_ref, bf16[384,256]{1,0:T(8,128)(2,1)} %k_hbm.3, bf16[384,256]{1,0:T(8,128)(2,1)} %v_hbm.3, s32[384]{0:T(512)} %seg_ref.3), custom_call_target="tpu_custom_call" | custom-call | flops 1 | bytes 1 | tf_op jit(solution)/shard_map/pack/pallas_call | solution.py:377
  2.4 0.0 copy-start
  2.4 0.0 copy-start.1
  2.4 3.0 %collective-permute-start.2 = (bf16[384,256]{1,0:T(8,128)(2,1)S(1)}, bf16[384,256]{1,0:T(8,128)(2,1)S(1)}, u32[]{:S(2)}, u32[]{:S(2)}) collective-permute-start(bf16[384,256]{1,0:T(8,128)(2,1)S(1)} %pack.1), channel_id=1, source_target_pairs={{0,8},{8,12},{1,9},{9,13},{2,10},{10,14},{3,11},{11,15},{16,24},{2... | collective-permute-start | bytes 589832 | tf_op jit(solution)/shard_map/ppermute | solution.py:387
  5.4 4.8 %own.1.state_in = f32[384,2304]{1,0:T(8,128)S(1)} custom-call(bf16[384,2048]{1,0:T(8,128)(2,1)} %q_ref.9, bf16[384,256]{1,0:T(8,128)(2,1)} %k_hbm.3, bf16[384,256]{1,0:T(8,128)(2,1)} %v_hbm.3, s32[384]{0:T(512)} %seg_ref.3), custom_call_target="tpu_custom_call" | custom-call | flops 4831838208 | bytes 1 | tf_op jit(solution)/shard_map/own/pallas_call | solution.py:390
  10.2 0.6 %collective-permute-done.k_ref = bf16[384,256]{1,0:T(8,128)(2,1)S(1)} collective-permute-done((bf16[384,256]{1,0:T(8,128)(2,1)}, bf16[384,256]{1,0:T(8,128)(2,1)S(1)}, u32[]{:S(2)}, u32[]{:S(2)}) %collective-permute-start) | collective-permute-done | bytes 196640 | tf_op jit(solution)/shard_map/ppermute | solution.py:375
  10.8 1.3 %collective-permute-start.5 = (bf16[384,256]{1,0:T(8,128)(2,1)S(1)}, bf16[384,256]{1,0:T(8,128)(2,1)S(1)}, u32[]{:S(2)}, u32[]{:S(2)}) collective-permute-start(bf16[384,256]{1,0:T(8,128)(2,1)S(1)} %collective-permute-done.k_ref), channel_id=1, source_target_pairs={{8,12},{9,13},{10,14},{11,15},{24,28},{25,29},{26,30},{27,31}} | collective-permute-start | bytes 589832 | tf_op jit(solution)/shard_map/ppermute | solution.py:410
  12.1 1.3 %collective-permute-start.3 = (bf16[384,256]{1,0:T(8,128)(2,1)S(1)}, bf16[384,256]{1,0:T(8,128)(2,1)S(1)}, u32[]{:S(2)}, u32[]{:S(2)}) collective-permute-start(bf16[384,256]{1,0:T(8,128)(2,1)S(1)} %collective-permute-done.k_ref), channel_id=1, source_target_pairs={{8,4},{9,5},{10,6},{11,7},{24,20},{25,21},{26,22},{27,23}} | collective-permute-start | bytes 589832 | tf_op jit(solution)/shard_map/ppermute | solution.py:411
  13.4 0.7 %collective-permute-start.4 = (bf16[384,256]{1,0:T(8,128)(2,1)S(1)}, bf16[384,256]{1,0:T(8,128)(2,1)S(1)}, u32[]{:S(2)}, u32[]{:S(2)}) collective-permute-start(bf16[384,256]{1,0:T(8,128)(2,1)S(1)} %pack.1), channel_id=1, source_target_pairs={{0,4},{1,5},{2,6},{3,7},{16,20},{17,21},{18,22},{19,23}} | collective-permute-start | bytes 589832 | tf_op jit(solution)/shard_map/ppermute | solution.py:412
  14.1 1.3 %collective-permute-start.1 = (bf16[384,256]{1,0:T(8,128)(2,1)S(1)}, bf16[384,256]{1,0:T(8,128)(2,1)S(1)}, u32[]{:S(2)}, u32[]{:S(2)}) collective-permute-start(bf16[384,256]{1,0:T(8,128)(2,1)S(1)} %pack.1), channel_id=1, source_target_pairs={{4,8},{5,9},{6,10},{7,11},{20,24},{21,25},{22,26},{23,27}} | collective-permute-start | bytes 589832 | tf_op jit(solution)/shard_map/ppermute | solution.py:413
  15.4 0.0 collective-permute-done.2.t_ref.v_ref
  15.4 1.3 %collective-permute-start.6 = (bf16[384,256]{1,0:T(8,128)(2,1)S(1)}, bf16[384,256]{1,0:T(8,128)(2,1)S(1)}, u32[]{:S(2)}, u32[]{:S(2)}) collective-permute-start(bf16[384,256]{1,0:T(8,128)(2,1)S(1)} %collective-permute-done.2.t_ref.v_ref), channel_id=1, source_target_pairs={{8,12},{9,13},{10,14},{11,15},{24,28},{25,29},{26,30},{27,31}} | collective-permute-start | bytes 589832 | tf_op jit(solution)/shard_map/ppermute | solution.py:414
  16.7 2.0 %scores_2.1 = (bf16[6144,384]{1,0:T(8,128)(2,1)S(1)}, f32[384,128]{1,0:T(8,128)S(1)}) custom-call(s32[1]{0:T(128)} %bitcast.place_ref, bf16[384,2048]{1,0:T(8,128)(2,1)S(1)} %copy-done, bf16[384,256]{1,0:T(8,128)(2,1)S(1)} %collective-permute-done.k_ref), custom_call_target="tpu_custom_call" | custom-call | flops 2415919104 | bytes 1 | tf_op jit(solution)/shard_map/scores_2/pallas_call | solution.py:433
  18.8 3.4 %prompt_2.1 = (bf16[384,2048]{1,0:T(8,128)(2,1)}, f32[256,6144]{1,0:T(8,128)S(1)}) custom-call(s32[1]{0:T(128)} %bitcast.place_ref, bf16[6144,384]{1,0:T(8,128)(2,1)S(1)} %get-tuple-element.18.w_ref, bf16[384,256]{1,0:T(8,128)(2,1)S(1)} %collective-permute-done.2.t_ref.v_ref, f32[384,2304]{1,0:T(8,128)S(1)} %tail.1.state, ...), custom_call_target="tpu_custom_call" | custom-call | flops 1 | bytes 1 | tf_op jit(solution)/shard_map/prompt_2/pallas_call | solution.py:452
  22.2 0.0 collective-permute-done.5.k_ref
  22.2 0.2 scores_3.1
  22.4 0.0 collective-permute-done.6.v_ref
  22.4 0.1 prompt_3.1.rest_0_
  22.5 0.0 collective-permute-done.3.k_ref
  22.5 0.0 collective-permute-done.4.v_ref
  22.5 0.1 prompt_1.1.out_in
  22.6 0.0 collective-permute-done.1.t_ref
  22.6 2.4 %last.1 = bf16[384,2048]{1,0:T(8,128)(2,1)} custom-call(s32[1]{0:T(128)} %bitcast.place_ref, bf16[384,2048]{1,0:T(8,128)(2,1)S(1)} %copy-done, bf16[384,256]{1,0:T(8,128)(2,1)S(1)} %collective-permute-done.1.t_ref, s32[384]{0:T(512)S(1)} %copy-done.1, f32[256,6144]{1,0:T(8,128)S(1)} %get-tuple-element.21.aux, ...), custom_call_target="tpu_custom_call", output_to_operand_aliasing={{}: (5, {})} | custom-call | flops 1 | bytes 1 | tf_op jit(solution)/shard_map/last/pallas_call | solution.py:476
  (4 shorter events, 0.0 us)
Async XLA Ops:
  0.0 10.8 %collective-permute-start = (bf16[384,256]{1,0:T(8,128)(2,1)}, bf16[384,256]{1,0:T(8,128)(2,1)S(1)}, u32[]{:S(2)}, u32[]{:S(2)}) collective-permute-start(bf16[384,256]{1,0:T(8,128)(2,1)} %k_hbm.3), channel_id=1, source_target_pairs={{0,8},{1,9},{2,10},{3,11},{16,24},{17,25},{18,26},{19,27}} | collective-permute-start | bytes 589832 | tf_op jit(solution)/shard_map/ppermute | solution.py:375
  2.4 14.3 %copy-start = (bf16[384,2048]{1,0:T(8,128)(2,1)S(1)}, bf16[384,2048]{1,0:T(8,128)(2,1)}, u32[]{:S(2)}) copy-start(bf16[384,2048]{1,0:T(8,128)(2,1)} %q_ref.9) | copy-start | bytes 4718596
  2.4 14.3 %copy-start.1 = (s32[384]{0:T(512)S(1)}, s32[384]{0:T(512)}, u32[]{:S(2)}) copy-start(s32[384]{0:T(512)} %seg_ref.3) | copy-start | bytes 4612
  2.4 13.0 %collective-permute-start.2 = (bf16[384,256]{1,0:T(8,128)(2,1)S(1)}, bf16[384,256]{1,0:T(8,128)(2,1)S(1)}, u32[]{:S(2)}, u32[]{:S(2)}) collective-permute-start(bf16[384,256]{1,0:T(8,128)(2,1)S(1)} %pack.1), channel_id=1, source_target_pairs={{0,8},{8,12},{1,9},{9,13},{2,10},{10,14},{3,11},{11,15},{16,24},{2... | collective-permute-start | bytes 589832 | tf_op jit(solution)/shard_map/ppermute | solution.py:387
  10.8 11.4 %collective-permute-start.5 = (bf16[384,256]{1,0:T(8,128)(2,1)S(1)}, bf16[384,256]{1,0:T(8,128)(2,1)S(1)}, u32[]{:S(2)}, u32[]{:S(2)}) collective-permute-start(bf16[384,256]{1,0:T(8,128)(2,1)S(1)} %collective-permute-done.k_ref), channel_id=1, source_target_pairs={{8,12},{9,13},{10,14},{11,15},{24,28},{25,29},{26,30},{27,31}} | collective-permute-start | bytes 589832 | tf_op jit(solution)/shard_map/ppermute | solution.py:410
  12.1 10.4 %collective-permute-start.3 = (bf16[384,256]{1,0:T(8,128)(2,1)S(1)}, bf16[384,256]{1,0:T(8,128)(2,1)S(1)}, u32[]{:S(2)}, u32[]{:S(2)}) collective-permute-start(bf16[384,256]{1,0:T(8,128)(2,1)S(1)} %collective-permute-done.k_ref), channel_id=1, source_target_pairs={{8,4},{9,5},{10,6},{11,7},{24,20},{25,21},{26,22},{27,23}} | collective-permute-start | bytes 589832 | tf_op jit(solution)/shard_map/ppermute | solution.py:411
  13.4 9.1 %collective-permute-start.4 = (bf16[384,256]{1,0:T(8,128)(2,1)S(1)}, bf16[384,256]{1,0:T(8,128)(2,1)S(1)}, u32[]{:S(2)}, u32[]{:S(2)}) collective-permute-start(bf16[384,256]{1,0:T(8,128)(2,1)S(1)} %pack.1), channel_id=1, source_target_pairs={{0,4},{1,5},{2,6},{3,7},{16,20},{17,21},{18,22},{19,23}} | collective-permute-start | bytes 589832 | tf_op jit(solution)/shard_map/ppermute | solution.py:412
  14.1 8.5 %collective-permute-start.1 = (bf16[384,256]{1,0:T(8,128)(2,1)S(1)}, bf16[384,256]{1,0:T(8,128)(2,1)S(1)}, u32[]{:S(2)}, u32[]{:S(2)}) collective-permute-start(bf16[384,256]{1,0:T(8,128)(2,1)S(1)} %pack.1), channel_id=1, source_target_pairs={{4,8},{5,9},{6,10},{7,11},{20,24},{21,25},{22,26},{23,27}} | collective-permute-start | bytes 589832 | tf_op jit(solution)/shard_map/ppermute | solution.py:413
  15.4 7.0 %collective-permute-start.6 = (bf16[384,256]{1,0:T(8,128)(2,1)S(1)}, bf16[384,256]{1,0:T(8,128)(2,1)S(1)}, u32[]{:S(2)}, u32[]{:S(2)}) collective-permute-start(bf16[384,256]{1,0:T(8,128)(2,1)S(1)} %collective-permute-done.2.t_ref.v_ref), channel_id=1, source_target_pairs={{8,12},{9,13},{10,14},{11,15},{24,28},{25,29},{26,30},{27,31}} | collective-permute-start | bytes 589832 | tf_op jit(solution)/shard_map/ppermute | solution.py:414

commit v4 on v3

--- a/solution.py
+++ b/solution.py
@@ -62,43 +62,42 @@
     return copy
 
 
-def pack_kernel(place_ref, k_hbm, v_hbm, seg_hbm, mixed_ref, seg_ref, sem):
+def pack_kernel(place_ref, q_hbm, k_hbm, v_hbm, seg_hbm, mixed_ref, state, seg_ref, sem, *own_scratch):
     count = k_hbm.shape[0]
     half = count // 2
     place = place_ref[0]
     low, high = pl.ds(0, half), pl.ds(half, half)
-    get_seg = fetch(seg_hbm, seg_ref, sem.at[2])
 
     @pl.when(place == 0)
     def _():
-        fetch(v_hbm.at[low], mixed_ref.at[low], sem.at[0])
-
-    @pl.when(place > 0)
-    def _():
-        fetch(k_hbm.at[high], mixed_ref.at[low], sem.at[0])
-
-    other = fetch(v_hbm.at[high], mixed_ref.at[high], sem.at[1])
-    get_seg.wait()
-    seg = seg_ref[...].reshape(1, count).astype(jnp.float32)[:, half:]
-    pltpu.make_async_copy(k_hbm.at[high], mixed_ref.at[low], sem.at[0]).wait()
-
-    @pl.when(place > 0)
-    def _():
-        first = lax.broadcasted_iota(jnp.int32, (16, half), 0) == 0
+        every = fetch(v_hbm, mixed_ref, sem.at[0])
+        get_seg = fetch(seg_hbm, seg_ref, sem.at[2])
+        attend_own(0, 1, get_seg, q_hbm, k_hbm, v_hbm, state, seg_ref, *own_scratch)
+        every.wait()
+
+    @pl.when((place > 0) & (place < 3))
+    def _():
+        get_seg = fetch(seg_hbm, seg_ref, sem.at[2])
+        first = fetch(k_hbm.at[high], mixed_ref.at[low], sem.at[0])
+        other = fetch(v_hbm.at[high], mixed_ref.at[high], sem.at[1])
+        get_seg.wait()
+        seg = seg_ref[...].reshape(1, count).astype(jnp.float32)[:, half:]
+        first.wait()
+        top = lax.broadcasted_iota(jnp.int32, (16, half), 0) == 0
         old = mixed_ref[0:16, 0:half].astype(jnp.float32)
-        mixed_ref[0:16, 0:half] = jnp.where(first, jnp.broadcast_to(seg, (16, half)), old).astype(jnp.bfloat16)
-
-    other.wait()
-
-
-def own_kernel(q_hbm, k_hbm, v_hbm, seg_hbm, state, q_ref, k_ref, v_ref, seg_ref, bias, wide, in_sem):
+        mixed_ref[0:16, 0:half] = jnp.where(top, jnp.broadcast_to(seg, (16, half)), old).astype(jnp.bfloat16)
+        other.wait()
+
+
+def attend_own(
+    first_head, heads, get_seg, q_hbm, k_hbm, v_hbm, state, seg_ref, q_ref, k_ref, v_ref, bias, wide, in_sem
+):
     count, width = q_ref.shape
-    heads = k_ref.shape[1] // HEAD_DIM
     blocks = count // ROWS
     span = [slice(b * ROWS, (b + 1) * ROWS) for b in range(blocks)]
-    get_seg = fetch(seg_hbm, seg_ref, in_sem.at[blocks + 2])
+    here = slice(first_head * GROUP * HEAD_DIM, (first_head + heads) * GROUP * HEAD_DIM)
     get_k = fetch(k_hbm, k_ref, in_sem.at[blocks])
-    get_q = [fetch(q_hbm.at[rows], q_ref.at[rows], in_sem.at[b]) for b, rows in enumerate(span)]
+    get_q = [fetch(q_hbm.at[rows, here], q_ref.at[rows, here], in_sem.at[b]) for b, rows in enumerate(span)]
     get_v = fetch(v_hbm, v_ref, in_sem.at[blocks + 1])
     get_seg.wait()
     seg = seg_ref[...].reshape(1, count).astype(jnp.float32)
@@ -112,17 +111,21 @@
                 j = lax.broadcasted_iota(jnp.int32, (ROWS, ROWS), 1)
                 seen = seen & (j <= i)
             bias[span[b], span[t]] = jnp.where(seen, 0.0, NEG)
-    fill_ones(wide, heads)
+    fill_ones(wide, k_ref.shape[1] // HEAD_DIM)
     get_k.wait()
     get_v.wait()
-    with_ones(wide, v_ref, count, heads)
+    with_ones(wide, v_ref, count, k_ref.shape[1] // HEAD_DIM)
     lane = lax.broadcasted_iota(jnp.int32, (ROWS, LANES), 1)
     for b in range(blocks):
         rows, keys = span[b], (b + 1) * ROWS
         get_q[b].wait()
-        peaks = jnp.zeros((ROWS, LANES), jnp.float32)
-        totals = jnp.ones((ROWS, LANES), jnp.float32)
-        for h in range(heads):
+        if first_head == 0:
+            peaks = jnp.zeros((ROWS, LANES), jnp.float32)
+            totals = jnp.ones((ROWS, LANES), jnp.float32)
+        else:
+            peaks = state[rows, width : width + LANES]
+            totals = state[rows, width + LANES : width + 2 * LANES]
+        for h in range(first_head, first_head + heads):
             cols = head_cols(h)
             scores = dot_t(stack(q_ref, rows, cols), k_ref[0:keys, h * HEAD_DIM : (h + 1) * HEAD_DIM])
             scores = scores.reshape(GROUP, ROWS, keys) + bias[rows, 0:keys][None]
@@ -133,20 +136,42 @@
             )
             unstack(state, rows, cols, sums[:, :HEAD_DIM] / sums[:, HEAD_DIM:])
             for g in range(GROUP):
-                here = lane == h * GROUP + g
-                peaks = jnp.where(here, peak[g], peaks)
-                totals = jnp.where(here, sums[g * ROWS : (g + 1) * ROWS, HEAD_DIM:], totals)
+                mine = lane == h * GROUP + g
+                peaks = jnp.where(mine, peak[g], peaks)
+                totals = jnp.where(mine, sums[g * ROWS : (g + 1) * ROWS, HEAD_DIM:], totals)
         state[rows, width : width + LANES] = peaks
         state[rows, width + LANES : width + 2 * LANES] = totals
 
 
-def scores_kernel(here, place_ref, q_ref, k_ref, w_ref, peak_ref):
+def own_kernel(place_ref, q_hbm, k_hbm, v_hbm, seg_hbm, state_in, state, seg_ref, *scratch):
+    heads = k_hbm.shape[1] // HEAD_DIM
+    get_seg = fetch(seg_hbm, seg_ref, scratch[-1].at[k_hbm.shape[0] // ROWS + 2])
+
+    @pl.when(place_ref[0] > 0)
+    def _():
+        attend_own(0, heads, get_seg, q_hbm, k_hbm, v_hbm, state, seg_ref, *scratch)
+
+    @pl.when(place_ref[0] == 0)
+    def _():
+        attend_own(1, heads - 1, get_seg, q_hbm, k_hbm, v_hbm, state, seg_ref, *scratch)
+
+
+def scores_kernel(places, place_ref, q_ref, *refs):
+    *k_refs, w_ref, peak_ref, k_ref = refs
     count = q_ref.shape[0]
     heads = k_ref.shape[1] // HEAD_DIM
-
-    @pl.when(place_ref[0] == here)
-    def _():
-        lane = lax.broadcasted_iota(jnp.int32, (ROWS, LANES), 1)
+    lane = lax.broadcasted_iota(jnp.int32, (ROWS, LANES), 1)
+
+    place = place_ref[0]
+
+    for here, ref in zip(places, k_refs):
+
+        @pl.when(place == here)
+        def _(ref=ref):
+            k_ref[...] = ref[...]
+
+    @pl.when(functools.reduce(jnp.logical_or, [place == here for here in places]))
+    def _():
         for b in range(count // ROWS):
             rows = slice(b * ROWS, (b + 1) * ROWS)
             peaks = jnp.zeros((ROWS, LANES), jnp.float32)
@@ -235,17 +260,10 @@
         merge_tail(q_ref, t_ref, seg_ref, peaks_of, tail, wide, finish)
 
 
-def put_out(staged, out_ref, sem, rows, h, waits):
-    box = (pl.ds(rows.start, rows.stop - rows.start), pl.ds(h * GROUP * HEAD_DIM, GROUP * HEAD_DIM))
-    waits.append(fetch(staged.at[box], out_ref.at[box], sem.at[rows.start // ROWS, h]))
-
-
-def prompt_blocks(w_ref, v_ref, state, ppeak_ref, wide, finish):
-    count = v_ref.shape[0]
-    heads = v_ref.shape[1] // HEAD_DIM
+def prompt_rows(w_ref, state, ppeak_ref, wide, finish):
+    count = wide.shape[0]
+    heads = wide.shape[1] // 2 // HEAD_DIM
     width = heads * GROUP * HEAD_DIM
-    fill_ones(wide, heads)
-    with_ones(wide, v_ref, count, heads)
     for b in range(count // ROWS):
         rows = slice(b * ROWS, (b + 1) * ROWS)
         own, prompt = state[rows, width : width + LANES], ppeak_ref[rows, :]
@@ -254,105 +272,126 @@
         own_total = state[rows, width + LANES : width + 2 * LANES] * jnp.exp2((own - peak) * EXP2_SCALE)
         for h in range(heads):
             first = (h * (count // ROWS) + b) * GROUP * ROWS
-            sums = jnp.dot(
-                w_ref[first : first + GROUP * ROWS, :],
-                wide[:, 2 * h * HEAD_DIM : (2 * h + 2) * HEAD_DIM],
-                preferred_element_type=jnp.float32,
-            )
-            for g, c in enumerate(head_cols(h)):
-                index = h * GROUP + g
-                mine = slice(g * ROWS, (g + 1) * ROWS)
-                own_part, prompt_part = column(own_total, index), column(prompt_scale, index)
-                total = own_part + sums[mine, HEAD_DIM:] * prompt_part
-                value = (state[rows, c] * own_part + sums[mine, :HEAD_DIM] * prompt_part) / total
-                finish(rows, h, g, c, value, peak, total)
-
-
-def prompt_kernel(here, place_ref, w_ref, v_ref, state, ppeak_ref, *rest):
-    out_ref, wide, staged, sem = rest[-4:]
-    count, width = staged.shape
+            pieces = 2 if (b, h) == (count // ROWS - 1, heads - 1) else 1
+            size = GROUP // pieces
+            for p in range(pieces):
+                low = first + p * size * ROWS
+                sums = jnp.dot(
+                    w_ref[low : low + size * ROWS, :],
+                    wide[:, 2 * h * HEAD_DIM : (2 * h + 2) * HEAD_DIM],
+                    preferred_element_type=jnp.float32,
+                )
+                cols = head_cols(h)[p * size : (p + 1) * size]
+                for g, c in enumerate(cols):
+                    index = h * GROUP + p * size + g
+                    mine = slice(g * ROWS, (g + 1) * ROWS)
+                    own_part, prompt_part = column(own_total, index), column(prompt_scale, index)
+                    total = own_part + sums[mine, HEAD_DIM:] * prompt_part
+                    value = (state[rows, c] * own_part + sums[mine, :HEAD_DIM] * prompt_part) / total
+                    finish(rows, c, value, index, peak, total)
+                finish(rows, slice(cols[0].start, cols[-1].stop), None, None, None, None)
+
+
+def middle_kernel(place_ref, w_ref, v_ref, state, ppeak_ref, out_ref, aux, wide, staged, sem):
+    width = staged.shape[1]
     heads = width // HEAD_DIM // GROUP
 
-    if here == 1:
-
-        @pl.when(place_ref[0] == 0)
-        def _():
-            waits = []
-            for b in range(count // ROWS):
-                rows = slice(b * ROWS, (b + 1) * ROWS)
-                for h in range(heads):
-                    for c in head_cols(h):
-                        staged[rows, c] = state[rows, c].astype(jnp.bfloat16)
-                    put_out(staged, out_ref, sem, rows, h, waits)
-            for wait in waits:
-                wait.wait()
-
-    @pl.when(place_ref[0] == here)
+    @pl.when(place_ref[0] == 2)
     def _():
         waits = []
 
-        def finish(rows, h, g, c, value, peak, total):
-            staged[rows, c] = value.astype(jnp.bfloat16)
-            if g == GROUP - 1:
-                put_out(staged, out_ref, sem, rows, h, waits)
-
-        prompt_blocks(w_ref, v_ref, state, ppeak_ref, wide, finish)
+        def finish(rows, cols, value, index, peak, total):
+            goes_on = rows.stop <= aux.shape[0]
+            if value is None:
+                if not goes_on:
+                    put_out(staged, out_ref, sem, rows, cols, waits)
+            elif goes_on:
+                aux[rows, cols] = value
+                aux[rows, shifted([cols], width)[0]] = column(peak, index)
+                aux[rows, shifted([cols], 2 * width)[0]] = total
+            else:
+                staged[rows, cols] = value.astype(jnp.bfloat16)
+
+        fill_ones(wide, heads)
+        with_ones(wide, v_ref, staged.shape[0], heads)
+        prompt_rows(w_ref, state, ppeak_ref, wide, finish)
         for wait in waits:
             wait.wait()
 
 
-def prompt_first_kernel(place_ref, w_ref, v_ref, state, ppeak_ref, out_ref, aux, wide, staged, sem):
-    width = staged.shape[1]
-
-    @pl.when(place_ref[0] == 2)
-    def _():
-        waits = []
-
-        def finish(rows, h, g, c, value, peak, total):
-            if rows.stop <= aux.shape[0]:
-                peak_cols, sum_cols = shifted([c], width)[0], shifted([c], 2 * width)[0]
-                aux[rows, c] = value
-                aux[rows, peak_cols] = column(peak, h * GROUP + g)
-                aux[rows, sum_cols] = total
-            else:
-                staged[rows, c] = value.astype(jnp.bfloat16)
-                if g == GROUP - 1:
-                    put_out(staged, out_ref, sem, rows, h, waits)
-
-        prompt_blocks(w_ref, v_ref, state, ppeak_ref, wide, finish)
-        for wait in waits:
-            wait.wait()
-
-
-def last_kernel(place_ref, q_ref, t_ref, seg_ref, aux, out_in, out_ref, tail, wide, staged, sem):
+def put_out(staged, out_ref, sem, rows, cols, waits):
+    box = (pl.ds(rows.start, rows.stop - rows.start), pl.ds(cols.start, cols.stop - cols.start))
+    waits.append(fetch(staged.at[box], out_ref.at[box], sem.at[len(waits)]))
+
+
+def last_kernel(
+    place_ref, q_ref, w_ref, one_ref, v3_ref, seg_ref, state, ppeak_ref, aux, out_in, out_ref, wide, tail, tail_wide, staged, sem
+):
     count, width = q_ref.shape
     heads = width // HEAD_DIM // GROUP
     half = count // 2
-
-    @pl.when(place_ref[0] == 2)
-    def _():
+    place = place_ref[0]
+
+    def run(body):
         waits = []
 
-        def peaks_of(rows, h):
-            return stack(aux, rows, shifted(head_cols(h), width))
-
-        def finish(rows, h, cols, peak, scale, sums):
-            size = rows.stop - rows.start
-            for g, c in enumerate(cols):
-                mine = slice(g * size, (g + 1) * size)
-                total = aux[rows, shifted([c], 2 * width)[0]] * scale[mine]
-                value = (aux[rows, c] * total + sums[mine, :HEAD_DIM]) / (total + sums[mine, HEAD_DIM:])
-                staged[rows, c] = value.astype(jnp.bfloat16)
-            put_out(staged, out_ref, sem, rows, h, waits)
-
-        if aux.shape[0] > half:
-            rest = slice(half, aux.shape[0])
-            staged[rest, :] = aux[rest, 0:width].astype(jnp.bfloat16)
-            box = (pl.ds(half, aux.shape[0] - half), pl.ds(0, width))
-            waits.append(fetch(staged.at[box], out_ref.at[box], sem.at[count // ROWS, 0]))
-        merge_tail(q_ref, t_ref, seg_ref, peaks_of, tail, wide, finish)
+        def put(rows, cols):
+            put_out(staged, out_ref, sem, rows, cols, waits)
+
+        body(put)
         for wait in waits:
             wait.wait()
+
+    @pl.when(place == 0)
+    def _():
+        def body(put):
+            for b in range(count // ROWS):
+                rows = slice(b * ROWS, (b + 1) * ROWS)
+                staged[rows, :] = state[rows, 0:width].astype(jnp.bfloat16)
+                put(rows, slice(0, width))
+
+        run(body)
+
+    for here, ref in ((1, one_ref), (3, v3_ref)):
+        pl.when(place == here)(functools.partial(with_ones, wide, ref, count, heads))
+
+    @pl.when((place == 1) | (place == 3))
+    def _():
+        fill_ones(wide, heads)
+
+        def body(put):
+            def finish(rows, cols, value, index, peak, total):
+                if value is None:
+                    put(rows, cols)
+                else:
+                    staged[rows, cols] = value.astype(jnp.bfloat16)
+
+            prompt_rows(w_ref, state, ppeak_ref, wide, finish)
+
+        run(body)
+
+    @pl.when(place == 2)
+    def _():
+        def body(put):
+            def peaks_of(rows, h):
+                return stack(aux, rows, shifted(head_cols(h), width))
+
+            def finish(rows, h, cols, peak, scale, sums):
+                size = rows.stop - rows.start
+                for g, c in enumerate(cols):
+                    mine = slice(g * size, (g + 1) * size)
+                    total = aux[rows, shifted([c], 2 * width)[0]] * scale[mine]
+                    value = (aux[rows, c] * total + sums[mine, :HEAD_DIM]) / (total + sums[mine, HEAD_DIM:])
+                    staged[rows, c] = value.astype(jnp.bfloat16)
+                put(rows, slice(cols[0].start, cols[-1].stop))
+
+            if aux.shape[0] > half:
+                rest = slice(half, aux.shape[0])
+                staged[rest, :] = aux[rest, 0:width].astype(jnp.bfloat16)
+                put(rest, slice(0, width))
+            merge_tail(q_ref, one_ref, seg_ref, peaks_of, tail, tail_wide, finish)
+
+        run(body)
 
 
 def params(mebibytes):
@@ -373,44 +412,43 @@
     in_hbm = [pltpu.with_memory_space_constraint(x, pltpu.HBM) for x in (queries, keys, values, segment_ids)]
 
     keys_2 = lax.ppermute(keys, "ctx", [(0, 2)])
-    mixed_shape = jax.ShapeDtypeStruct(keys.shape, jnp.bfloat16)
-    mixed = pl.pallas_call(
+    state_shape = jax.ShapeDtypeStruct((count, width + 2 * LANES), jnp.float32)
+    own_scratch = [
+        pltpu.VMEM(queries.shape, jnp.bfloat16),
+        pltpu.VMEM(keys.shape, jnp.bfloat16),
+        pltpu.VMEM(keys.shape, jnp.bfloat16),
+        pltpu.VMEM((count, count), jnp.float32),
+        pltpu.VMEM((count, 2 * kv_width), jnp.bfloat16),
+        pltpu.SemaphoreType.DMA((blocks + 3,)),
+    ]
+    mixed, state = pl.pallas_call(
         pack_kernel,
-        out_shape=mixed_shape,
-        in_specs=[SMEM] + [HBM] * 3,
-        out_specs=VMEM,
-        scratch_shapes=[pltpu.VMEM(segment_ids.shape, jnp.int32), pltpu.SemaphoreType.DMA((3,))],
-        compiler_params=params(2),
+        out_shape=(jax.ShapeDtypeStruct(keys.shape, jnp.bfloat16), state_shape),
+        in_specs=[SMEM] + [HBM] * 4,
+        out_specs=(VMEM,) * 2,
+        scratch_shapes=[pltpu.VMEM(segment_ids.shape, jnp.int32), pltpu.SemaphoreType.DMA((3,))] + own_scratch,
+        compiler_params=params(10),
         cost_estimate=cost(1),
         name="pack",
-    )(place, *in_hbm[1:])
+    )(place, *in_hbm)
     two_left = lax.ppermute(mixed, "ctx", [(0, 2), (2, 3)])
 
-    state_shape = jax.ShapeDtypeStruct((count, width + 2 * LANES), jnp.float32)
     state = pl.pallas_call(
         own_kernel,
         out_shape=state_shape,
-        in_specs=[HBM] * 4,
+        in_specs=[SMEM] + [HBM] * 4 + [VMEM],
         out_specs=VMEM,
-        scratch_shapes=[
-            pltpu.VMEM(queries.shape, jnp.bfloat16),
-            pltpu.VMEM(keys.shape, jnp.bfloat16),
-            pltpu.VMEM(keys.shape, jnp.bfloat16),
-            pltpu.VMEM(segment_ids.shape, jnp.int32),
-            pltpu.VMEM((count, count), jnp.float32),
-            pltpu.VMEM((count, 2 * kv_width), jnp.bfloat16),
-            pltpu.SemaphoreType.DMA((blocks + 3,)),
-        ],
+        scratch_shapes=[pltpu.VMEM(segment_ids.shape, jnp.int32)] + own_scratch,
+        input_output_aliases={5: 0},
         compiler_params=params(10),
         cost_estimate=cost(16 * count * count * width),
         name="own",
-    )(*in_hbm)
+    )(place, *in_hbm, state)
 
     keys_2, mixed, state = lax.optimization_barrier((keys_2, mixed, state))
     keys_3 = lax.ppermute(keys_2, "ctx", [(2, 3)])
     keys_1 = lax.ppermute(keys_2, "ctx", [(2, 1)])
-    values_1 = lax.ppermute(mixed, "ctx", [(0, 1)])
-    tail_2 = lax.ppermute(mixed, "ctx", [(1, 2)])
+    one_left = lax.ppermute(mixed, "ctx", [(0, 1), (1, 2)])
     values_3 = lax.ppermute(two_left, "ctx", [(2, 3)])
 
     tail_scratch = [pltpu.VMEM((padded, kv_width), jnp.bfloat16), pltpu.VMEM((padded, 2 * kv_width), jnp.bfloat16)]
@@ -426,65 +464,50 @@
         name="tail",
     )(place, queries, two_left, segment_ids, state)
 
-    stats = jax.ShapeDtypeStruct((count, LANES), jnp.float32)
-    weights_shape = jax.ShapeDtypeStruct((count * width // HEAD_DIM, count), jnp.bfloat16)
-
-    def scores(here, key_block):
+    out_shape = jax.ShapeDtypeStruct(queries.shape, jnp.bfloat16)
+    reached = -(-half // ROWS) * ROWS
+    chunks = blocks * (kv_width // HEAD_DIM) + 1
+    out_scratch = [pltpu.VMEM(queries.shape, jnp.bfloat16), pltpu.SemaphoreType.DMA((chunks,))]
+    wide_scratch = [pltpu.VMEM((count, 2 * kv_width), jnp.bfloat16)]
+
+    def scores(places, key_blocks):
         return pl.pallas_call(
-            functools.partial(scores_kernel, here),
-            out_shape=(weights_shape, stats),
-            in_specs=[SMEM] + [VMEM] * 2,
+            functools.partial(scores_kernel, places),
+            out_shape=(
+                jax.ShapeDtypeStruct((count * width // HEAD_DIM, count), jnp.bfloat16),
+                jax.ShapeDtypeStruct((count, LANES), jnp.float32),
+            ),
+            in_specs=[SMEM] + [VMEM] * (1 + len(places)),
             out_specs=(VMEM,) * 2,
+            scratch_shapes=[pltpu.VMEM(keys.shape, jnp.bfloat16)],
             compiler_params=params(8),
             cost_estimate=cost(8 * count * count * width),
-            name=f"scores_{here}",
-        )(place, queries, key_block)
-
-    out_shape = jax.ShapeDtypeStruct(queries.shape, jnp.bfloat16)
-    reached = -(-half // ROWS) * ROWS
-    aux_shape = jax.ShapeDtypeStruct((reached, 3 * width), jnp.float32)
-    out_scratch = [
-        pltpu.VMEM((count, 2 * kv_width), jnp.bfloat16),
-        pltpu.VMEM(queries.shape, jnp.bfloat16),
-        pltpu.SemaphoreType.DMA((blocks, kv_width // HEAD_DIM)),
-    ]
-    weights, prompt_peak = scores(2, keys_2)
+            name="scores_" + "".join(str(p) for p in places),
+        )(place, queries, *key_blocks)
+
+    weights, prompt_peak = scores((2,), (keys_2,))
     out, aux = pl.pallas_call(
-        prompt_first_kernel,
-        out_shape=(out_shape, aux_shape),
+        middle_kernel,
+        out_shape=(out_shape, jax.ShapeDtypeStruct((reached, 3 * width), jnp.float32)),
         in_specs=[SMEM] + [VMEM] * 4,
         out_specs=(HBM, VMEM),
-        scratch_shapes=out_scratch,
+        scratch_shapes=wide_scratch + out_scratch,
         compiler_params=params(8),
         cost_estimate=cost(1),
-        name="prompt_2",
+        name="middle",
     )(place, weights, two_left, state, prompt_peak)
-    for here, key_block, value_block in ((3, keys_3, values_3), (1, keys_1, values_1)):
-        weights, prompt_peak = scores(here, key_block)
-        out = pl.pallas_call(
-            functools.partial(prompt_kernel, here),
-            out_shape=out_shape,
-            in_specs=[SMEM] + [VMEM] * 4 + [HBM],
-            out_specs=HBM,
-            scratch_shapes=out_scratch,
-            input_output_aliases={5: 0},
-            compiler_params=params(8),
-            cost_estimate=cost(1),
-            name=f"prompt_{here}",
-        )(place, weights, value_block, state, prompt_peak, out)
-
+    weights, prompt_peak = scores((3, 1), (keys_3, keys_1))
     return pl.pallas_call(
         last_kernel,
         out_shape=out_shape,
-        in_specs=[SMEM] + [VMEM] * 4 + [HBM],
+        in_specs=[SMEM] + [VMEM] * 8 + [HBM],
         out_specs=HBM,
-        scratch_shapes=tail_scratch
-        + [pltpu.VMEM((reached, width), jnp.bfloat16), pltpu.SemaphoreType.DMA((blocks + 1, kv_width // HEAD_DIM))],
-        input_output_aliases={5: 0},
-        compiler_params=params(8),
+        scratch_shapes=wide_scratch + tail_scratch + out_scratch,
+        input_output_aliases={9: 0},
+        compiler_params=params(10),
         cost_estimate=cost(1),
         name="last",
-    )(place, queries, tail_2, segment_ids, aux, out)
+    )(place, queries, weights, one_left, values_3, segment_ids, state, prompt_peak, aux, out)
 
 
 def attend_block(
@@ -562,7 +585,7 @@
     rows = queries.shape[0]
     tokens = rows * parts
     prompt, chain = tokens // 4, tokens // 8
-    if parts == 4 and prompt == rows and 2 * chain == rows and rows % ROWS == 0 and keys.shape[1] >= chain:
+    if parts == 4 and prompt == rows and 2 * chain == rows and rows % ROWS == 0 and keys.shape[1] >= max(chain, 2 * HEAD_DIM):
         return prompt_block_path(queries, keys, values, segment_ids)
     return gathered_path(queries, keys, values, segment_ids)
 

time: 25.4 us -> 24 us (0.945)
  starting transfers between devices: 10.1 us -> 8.37 us
  waiting for transfers between devices: 0.61 us -> 0.99 us
    ppermute x1, starting transfers between devices: 3 us -> 1.92 us  [prompt_block_path(): two_left = lax.ppermute(mixed, 'ctx', [(0, 2), (2, 3)])]
    ppermute x2 -> x1, starting transfers between devices: 1.97 us -> 1.29 us  [prompt_block_path(): one_left = lax.ppermute(mixed, 'ctx', [(0, 1), (1, 2)])]
    ppermute x1, waiting for transfers between devices: 0.01 us -> 0.64 us  [prompt_block_path(): two_left = lax.ppermute(mixed, 'ctx', [(0, 2), (2, 3)])]
    pallas_call x8 -> x5, Pallas kernels: 11.6 us -> 11.6 us  [the longest x1 4.89 us: prompt_block_path(): pl.pallas_call(own_kernel, out_shape=state_shape, in_specs=[SMEM] + [HBM]...]
  transfers between devices with their start and end apart: 7 -> 6, of which waited for: 1 -> 2; matrix products, arithmetic and copies ran while one was open for 0% -> 0% of each run, Pallas kernels for 46% -> 49%
where the time goes in v4:
time: 24 us; the launch traced here: 23.8 us
  Pallas kernels  14.1 us (59%)
  starting transfers between devices  8.37 us (35%)
  waiting for transfers between devices  0.99 us (4%)
  between operations  0.33 us (1%)
    pallas_call x1, Pallas kernels, prompt_block_path(): pl.pallas_call(own_kernel, out_shape=state_shape, in_specs=[SMEM] + [HBM]...  4.89 us
    pallas_call x1, Pallas kernels, prompt_block_path(): pl.pallas_call(middle_kernel, out_shape=(out_shape, jax.ShapeDtypeStruct(...  3.32 us
    pallas_call x1, Pallas kernels, prompt_block_path(): pl.pallas_call(last_kernel, out_shape=out_shape, in_specs=[SMEM] + [VMEM]...  2.43 us
    pallas_call x2, Pallas kernels, scores(): pl.pallas_call(functools.partial(scores_kernel, places), out_shape=(jax.S...  2.27 us
    ppermute x1, starting transfers between devices, prompt_block_path(): two_left = lax.ppermute(mixed, 'ctx', [(0, 2), (2, 3)])  1.92 us
    ppermute x1, starting transfers between devices, prompt_block_path(): keys_1 = lax.ppermute(keys_2, 'ctx', [(2, 1)])  1.3 us
    ppermute x1, starting transfers between devices, prompt_block_path(): one_left = lax.ppermute(mixed, 'ctx', [(0, 1), (1, 2)])  1.29 us
    ppermute x1, starting transfers between devices, prompt_block_path(): keys_3 = lax.ppermute(keys_2, 'ctx', [(2, 3)])  1.29 us
  transfers between devices with their start and end apart: 6, of which 2 were waited for; matrix products, arithmetic and copies ran while one was open for 0% of the time, Pallas kernels for 49%

profile of v4, /device:TPU:22, one launch (start us, length us, event | category | flops | bytes accessed | tf_op | source)
XLA Modules:
  0.0 23.8 jit_solution(1217232725735137657)
XLA Ops:
  0.0 1.3 %collective-permute-start = (bf16[384,256]{1,0:T(8,128)(2,1)}, bf16[384,256]{1,0:T(8,128)(2,1)S(1)}, u32[]{:S(2)}, u32[]{:S(2)}) collective-permute-start(bf16[384,256]{1,0:T(8,128)(2,1)} %k_hbm.3), channel_id=1, source_target_pairs={{0,8},{1,9},{2,10},{3,11},{16,24},{17,25},{18,26},{19,27}} | collective-permute-start | bytes 589832 | tf_op jit(solution)/shard_map/ppermute | solution.py:414
  1.3 1.1 %pack.1 = (bf16[384,256]{1,0:T(8,128)(2,1)S(1)}, f32[384,2304]{1,0:T(8,128)S(1)}) custom-call(s32[1]{0:T(128)} %bitcast.place_ref, bf16[384,2048]{1,0:T(8,128)(2,1)} %q_ref.7, bf16[384,256]{1,0:T(8,128)(2,1)} %k_hbm.3, bf16[384,256]{1,0:T(8,128)(2,1)} %v_hbm.3, s32[384]{0:T(512)} %seg_ref.3), custom_call_target="tpu_custom_call" | custom-call | flops 1 | bytes 1 | tf_op jit(solution)/shard_map/pack/pallas_call | solution.py:424
  2.4 1.9 %collective-permute-start.4 = (bf16[384,256]{1,0:T(8,128)(2,1)S(1)}, bf16[384,256]{1,0:T(8,128)(2,1)S(1)}, u32[]{:S(2)}, u32[]{:S(2)}) collective-permute-start(bf16[384,256]{1,0:T(8,128)(2,1)S(1)} %get-tuple-element.20), channel_id=1, source_target_pairs={{0,8},{8,12},{1,9},{9,13},{2,10},{10,14},{3,11},{11,15},{16,24},{2... | collective-permute-start | bytes 589832 | tf_op jit(solution)/shard_map/ppermute | solution.py:434
  4.4 0.0 copy-start
  4.4 0.0 copy-start.1
  4.4 4.9 %own.1.state_in = f32[384,2304]{1,0:T(8,128)S(1)} custom-call(s32[1]{0:T(128)} %bitcast.place_ref, bf16[384,2048]{1,0:T(8,128)(2,1)} %q_ref.7, bf16[384,256]{1,0:T(8,128)(2,1)} %k_hbm.3, bf16[384,256]{1,0:T(8,128)(2,1)} %v_hbm.3, s32[384]{0:T(512)} %seg_ref.3, f32[384,2304]{1,0:T(8,128)S(1)} %get-tuple-element.17.state_in), custom_call_target="tpu_custom_call", output_to_operand_aliasing={{}: (5, {})} | custom-call | flops 4831838208 | bytes 1 | tf_op jit(solution)/shard_map/own/pallas_call | solution.py:436
  9.3 0.3 %collective-permute-done.refs_0_ = bf16[384,256]{1,0:T(8,128)(2,1)S(1)} collective-permute-done((bf16[384,256]{1,0:T(8,128)(2,1)}, bf16[384,256]{1,0:T(8,128)(2,1)S(1)}, u32[]{:S(2)}, u32[]{:S(2)}) %collective-permute-start) | collective-permute-done | bytes 196640 | tf_op jit(solution)/shard_map/ppermute | solution.py:414
  9.6 1.3 %collective-permute-start.1 = (bf16[384,256]{1,0:T(8,128)(2,1)S(1)}, bf16[384,256]{1,0:T(8,128)(2,1)S(1)}, u32[]{:S(2)}, u32[]{:S(2)}) collective-permute-start(bf16[384,256]{1,0:T(8,128)(2,1)S(1)} %collective-permute-done.refs_0_), channel_id=1, source_target_pairs={{8,12},{9,13},{10,14},{11,15},{24,28},{25,29},{26,30},{27,31}} | collective-permute-start | bytes 589832 | tf_op jit(solution)/shard_map/ppermute | solution.py:449
  10.9 1.3 %collective-permute-start.2 = (bf16[384,256]{1,0:T(8,128)(2,1)S(1)}, bf16[384,256]{1,0:T(8,128)(2,1)S(1)}, u32[]{:S(2)}, u32[]{:S(2)}) collective-permute-start(bf16[384,256]{1,0:T(8,128)(2,1)S(1)} %collective-permute-done.refs_0_), channel_id=1, source_target_pairs={{8,4},{9,5},{10,6},{11,7},{24,20},{25,21},{26,22},{27,23}} | collective-permute-start | bytes 589832 | tf_op jit(solution)/shard_map/ppermute | solution.py:450
  12.2 1.3 %collective-permute-start.3 = (bf16[384,256]{1,0:T(8,128)(2,1)S(1)}, bf16[384,256]{1,0:T(8,128)(2,1)S(1)}, u32[]{:S(2)}, u32[]{:S(2)}) collective-permute-start(bf16[384,256]{1,0:T(8,128)(2,1)S(1)} %get-tuple-element.20), channel_id=1, source_target_pairs={{0,4},{4,8},{1,5},{5,9},{2,6},{6,10},{3,7},{7,11},{16,20},{20,24},... | collective-permute-start | bytes 589832 | tf_op jit(solution)/shard_map/ppermute | solution.py:451
  13.5 0.6 %collective-permute-done.4.t_ref.v_ref = bf16[384,256]{1,0:T(8,128)(2,1)S(1)} collective-permute-done((bf16[384,256]{1,0:T(8,128)(2,1)S(1)}, bf16[384,256]{1,0:T(8,128)(2,1)S(1)}, u32[]{:S(2)}, u32[]{:S(2)}) %collective-permute-start.4) | collective-permute-done | bytes 196640 | tf_op jit(solution)/shard_map/ppermute | solution.py:434
  14.2 1.3 %collective-permute-start.5 = (bf16[384,256]{1,0:T(8,128)(2,1)S(1)}, bf16[384,256]{1,0:T(8,128)(2,1)S(1)}, u32[]{:S(2)}, u32[]{:S(2)}) collective-permute-start(bf16[384,256]{1,0:T(8,128)(2,1)S(1)} %collective-permute-done.4.t_ref.v_ref), channel_id=1, source_target_pairs={{8,12},{9,13},{10,14},{11,15},{24,28},{25,29},{26,30},{27,31}} | collective-permute-start | bytes 589832 | tf_op jit(solution)/shard_map/ppermute | solution.py:452
  15.5 0.0 copy-done
  15.5 0.0 copy-done.1
  15.5 2.2 %scores_2.1 = (bf16[6144,384]{1,0:T(8,128)(2,1)S(1)}, f32[384,128]{1,0:T(8,128)S(1)}) custom-call(s32[1]{0:T(128)} %bitcast.place_ref, bf16[384,2048]{1,0:T(8,128)(2,1)S(1)} %copy-done, bf16[384,256]{1,0:T(8,128)(2,1)S(1)} %collective-permute-done.refs_0_), custom_call_target="tpu_custom_call" | custom-call | flops 2415919104 | bytes 1 | tf_op jit(solution)/shard_map/scores_2/pallas_call | solution.py:474
  17.8 3.3 %middle.1 = (bf16[384,2048]{1,0:T(8,128)(2,1)}, f32[256,6144]{1,0:T(8,128)S(1)}) custom-call(s32[1]{0:T(128)} %bitcast.place_ref, bf16[6144,384]{1,0:T(8,128)(2,1)S(1)} %get-tuple-element.23.w_ref, bf16[384,256]{1,0:T(8,128)(2,1)S(1)} %collective-permute-done.4.t_ref.v_ref, f32[384,2304]{1,0:T(8,128)S(1)} %tail.1.state, ...), custom_call_target="tpu_custom_call" | custom-call | flops 1 | bytes 1 | tf_op jit(solution)/shard_map/middle/pallas_call | solution.py:489
  21.1 0.0 collective-permute-done.1.refs_0_
  21.1 0.0 collective-permute-done.2.refs_1_
  21.2 0.0 collective-permute-done.3.one_ref
  21.2 0.0 collective-permute-done.5.v3_ref
  21.2 2.4 %last.1 = bf16[384,2048]{1,0:T(8,128)(2,1)} custom-call(s32[1]{0:T(128)} %bitcast.place_ref, bf16[384,2048]{1,0:T(8,128)(2,1)S(1)} %copy-done, bf16[6144,384]{1,0:T(8,128)(2,1)S(1)} %get-tuple-element.19.w_ref, bf16[384,256]{1,0:T(8,128)(2,1)S(1)} %collective-permute-done.3.one_ref, ...), custom_call_target="tpu_custom_call", output_to_operand_aliasing={{}: (9, {})} | custom-call | flops 1 | bytes 1 | tf_op jit(solution)/shard_map/last/pallas_call | solution.py:500
  (2 shorter events, 0.0 us)
Async XLA Ops:
  0.0 9.6 %collective-permute-start = (bf16[384,256]{1,0:T(8,128)(2,1)}, bf16[384,256]{1,0:T(8,128)(2,1)S(1)}, u32[]{:S(2)}, u32[]{:S(2)}) collective-permute-start(bf16[384,256]{1,0:T(8,128)(2,1)} %k_hbm.3), channel_id=1, source_target_pairs={{0,8},{1,9},{2,10},{3,11},{16,24},{17,25},{18,26},{19,27}} | collective-permute-start | bytes 589832 | tf_op jit(solution)/shard_map/ppermute | solution.py:414
  2.4 11.7 %collective-permute-start.4 = (bf16[384,256]{1,0:T(8,128)(2,1)S(1)}, bf16[384,256]{1,0:T(8,128)(2,1)S(1)}, u32[]{:S(2)}, u32[]{:S(2)}) collective-permute-start(bf16[384,256]{1,0:T(8,128)(2,1)S(1)} %get-tuple-element.20), channel_id=1, source_target_pairs={{0,8},{8,12},{1,9},{9,13},{2,10},{10,14},{3,11},{11,15},{16,24},{2... | collective-permute-start | bytes 589832 | tf_op jit(solution)/shard_map/ppermute | solution.py:434
  4.4 11.1 %copy-start = (bf16[384,2048]{1,0:T(8,128)(2,1)S(1)}, bf16[384,2048]{1,0:T(8,128)(2,1)}, u32[]{:S(2)}) copy-start(bf16[384,2048]{1,0:T(8,128)(2,1)} %q_ref.7) | copy-start | bytes 4718596
  4.4 11.1 %copy-start.1 = (s32[384]{0:T(512)S(1)}, s32[384]{0:T(512)}, u32[]{:S(2)}) copy-start(s32[384]{0:T(512)} %seg_ref.3) | copy-start | bytes 4612
  9.6 11.5 %collective-permute-start.1 = (bf16[384,256]{1,0:T(8,128)(2,1)S(1)}, bf16[384,256]{1,0:T(8,128)(2,1)S(1)}, u32[]{:S(2)}, u32[]{:S(2)}) collective-permute-start(bf16[384,256]{1,0:T(8,128)(2,1)S(1)} %collective-permute-done.refs_0_), channel_id=1, source_target_pairs={{8,12},{9,13},{10,14},{11,15},{24,28},{25,29},{26,30},{27,31}} | collective-permute-start | bytes 589832 | tf_op jit(solution)/shard_map/ppermute | solution.py:449
  10.9 10.2 %collective-permute-start.2 = (bf16[384,256]{1,0:T(8,128)(2,1)S(1)}, bf16[384,256]{1,0:T(8,128)(2,1)S(1)}, u32[]{:S(2)}, u32[]{:S(2)}) collective-permute-start(bf16[384,256]{1,0:T(8,128)(2,1)S(1)} %collective-permute-done.refs_0_), channel_id=1, source_target_pairs={{8,4},{9,5},{10,6},{11,7},{24,20},{25,21},{26,22},{27,23}} | collective-permute-start | bytes 589832 | tf_op jit(solution)/shard_map/ppermute | solution.py:450
  12.2 8.9 %collective-permute-start.3 = (bf16[384,256]{1,0:T(8,128)(2,1)S(1)}, bf16[384,256]{1,0:T(8,128)(2,1)S(1)}, u32[]{:S(2)}, u32[]{:S(2)}) collective-permute-start(bf16[384,256]{1,0:T(8,128)(2,1)S(1)} %get-tuple-element.20), channel_id=1, source_target_pairs={{0,4},{4,8},{1,5},{5,9},{2,6},{6,10},{3,7},{7,11},{16,20},{20,24},... | collective-permute-start | bytes 589832 | tf_op jit(solution)/shard_map/ppermute | solution.py:451
  14.2 7.0 %collective-permute-start.5 = (bf16[384,256]{1,0:T(8,128)(2,1)S(1)}, bf16[384,256]{1,0:T(8,128)(2,1)S(1)}, u32[]{:S(2)}, u32[]{:S(2)}) collective-permute-start(bf16[384,256]{1,0:T(8,128)(2,1)S(1)} %collective-permute-done.4.t_ref.v_ref), channel_id=1, source_target_pairs={{8,12},{9,13},{10,14},{11,15},{24,28},{25,29},{26,30},{27,31}} | collective-permute-start | bytes 589832 | tf_op jit(solution)/shard_map/ppermute | solution.py:452

commit v5 on v4

--- a/solution.py
+++ b/solution.py
@@ -272,7 +272,7 @@
         own_total = state[rows, width + LANES : width + 2 * LANES] * jnp.exp2((own - peak) * EXP2_SCALE)
         for h in range(heads):
             first = (h * (count // ROWS) + b) * GROUP * ROWS
-            pieces = 2 if (b, h) == (count // ROWS - 1, heads - 1) else 1
+            pieces = 4
             size = GROUP // pieces
             for p in range(pieces):
                 low = first + p * size * ROWS
@@ -298,13 +298,11 @@
 
     @pl.when(place_ref[0] == 2)
     def _():
-        waits = []
-
         def finish(rows, cols, value, index, peak, total):
             goes_on = rows.stop <= aux.shape[0]
             if value is None:
                 if not goes_on:
-                    put_out(staged, out_ref, sem, rows, cols, waits)
+                    put_out(staged, out_ref, sem, rows, cols)
             elif goes_on:
                 aux[rows, cols] = value
                 aux[rows, shifted([cols], width)[0]] = column(peak, index)
@@ -315,13 +313,18 @@
         fill_ones(wide, heads)
         with_ones(wide, v_ref, staged.shape[0], heads)
         prompt_rows(w_ref, state, ppeak_ref, wide, finish)
-        for wait in waits:
-            wait.wait()
-
-
-def put_out(staged, out_ref, sem, rows, cols, waits):
+        if aux.shape[0] < staged.shape[0]:
+            wait_out(staged, out_ref, sem, aux.shape[0], staged.shape[0] - aux.shape[0])
+
+
+def put_out(staged, out_ref, sem, rows, cols):
     box = (pl.ds(rows.start, rows.stop - rows.start), pl.ds(cols.start, cols.stop - cols.start))
-    waits.append(fetch(staged.at[box], out_ref.at[box], sem.at[len(waits)]))
+    fetch(staged.at[box], out_ref.at[box], sem)
+
+
+def wait_out(staged, out_ref, sem, first, number):
+    rows = pl.ds(first, number)
+    pltpu.make_async_copy(staged.at[rows], out_ref.at[rows], sem).wait()
 
 
 def last_kernel(
@@ -332,15 +335,9 @@
     half = count // 2
     place = place_ref[0]
 
-    def run(body):
-        waits = []
-
-        def put(rows, cols):
-            put_out(staged, out_ref, sem, rows, cols, waits)
-
-        body(put)
-        for wait in waits:
-            wait.wait()
+    def run(body, number):
+        body(functools.partial(put_out, staged, out_ref, sem))
+        wait_out(staged, out_ref, sem, 0, number)
 
     @pl.when(place == 0)
     def _():
@@ -350,7 +347,7 @@
                 staged[rows, :] = state[rows, 0:width].astype(jnp.bfloat16)
                 put(rows, slice(0, width))
 
-        run(body)
+        run(body, count)
 
     for here, ref in ((1, one_ref), (3, v3_ref)):
         pl.when(place == here)(functools.partial(with_ones, wide, ref, count, heads))
@@ -368,7 +365,7 @@
 
             prompt_rows(w_ref, state, ppeak_ref, wide, finish)
 
-        run(body)
+        run(body, count)
 
     @pl.when(place == 2)
     def _():
@@ -391,7 +388,7 @@
                 put(rest, slice(0, width))
             merge_tail(q_ref, one_ref, seg_ref, peaks_of, tail, tail_wide, finish)
 
-        run(body)
+        run(body, aux.shape[0])
 
 
 def params(mebibytes):
@@ -466,8 +463,7 @@
 
     out_shape = jax.ShapeDtypeStruct(queries.shape, jnp.bfloat16)
     reached = -(-half // ROWS) * ROWS
-    chunks = blocks * (kv_width // HEAD_DIM) + 1
-    out_scratch = [pltpu.VMEM(queries.shape, jnp.bfloat16), pltpu.SemaphoreType.DMA((chunks,))]
+    out_scratch = [pltpu.VMEM(queries.shape, jnp.bfloat16), pltpu.SemaphoreType.DMA]
     wide_scratch = [pltpu.VMEM((count, 2 * kv_width), jnp.bfloat16)]
 
     def scores(places, key_blocks):

time: 24 us -> 23.9 us (level)
  no operation moved by 1% of the time
where the time goes in v5:
time: 23.9 us; the launch traced here: 23.7 us
  Pallas kernels  14 us (59%)
  starting transfers between devices  8.37 us (35%)
  waiting for transfers between devices  0.99 us (4%)
  between operations  0.33 us (1%)
    pallas_call x1, Pallas kernels, prompt_block_path(): pl.pallas_call(own_kernel, out_shape=state_shape, in_specs=[SMEM] + [HBM]...  4.89 us
    pallas_call x1, Pallas kernels, prompt_block_path(): pl.pallas_call(middle_kernel, out_shape=(out_shape, jax.ShapeDtypeStruct(...  3.29 us
    pallas_call x1, Pallas kernels, prompt_block_path(): pl.pallas_call(last_kernel, out_shape=out_shape, in_specs=[SMEM] + [VMEM]...  2.37 us
    pallas_call x2, Pallas kernels, scores(): pl.pallas_call(functools.partial(scores_kernel, places), out_shape=(jax.S...  2.27 us
    ppermute x1, starting transfers between devices, prompt_block_path(): two_left = lax.ppermute(mixed, 'ctx', [(0, 2), (2, 3)])  1.92 us
    ppermute x1, starting transfers between devices, prompt_block_path(): keys_1 = lax.ppermute(keys_2, 'ctx', [(2, 1)])  1.3 us
    ppermute x1, starting transfers between devices, prompt_block_path(): one_left = lax.ppermute(mixed, 'ctx', [(0, 1), (1, 2)])  1.29 us
    ppermute x1, starting transfers between devices, prompt_block_path(): keys_3 = lax.ppermute(keys_2, 'ctx', [(2, 3)])  1.29 us
  transfers between devices with their start and end apart: 6, of which 2 were waited for; matrix products, arithmetic and copies ran while one was open for 0% of the time, Pallas kernels for 49%

profile of v5, /device:TPU:22, one launch (start us, length us, event | category | flops | bytes accessed | tf_op | source)
XLA Modules:
  0.0 23.7 jit_solution(4303794678693248284)
XLA Ops:
  0.0 1.3 %collective-permute-start = (bf16[384,256]{1,0:T(8,128)(2,1)}, bf16[384,256]{1,0:T(8,128)(2,1)S(1)}, u32[]{:S(2)}, u32[]{:S(2)}) collective-permute-start(bf16[384,256]{1,0:T(8,128)(2,1)} %k_hbm.3), channel_id=1, source_target_pairs={{0,8},{1,9},{2,10},{3,11},{16,24},{17,25},{18,26},{19,27}} | collective-permute-start | bytes 589832 | tf_op jit(solution)/shard_map/ppermute | solution.py:411
  1.3 1.1 %pack.1 = (bf16[384,256]{1,0:T(8,128)(2,1)S(1)}, f32[384,2304]{1,0:T(8,128)S(1)}) custom-call(s32[1]{0:T(128)} %bitcast.place_ref, bf16[384,2048]{1,0:T(8,128)(2,1)} %q_ref.7, bf16[384,256]{1,0:T(8,128)(2,1)} %k_hbm.3, bf16[384,256]{1,0:T(8,128)(2,1)} %v_hbm.3, s32[384]{0:T(512)} %seg_ref.3), custom_call_target="tpu_custom_call" | custom-call | flops 1 | bytes 1 | tf_op jit(solution)/shard_map/pack/pallas_call | solution.py:421
  2.4 1.9 %collective-permute-start.4 = (bf16[384,256]{1,0:T(8,128)(2,1)S(1)}, bf16[384,256]{1,0:T(8,128)(2,1)S(1)}, u32[]{:S(2)}, u32[]{:S(2)}) collective-permute-start(bf16[384,256]{1,0:T(8,128)(2,1)S(1)} %get-tuple-element.20), channel_id=1, source_target_pairs={{0,8},{8,12},{1,9},{9,13},{2,10},{10,14},{3,11},{11,15},{16,24},{2... | collective-permute-start | bytes 589832 | tf_op jit(solution)/shard_map/ppermute | solution.py:431
  4.4 0.0 copy-start
  4.4 0.0 copy-start.1
  4.4 4.9 %own.1.state_in = f32[384,2304]{1,0:T(8,128)S(1)} custom-call(s32[1]{0:T(128)} %bitcast.place_ref, bf16[384,2048]{1,0:T(8,128)(2,1)} %q_ref.7, bf16[384,256]{1,0:T(8,128)(2,1)} %k_hbm.3, bf16[384,256]{1,0:T(8,128)(2,1)} %v_hbm.3, s32[384]{0:T(512)} %seg_ref.3, f32[384,2304]{1,0:T(8,128)S(1)} %get-tuple-element.17.state_in), custom_call_target="tpu_custom_call", output_to_operand_aliasing={{}: (5, {})} | custom-call | flops 4831838208 | bytes 1 | tf_op jit(solution)/shard_map/own/pallas_call | solution.py:433
  9.3 0.3 %collective-permute-done.refs_0_ = bf16[384,256]{1,0:T(8,128)(2,1)S(1)} collective-permute-done((bf16[384,256]{1,0:T(8,128)(2,1)}, bf16[384,256]{1,0:T(8,128)(2,1)S(1)}, u32[]{:S(2)}, u32[]{:S(2)}) %collective-permute-start) | collective-permute-done | bytes 196640 | tf_op jit(solution)/shard_map/ppermute | solution.py:411
  9.6 1.3 %collective-permute-start.1 = (bf16[384,256]{1,0:T(8,128)(2,1)S(1)}, bf16[384,256]{1,0:T(8,128)(2,1)S(1)}, u32[]{:S(2)}, u32[]{:S(2)}) collective-permute-start(bf16[384,256]{1,0:T(8,128)(2,1)S(1)} %collective-permute-done.refs_0_), channel_id=1, source_target_pairs={{8,12},{9,13},{10,14},{11,15},{24,28},{25,29},{26,30},{27,31}} | collective-permute-start | bytes 589832 | tf_op jit(solution)/shard_map/ppermute | solution.py:446
  10.9 1.3 %collective-permute-start.2 = (bf16[384,256]{1,0:T(8,128)(2,1)S(1)}, bf16[384,256]{1,0:T(8,128)(2,1)S(1)}, u32[]{:S(2)}, u32[]{:S(2)}) collective-permute-start(bf16[384,256]{1,0:T(8,128)(2,1)S(1)} %collective-permute-done.refs_0_), channel_id=1, source_target_pairs={{8,4},{9,5},{10,6},{11,7},{24,20},{25,21},{26,22},{27,23}} | collective-permute-start | bytes 589832 | tf_op jit(solution)/shard_map/ppermute | solution.py:447
  12.2 1.3 %collective-permute-start.3 = (bf16[384,256]{1,0:T(8,128)(2,1)S(1)}, bf16[384,256]{1,0:T(8,128)(2,1)S(1)}, u32[]{:S(2)}, u32[]{:S(2)}) collective-permute-start(bf16[384,256]{1,0:T(8,128)(2,1)S(1)} %get-tuple-element.20), channel_id=1, source_target_pairs={{0,4},{4,8},{1,5},{5,9},{2,6},{6,10},{3,7},{7,11},{16,20},{20,24},... | collective-permute-start | bytes 589832 | tf_op jit(solution)/shard_map/ppermute | solution.py:448
  13.5 0.6 %collective-permute-done.4.t_ref.v_ref = bf16[384,256]{1,0:T(8,128)(2,1)S(1)} collective-permute-done((bf16[384,256]{1,0:T(8,128)(2,1)S(1)}, bf16[384,256]{1,0:T(8,128)(2,1)S(1)}, u32[]{:S(2)}, u32[]{:S(2)}) %collective-permute-start.4) | collective-permute-done | bytes 196640 | tf_op jit(solution)/shard_map/ppermute | solution.py:431
  14.2 1.3 %collective-permute-start.5 = (bf16[384,256]{1,0:T(8,128)(2,1)S(1)}, bf16[384,256]{1,0:T(8,128)(2,1)S(1)}, u32[]{:S(2)}, u32[]{:S(2)}) collective-permute-start(bf16[384,256]{1,0:T(8,128)(2,1)S(1)} %collective-permute-done.4.t_ref.v_ref), channel_id=1, source_target_pairs={{8,12},{9,13},{10,14},{11,15},{24,28},{25,29},{26,30},{27,31}} | collective-permute-start | bytes 589832 | tf_op jit(solution)/shard_map/ppermute | solution.py:449
  15.5 0.0 copy-done
  15.5 0.0 copy-done.1
  15.5 2.2 %scores_2.1 = (bf16[6144,384]{1,0:T(8,128)(2,1)S(1)}, f32[384,128]{1,0:T(8,128)S(1)}) custom-call(s32[1]{0:T(128)} %bitcast.place_ref, bf16[384,2048]{1,0:T(8,128)(2,1)S(1)} %copy-done, bf16[384,256]{1,0:T(8,128)(2,1)S(1)} %collective-permute-done.refs_0_), custom_call_target="tpu_custom_call" | custom-call | flops 2415919104 | bytes 1 | tf_op jit(solution)/shard_map/scores_2/pallas_call | solution.py:470
  17.8 3.3 %middle.1 = (bf16[384,2048]{1,0:T(8,128)(2,1)}, f32[256,6144]{1,0:T(8,128)S(1)}) custom-call(s32[1]{0:T(128)} %bitcast.place_ref, bf16[6144,384]{1,0:T(8,128)(2,1)S(1)} %get-tuple-element.23.w_ref, bf16[384,256]{1,0:T(8,128)(2,1)S(1)} %collective-permute-done.4.t_ref.v_ref, f32[384,2304]{1,0:T(8,128)S(1)} %tail.1.state, ...), custom_call_target="tpu_custom_call" | custom-call | flops 1 | bytes 1 | tf_op jit(solution)/shard_map/middle/pallas_call | solution.py:485
  21.1 0.0 collective-permute-done.1.refs_0_
  21.1 0.0 collective-permute-done.2.refs_1_
  21.1 0.0 collective-permute-done.3.one_ref
  21.1 0.0 collective-permute-done.5.v3_ref
  21.1 2.4 %last.1 = bf16[384,2048]{1,0:T(8,128)(2,1)} custom-call(s32[1]{0:T(128)} %bitcast.place_ref, bf16[384,2048]{1,0:T(8,128)(2,1)S(1)} %copy-done, bf16[6144,384]{1,0:T(8,128)(2,1)S(1)} %get-tuple-element.19.w_ref, bf16[384,256]{1,0:T(8,128)(2,1)S(1)} %collective-permute-done.3.one_ref, ...), custom_call_target="tpu_custom_call", output_to_operand_aliasing={{}: (9, {})} | custom-call | flops 1 | bytes 1 | tf_op jit(solution)/shard_map/last/pallas_call | solution.py:496
  (2 shorter events, 0.0 us)
Async XLA Ops:
  0.0 9.6 %collective-permute-start = (bf16[384,256]{1,0:T(8,128)(2,1)}, bf16[384,256]{1,0:T(8,128)(2,1)S(1)}, u32[]{:S(2)}, u32[]{:S(2)}) collective-permute-start(bf16[384,256]{1,0:T(8,128)(2,1)} %k_hbm.3), channel_id=1, source_target_pairs={{0,8},{1,9},{2,10},{3,11},{16,24},{17,25},{18,26},{19,27}} | collective-permute-start | bytes 589832 | tf_op jit(solution)/shard_map/ppermute | solution.py:411
  2.4 11.7 %collective-permute-start.4 = (bf16[384,256]{1,0:T(8,128)(2,1)S(1)}, bf16[384,256]{1,0:T(8,128)(2,1)S(1)}, u32[]{:S(2)}, u32[]{:S(2)}) collective-permute-start(bf16[384,256]{1,0:T(8,128)(2,1)S(1)} %get-tuple-element.20), channel_id=1, source_target_pairs={{0,8},{8,12},{1,9},{9,13},{2,10},{10,14},{3,11},{11,15},{16,24},{2... | collective-permute-start | bytes 589832 | tf_op jit(solution)/shard_map/ppermute | solution.py:431
  4.4 11.1 %copy-start = (bf16[384,2048]{1,0:T(8,128)(2,1)S(1)}, bf16[384,2048]{1,0:T(8,128)(2,1)}, u32[]{:S(2)}) copy-start(bf16[384,2048]{1,0:T(8,128)(2,1)} %q_ref.7) | copy-start | bytes 4718596
  4.4 11.1 %copy-start.1 = (s32[384]{0:T(512)S(1)}, s32[384]{0:T(512)}, u32[]{:S(2)}) copy-start(s32[384]{0:T(512)} %seg_ref.3) | copy-start | bytes 4612
  9.6 11.4 %collective-permute-start.1 = (bf16[384,256]{1,0:T(8,128)(2,1)S(1)}, bf16[384,256]{1,0:T(8,128)(2,1)S(1)}, u32[]{:S(2)}, u32[]{:S(2)}) collective-permute-start(bf16[384,256]{1,0:T(8,128)(2,1)S(1)} %collective-permute-done.refs_0_), channel_id=1, source_target_pairs={{8,12},{9,13},{10,14},{11,15},{24,28},{25,29},{26,30},{27,31}} | collective-permute-start | bytes 589832 | tf_op jit(solution)/shard_map/ppermute | solution.py:446
  10.9 10.2 %collective-permute-start.2 = (bf16[384,256]{1,0:T(8,128)(2,1)S(1)}, bf16[384,256]{1,0:T(8,128)(2,1)S(1)}, u32[]{:S(2)}, u32[]{:S(2)}) collective-permute-start(bf16[384,256]{1,0:T(8,128)(2,1)S(1)} %collective-permute-done.refs_0_), channel_id=1, source_target_pairs={{8,4},{9,5},{10,6},{11,7},{24,20},{25,21},{26,22},{27,23}} | collective-permute-start | bytes 589832 | tf_op jit(solution)/shard_map/ppermute | solution.py:447
  12.2 8.9 %collective-permute-start.3 = (bf16[384,256]{1,0:T(8,128)(2,1)S(1)}, bf16[384,256]{1,0:T(8,128)(2,1)S(1)}, u32[]{:S(2)}, u32[]{:S(2)}) collective-permute-start(bf16[384,256]{1,0:T(8,128)(2,1)S(1)} %get-tuple-element.20), channel_id=1, source_target_pairs={{0,4},{4,8},{1,5},{5,9},{2,6},{6,10},{3,7},{7,11},{16,20},{20,24},... | collective-permute-start | bytes 589832 | tf_op jit(solution)/shard_map/ppermute | solution.py:448
  14.2 7.0 %collective-permute-start.5 = (bf16[384,256]{1,0:T(8,128)(2,1)S(1)}, bf16[384,256]{1,0:T(8,128)(2,1)S(1)}, u32[]{:S(2)}, u32[]{:S(2)}) collective-permute-start(bf16[384,256]{1,0:T(8,128)(2,1)S(1)} %collective-permute-done.4.t_ref.v_ref), channel_id=1, source_target_pairs={{8,12},{9,13},{10,14},{11,15},{24,28},{25,29},{26,30},{27,31}} | collective-permute-start | bytes 589832 | tf_op jit(solution)/shard_map/ppermute | solution.py:449

commit v6 on v5

--- a/solution.py
+++ b/solution.py
@@ -176,14 +176,16 @@
             rows = slice(b * ROWS, (b + 1) * ROWS)
             peaks = jnp.zeros((ROWS, LANES), jnp.float32)
             for h in range(heads):
-                cols = head_cols(h)
-                scores = dot_t(stack(q_ref, rows, cols), k_ref[:, h * HEAD_DIM : (h + 1) * HEAD_DIM])
-                peak = jnp.max(scores, axis=-1, keepdims=True)
-                weights = jnp.exp2((scores - peak) * EXP2_SCALE).astype(jnp.bfloat16)
-                first = (h * (count // ROWS) + b) * GROUP * ROWS
-                w_ref[first : first + GROUP * ROWS, :] = weights
-                for g in range(GROUP):
-                    peaks = jnp.where(lane == h * GROUP + g, peak[g * ROWS : (g + 1) * ROWS], peaks)
+                for low in range(0, GROUP, 2):
+                    cols = head_cols(h)[low : low + 2]
+                    scores = dot_t(stack(q_ref, rows, cols), k_ref[:, h * HEAD_DIM : (h + 1) * HEAD_DIM])
+                    peak = jnp.max(scores, axis=-1, keepdims=True)
+                    weights = jnp.exp2((scores - peak) * EXP2_SCALE).astype(jnp.bfloat16)
+                    first = ((h * (count // ROWS) + b) * GROUP + low) * ROWS
+                    w_ref[first : first + 2 * ROWS, :] = weights
+                    for g in range(2):
+                        here = lane == h * GROUP + low + g
+                        peaks = jnp.where(here, peak[g * ROWS : (g + 1) * ROWS], peaks)
             peak_ref[rows, :] = peaks
 
 

time: 23.9 us -> 23.9 us (level)
  no operation moved by 1% of the time
where the time goes in v6:
time: 23.9 us; the launch traced here: 23.7 us
  Pallas kernels  14 us (59%)
  starting transfers between devices  8.37 us (35%)
  waiting for transfers between devices  0.99 us (4%)
  between operations  0.33 us (1%)
    pallas_call x1, Pallas kernels, prompt_block_path(): pl.pallas_call(own_kernel, out_shape=state_shape, in_specs=[SMEM] + [HBM]...  4.89 us
    pallas_call x1, Pallas kernels, prompt_block_path(): pl.pallas_call(middle_kernel, out_shape=(out_shape, jax.ShapeDtypeStruct(...  3.3 us
    pallas_call x1, Pallas kernels, prompt_block_path(): pl.pallas_call(last_kernel, out_shape=out_shape, in_specs=[SMEM] + [VMEM]...  2.37 us
    pallas_call x2, Pallas kernels, scores(): pl.pallas_call(functools.partial(scores_kernel, places), out_shape=(jax.S...  2.27 us
    ppermute x1, starting transfers between devices, prompt_block_path(): two_left = lax.ppermute(mixed, 'ctx', [(0, 2), (2, 3)])  1.92 us
    ppermute x1, starting transfers between devices, prompt_block_path(): keys_1 = lax.ppermute(keys_2, 'ctx', [(2, 1)])  1.3 us
    ppermute x1, starting transfers between devices, prompt_block_path(): one_left = lax.ppermute(mixed, 'ctx', [(0, 1), (1, 2)])  1.29 us
    ppermute x1, starting transfers between devices, prompt_block_path(): keys_3 = lax.ppermute(keys_2, 'ctx', [(2, 3)])  1.29 us
  transfers between devices with their start and end apart: 6, of which 2 were waited for; matrix products, arithmetic and copies ran while one was open for 0% of the time, Pallas kernels for 49%

profile of v6, /device:TPU:22, one launch (start us, length us, event | category | flops | bytes accessed | tf_op | source)
XLA Modules:
  0.0 23.7 jit_solution(17513897521770202839)
XLA Ops:
  0.0 1.3 %collective-permute-start = (bf16[384,256]{1,0:T(8,128)(2,1)}, bf16[384,256]{1,0:T(8,128)(2,1)S(1)}, u32[]{:S(2)}, u32[]{:S(2)}) collective-permute-start(bf16[384,256]{1,0:T(8,128)(2,1)} %k_hbm.3), channel_id=1, source_target_pairs={{0,8},{1,9},{2,10},{3,11},{16,24},{17,25},{18,26},{19,27}} | collective-permute-start | bytes 589832 | tf_op jit(solution)/shard_map/ppermute | solution.py:413
  1.3 1.1 %pack.1 = (bf16[384,256]{1,0:T(8,128)(2,1)S(1)}, f32[384,2304]{1,0:T(8,128)S(1)}) custom-call(s32[1]{0:T(128)} %bitcast.place_ref, bf16[384,2048]{1,0:T(8,128)(2,1)} %q_ref.7, bf16[384,256]{1,0:T(8,128)(2,1)} %k_hbm.3, bf16[384,256]{1,0:T(8,128)(2,1)} %v_hbm.3, s32[384]{0:T(512)} %seg_ref.3), custom_call_target="tpu_custom_call" | custom-call | flops 1 | bytes 1 | tf_op jit(solution)/shard_map/pack/pallas_call | solution.py:423
  2.4 1.9 %collective-permute-start.4 = (bf16[384,256]{1,0:T(8,128)(2,1)S(1)}, bf16[384,256]{1,0:T(8,128)(2,1)S(1)}, u32[]{:S(2)}, u32[]{:S(2)}) collective-permute-start(bf16[384,256]{1,0:T(8,128)(2,1)S(1)} %get-tuple-element.20), channel_id=1, source_target_pairs={{0,8},{8,12},{1,9},{9,13},{2,10},{10,14},{3,11},{11,15},{16,24},{2... | collective-permute-start | bytes 589832 | tf_op jit(solution)/shard_map/ppermute | solution.py:433
  4.4 0.0 copy-start
  4.4 0.0 copy-start.1
  4.4 4.9 %own.1.state_in = f32[384,2304]{1,0:T(8,128)S(1)} custom-call(s32[1]{0:T(128)} %bitcast.place_ref, bf16[384,2048]{1,0:T(8,128)(2,1)} %q_ref.7, bf16[384,256]{1,0:T(8,128)(2,1)} %k_hbm.3, bf16[384,256]{1,0:T(8,128)(2,1)} %v_hbm.3, s32[384]{0:T(512)} %seg_ref.3, f32[384,2304]{1,0:T(8,128)S(1)} %get-tuple-element.17.state_in), custom_call_target="tpu_custom_call", output_to_operand_aliasing={{}: (5, {})} | custom-call | flops 4831838208 | bytes 1 | tf_op jit(solution)/shard_map/own/pallas_call | solution.py:435
  9.3 0.3 %collective-permute-done.refs_0_ = bf16[384,256]{1,0:T(8,128)(2,1)S(1)} collective-permute-done((bf16[384,256]{1,0:T(8,128)(2,1)}, bf16[384,256]{1,0:T(8,128)(2,1)S(1)}, u32[]{:S(2)}, u32[]{:S(2)}) %collective-permute-start) | collective-permute-done | bytes 196640 | tf_op jit(solution)/shard_map/ppermute | solution.py:413
  9.6 1.3 %collective-permute-start.1 = (bf16[384,256]{1,0:T(8,128)(2,1)S(1)}, bf16[384,256]{1,0:T(8,128)(2,1)S(1)}, u32[]{:S(2)}, u32[]{:S(2)}) collective-permute-start(bf16[384,256]{1,0:T(8,128)(2,1)S(1)} %collective-permute-done.refs_0_), channel_id=1, source_target_pairs={{8,12},{9,13},{10,14},{11,15},{24,28},{25,29},{26,30},{27,31}} | collective-permute-start | bytes 589832 | tf_op jit(solution)/shard_map/ppermute | solution.py:448
  10.9 1.3 %collective-permute-start.2 = (bf16[384,256]{1,0:T(8,128)(2,1)S(1)}, bf16[384,256]{1,0:T(8,128)(2,1)S(1)}, u32[]{:S(2)}, u32[]{:S(2)}) collective-permute-start(bf16[384,256]{1,0:T(8,128)(2,1)S(1)} %collective-permute-done.refs_0_), channel_id=1, source_target_pairs={{8,4},{9,5},{10,6},{11,7},{24,20},{25,21},{26,22},{27,23}} | collective-permute-start | bytes 589832 | tf_op jit(solution)/shard_map/ppermute | solution.py:449
  12.2 1.3 %collective-permute-start.3 = (bf16[384,256]{1,0:T(8,128)(2,1)S(1)}, bf16[384,256]{1,0:T(8,128)(2,1)S(1)}, u32[]{:S(2)}, u32[]{:S(2)}) collective-permute-start(bf16[384,256]{1,0:T(8,128)(2,1)S(1)} %get-tuple-element.20), channel_id=1, source_target_pairs={{0,4},{4,8},{1,5},{5,9},{2,6},{6,10},{3,7},{7,11},{16,20},{20,24},... | collective-permute-start | bytes 589832 | tf_op jit(solution)/shard_map/ppermute | solution.py:450
  13.5 0.6 %collective-permute-done.4.t_ref.v_ref = bf16[384,256]{1,0:T(8,128)(2,1)S(1)} collective-permute-done((bf16[384,256]{1,0:T(8,128)(2,1)S(1)}, bf16[384,256]{1,0:T(8,128)(2,1)S(1)}, u32[]{:S(2)}, u32[]{:S(2)}) %collective-permute-start.4) | collective-permute-done | bytes 196640 | tf_op jit(solution)/shard_map/ppermute | solution.py:433
  14.2 1.3 %collective-permute-start.5 = (bf16[384,256]{1,0:T(8,128)(2,1)S(1)}, bf16[384,256]{1,0:T(8,128)(2,1)S(1)}, u32[]{:S(2)}, u32[]{:S(2)}) collective-permute-start(bf16[384,256]{1,0:T(8,128)(2,1)S(1)} %collective-permute-done.4.t_ref.v_ref), channel_id=1, source_target_pairs={{8,12},{9,13},{10,14},{11,15},{24,28},{25,29},{26,30},{27,31}} | collective-permute-start | bytes 589832 | tf_op jit(solution)/shard_map/ppermute | solution.py:451
  15.5 0.0 copy-done
  15.5 0.0 copy-done.1
  15.5 2.3 %scores_2.1 = (bf16[6144,384]{1,0:T(8,128)(2,1)S(1)}, f32[384,128]{1,0:T(8,128)S(1)}) custom-call(s32[1]{0:T(128)} %bitcast.place_ref, bf16[384,2048]{1,0:T(8,128)(2,1)S(1)} %copy-done, bf16[384,256]{1,0:T(8,128)(2,1)S(1)} %collective-permute-done.refs_0_), custom_call_target="tpu_custom_call" | custom-call | flops 2415919104 | bytes 1 | tf_op jit(solution)/shard_map/scores_2/pallas_call | solution.py:472
  17.8 3.3 %middle.1 = (bf16[384,2048]{1,0:T(8,128)(2,1)}, f32[256,6144]{1,0:T(8,128)S(1)}) custom-call(s32[1]{0:T(128)} %bitcast.place_ref, bf16[6144,384]{1,0:T(8,128)(2,1)S(1)} %get-tuple-element.23.w_ref, bf16[384,256]{1,0:T(8,128)(2,1)S(1)} %collective-permute-done.4.t_ref.v_ref, f32[384,2304]{1,0:T(8,128)S(1)} %tail.1.state, ...), custom_call_target="tpu_custom_call" | custom-call | flops 1 | bytes 1 | tf_op jit(solution)/shard_map/middle/pallas_call | solution.py:487
  21.1 0.0 collective-permute-done.1.refs_0_
  21.1 0.0 collective-permute-done.2.refs_1_
  21.1 0.0 collective-permute-done.3.one_ref
  21.1 0.0 collective-permute-done.5.v3_ref
  21.2 2.4 %last.1 = bf16[384,2048]{1,0:T(8,128)(2,1)} custom-call(s32[1]{0:T(128)} %bitcast.place_ref, bf16[384,2048]{1,0:T(8,128)(2,1)S(1)} %copy-done, bf16[6144,384]{1,0:T(8,128)(2,1)S(1)} %get-tuple-element.19.w_ref, bf16[384,256]{1,0:T(8,128)(2,1)S(1)} %collective-permute-done.3.one_ref, ...), custom_call_target="tpu_custom_call", output_to_operand_aliasing={{}: (9, {})} | custom-call | flops 1 | bytes 1 | tf_op jit(solution)/shard_map/last/pallas_call | solution.py:498
  (2 shorter events, 0.0 us)
Async XLA Ops:
  0.0 9.6 %collective-permute-start = (bf16[384,256]{1,0:T(8,128)(2,1)}, bf16[384,256]{1,0:T(8,128)(2,1)S(1)}, u32[]{:S(2)}, u32[]{:S(2)}) collective-permute-start(bf16[384,256]{1,0:T(8,128)(2,1)} %k_hbm.3), channel_id=1, source_target_pairs={{0,8},{1,9},{2,10},{3,11},{16,24},{17,25},{18,26},{19,27}} | collective-permute-start | bytes 589832 | tf_op jit(solution)/shard_map/ppermute | solution.py:413
  2.4 11.7 %collective-permute-start.4 = (bf16[384,256]{1,0:T(8,128)(2,1)S(1)}, bf16[384,256]{1,0:T(8,128)(2,1)S(1)}, u32[]{:S(2)}, u32[]{:S(2)}) collective-permute-start(bf16[384,256]{1,0:T(8,128)(2,1)S(1)} %get-tuple-element.20), channel_id=1, source_target_pairs={{0,8},{8,12},{1,9},{9,13},{2,10},{10,14},{3,11},{11,15},{16,24},{2... | collective-permute-start | bytes 589832 | tf_op jit(solution)/shard_map/ppermute | solution.py:433
  4.4 11.1 %copy-start = (bf16[384,2048]{1,0:T(8,128)(2,1)S(1)}, bf16[384,2048]{1,0:T(8,128)(2,1)}, u32[]{:S(2)}) copy-start(bf16[384,2048]{1,0:T(8,128)(2,1)} %q_ref.7) | copy-start | bytes 4718596
  4.4 11.1 %copy-start.1 = (s32[384]{0:T(512)S(1)}, s32[384]{0:T(512)}, u32[]{:S(2)}) copy-start(s32[384]{0:T(512)} %seg_ref.3) | copy-start | bytes 4612
  9.6 11.5 %collective-permute-start.1 = (bf16[384,256]{1,0:T(8,128)(2,1)S(1)}, bf16[384,256]{1,0:T(8,128)(2,1)S(1)}, u32[]{:S(2)}, u32[]{:S(2)}) collective-permute-start(bf16[384,256]{1,0:T(8,128)(2,1)S(1)} %collective-permute-done.refs_0_), channel_id=1, source_target_pairs={{8,12},{9,13},{10,14},{11,15},{24,28},{25,29},{26,30},{27,31}} | collective-permute-start | bytes 589832 | tf_op jit(solution)/shard_map/ppermute | solution.py:448
  10.9 10.2 %collective-permute-start.2 = (bf16[384,256]{1,0:T(8,128)(2,1)S(1)}, bf16[384,256]{1,0:T(8,128)(2,1)S(1)}, u32[]{:S(2)}, u32[]{:S(2)}) collective-permute-start(bf16[384,256]{1,0:T(8,128)(2,1)S(1)} %collective-permute-done.refs_0_), channel_id=1, source_target_pairs={{8,4},{9,5},{10,6},{11,7},{24,20},{25,21},{26,22},{27,23}} | collective-permute-start | bytes 589832 | tf_op jit(solution)/shard_map/ppermute | solution.py:449
  12.2 8.9 %collective-permute-start.3 = (bf16[384,256]{1,0:T(8,128)(2,1)S(1)}, bf16[384,256]{1,0:T(8,128)(2,1)S(1)}, u32[]{:S(2)}, u32[]{:S(2)}) collective-permute-start(bf16[384,256]{1,0:T(8,128)(2,1)S(1)} %get-tuple-element.20), channel_id=1, source_target_pairs={{0,4},{4,8},{1,5},{5,9},{2,6},{6,10},{3,7},{7,11},{16,20},{20,24},... | collective-permute-start | bytes 589832 | tf_op jit(solution)/shard_map/ppermute | solution.py:450
  14.2 7.0 %collective-permute-start.5 = (bf16[384,256]{1,0:T(8,128)(2,1)S(1)}, bf16[384,256]{1,0:T(8,128)(2,1)S(1)}, u32[]{:S(2)}, u32[]{:S(2)}) collective-permute-start(bf16[384,256]{1,0:T(8,128)(2,1)S(1)} %collective-permute-done.4.t_ref.v_ref), channel_id=1, source_target_pairs={{8,12},{9,13},{10,14},{11,15},{24,28},{25,29},{26,30},{27,31}} | collective-permute-start | bytes 589832 | tf_op jit(solution)/shard_map/ppermute | solution.py:451
